TPU v7x, 32 devices: a whole 2x2x4 slice. The times are simulated.
32 devices in a mesh: fsdp: 4 (over z), ctx: 4 (over y, x), tp: 2 (over core).
Axes of the slice: x: 2, y: 2, z: 4, core: 2. Of those that a mesh axis runs over, the one named last changes fastest.
Arguments:
- tokens: bfloat16 [16384, 2048], P(('fsdp', 'ctx')), may hold values from -6 to 6
- cotangent: bfloat16 [16384, 2048], P(('fsdp', 'ctx')), may hold values from -6 to 6
- routes: int32 [16384, 8], P(('fsdp', 'ctx')), may hold values from 0 to 15, all different within a row; in each aligned block of 1024 rows (0 to 1023, 1024 to 2047, ...) at most 576 rows name the same one
- adapter_ids: int32 [4, 9], P('fsdp'), may hold values from 0 to 7
- norm_in: bfloat16 [2048], replicated, may hold values from 0.5 to 1.5
- norm_mid: bfloat16 [2048], replicated, may hold values from 0.5 to 1.5
- q_gain: bfloat16 [2048], P('tp'), may hold values from 1 to 2
- k_gain: bfloat16 [2048], P('tp'), may hold values from 1 to 2
- w_qkv: bfloat16 [2048, 3, 2048], P('fsdp', None, 'tp'), may hold values from -0.125 to 0.125
- w_out: bfloat16 [2048, 2048], P('tp', 'fsdp'), may hold values from -0.375 to 0.375
- w_router: bfloat16 [2048, 16], replicated, may hold values from -0.0625 to 0.0625
- w_gate_up: bfloat16 [16, 2048, 2, 1024], P('fsdp', None, None, 'tp'), may hold values from -0.125 to 0.125
- w_down: bfloat16 [16, 1024, 2048], P('fsdp', 'tp'), may hold values from -1.5 to 1.5
- qkv_a: bfloat16 [8, 2048, 3, 16], P('fsdp'), may hold values from -0.125 to 0.125
- qkv_b: bfloat16 [8, 16, 3, 2048], P('fsdp', None, None, 'tp'), may hold values from -1.5 to 1.5
- out_a: bfloat16 [8, 2048, 16], P('fsdp', 'tp'), may hold values from -0.125 to 0.125
- out_b: bfloat16 [8, 16, 2048], P('fsdp'), may hold values from -4 to 4
- router_a: bfloat16 [8, 2048, 16], P('fsdp'), may hold values from -0.125 to 0.125
- router_b: bfloat16 [8, 16, 16], P('fsdp'), may hold values from -0.75 to 0.75
- gu_a: bfloat16 [8, 16, 2048, 2, 16], P('fsdp'), may hold values from -0.125 to 0.125
- gu_b: bfloat16 [8, 16, 16, 2, 1024], P('fsdp', None, None, None, 'tp'), may hold values from -1.5 to 1.5
- down_a: bfloat16 [8, 16, 1024, 16], P('fsdp', None, 'tp'), may hold values from -0.1875 to 0.1875
- down_b: bfloat16 [8, 16, 16, 2048], P('fsdp'), may hold values from -6 to 6
Outputs:
- mixed: bfloat16 [16384, 2048], P(('fsdp', 'ctx'))
- grad_input: float32 [16384, 2048], P(('fsdp', 'ctx'))
- grad_qkv_a: float32 [8, 2048, 3, 16], P('fsdp')
- grad_qkv_b: float32 [8, 16, 3, 2048], P('fsdp', None, None, 'tp')
- grad_out_a: float32 [8, 2048, 16], P('fsdp', 'tp')
- grad_out_b: float32 [8, 16, 2048], P('fsdp')
- grad_router_a: float32 [8, 2048, 16], P('fsdp')
- grad_router_b: float32 [8, 16, 16], P('fsdp')
- grad_gu_a: float32 [8, 16, 2048, 2, 16], P('fsdp')
- grad_gu_b: float32 [8, 16, 16, 2, 1024], P('fsdp', None, None, None, 'tp')
- grad_down_a: float32 [8, 16, 1024, 16], P('fsdp', None, 'tp')
- grad_down_b: float32 [8, 16, 16, 2048], P('fsdp')
Inputs may be any that keep to these rules, and one draw needn't show every extreme that they name: `routes`: each row names 8 different experts. In the rows of one device (each aligned block of 1024 rows) no expert is named by more than 576 rows, and in some block some expert is named by exactly 576 rows.
All inputs are finite; a program needn't handle non-finite values.
Results may differ from a plain program's by a relative error of at most 0.023.
Values may be sent and summed in bfloat16 or wider, within the bound.
No kernel may reach another device: no remote copies, remote signals or barrier semaphores. Data moves between devices by JAX's collectives and lax.ppermute only.
A program may use at most 576 MiB of HBM per device.

v0:
```python
import jax
import jax.numpy as jnp
from jax import lax
from jax.sharding import PartitionSpec as P

HEAD_DIM = 128
TOPK = 8
EXPERTS = 16
RANK = 16
PROMPT = 2048
CONT_LEN = 256
CONTS = 8


epsilon = 1e-05
ADAPTER_SCALE = 0.5
ROPE_BASE = 10000.0
masked_score = -1e30
highest_precision = lax.Precision.HIGHEST


def head_sum(parts):
    return lax.psum(parts, "tp")


def rms_back(value, gain, grad, scale_col, full_width):
    inner = jnp.sum(gain * value * grad, axis=-1, keepdims=True)
    return (
        scale_col * gain * grad - value * (scale_col * scale_col * scale_col) * inner / full_width
    )


def angles(positions):
    freqs = ROPE_BASE ** (-(2.0 * jnp.arange(HEAD_DIM // 2, dtype=jnp.float32)) / HEAD_DIM)
    turned = positions.astype(jnp.float32)[:, None] * freqs[None, :]
    return (jnp.cos(turned)[:, None, :], jnp.sin(turned)[:, None, :])


def rotate(value, cosine, sine_part):
    half_dim = value.shape[-1] // 2
    first_half = value[..., :half_dim]
    second_half = value[..., half_dim:]
    return jnp.concatenate(
        [
            first_half * cosine - second_half * sine_part,
            second_half * cosine + first_half * sine_part,
        ],
        axis=-1,
    )


def run_piece(step_fn, acc_value, weight_rows):
    count = weight_rows[0].shape[0]
    step_inputs = (weight_rows[0], weight_rows[1], jnp.arange(count, dtype=jnp.int32))
    acc_value, unused = lax.scan(step_fn, acc_value, step_inputs)
    return acc_value


def per_device(
    tokens,
    cotangent,
    routes,
    adapter_ids,
    norm_in,
    norm_mid,
    q_gain,
    k_gain,
    w_qkv,
    w_out,
    w_router,
    w_gate_up,
    w_down,
    qkv_a,
    qkv_b,
    out_a,
    out_b,
    router_a,
    router_b,
    gu_a,
    gu_b,
    down_a,
    down_b,
):
    row_count, full_width = tokens.shape
    local_width = q_gain.shape[0]
    local_heads = local_width // HEAD_DIM
    ff_local = w_gate_up.shape[3]
    slab_count = lax.axis_size("ctx")
    slab_index = lax.axis_index("ctx")
    prompt_rows = PROMPT // slab_count
    cont_count = CONTS // slab_count
    use_count = cont_count + 1
    capacity = row_count * TOPK * 9 // (8 * EXPERTS)
    score_scale = HEAD_DIM ** (-0.5)
    key_width = min(512, PROMPT)
    key_blocks_n = PROMPT // key_width
    row_index = jnp.arange(row_count, dtype=jnp.int32)
    tail_offset = jnp.maximum(row_index - prompt_rows, 0)
    leading = row_index < prompt_rows
    positions = jnp.where(
        leading, slab_index * prompt_rows + row_index, PROMPT + tail_offset % CONT_LEN
    )
    segment = jnp.where(leading, 0, 1 + tail_offset // CONT_LEN)
    cont_sets = lax.dynamic_slice_in_dim(adapter_ids[0], 1 + slab_index * cont_count, cont_count)
    used_sets = jnp.concatenate([adapter_ids[0][:1], cont_sets])
    row_adapter_index = (
        segment[:, None] == jnp.arange(use_count, dtype=jnp.int32)[None, :]
    ).astype(jnp.float32)
    cosine, sine_part = angles(positions)
    (
        full_qkv_a,
        full_qkv_b,
        full_out_a,
        full_out_b,
        full_router_a,
        full_router_b,
        full_gu_a,
        full_gu_b,
        full_down_a,
        full_down_b,
    ) = (
        lax.all_gather(qkv_a, "fsdp", axis=0, tiled=True),
        lax.all_gather(qkv_b, "fsdp", axis=0, tiled=True),
        lax.all_gather(out_a, "fsdp", axis=0, tiled=True),
        lax.all_gather(out_b, "fsdp", axis=0, tiled=True),
        lax.all_gather(router_a, "fsdp", axis=0, tiled=True),
        lax.all_gather(router_b, "fsdp", axis=0, tiled=True),
        lax.all_gather(gu_a, "fsdp", axis=0, tiled=True),
        lax.all_gather(gu_b, "fsdp", axis=0, tiled=True),
        lax.all_gather(down_a, "fsdp", axis=0, tiled=True),
        lax.all_gather(down_b, "fsdp", axis=0, tiled=True),
    )

    def pick(whole_sets):
        return jnp.take(whole_sets, used_sets, axis=0)

    def spread(grad_used, whole_sets):
        return jnp.zeros(whole_sets.shape, jnp.float32).at[used_sets].add(grad_used)

    use_qkv_a = pick(full_qkv_a)
    use_qkv_b = pick(full_qkv_b)
    selected_output_down = pick(full_out_a)
    use_out_b = pick(full_out_b)
    use_router_a = pick(full_router_a)
    use_router_b = pick(full_router_b)
    use_gu_a = pick(full_gu_a)
    use_gu_b = pick(full_gu_b)
    use_down_a = pick(full_down_a)
    use_down_b = pick(full_down_b)
    token_vals = tokens.astype(jnp.float32)
    cot_vals = cotangent.astype(jnp.float32)
    gain_in = norm_in.astype(jnp.float32)
    gain_mid = norm_mid.astype(jnp.float32)
    gain_q = q_gain.astype(jnp.float32)
    gain_k = k_gain.astype(jnp.float32)
    first_scale = lax.rsqrt(jnp.mean(token_vals * token_vals, axis=1, keepdims=True) + epsilon)
    hidden_after_attention = (token_vals * first_scale * gain_in).astype(jnp.bfloat16)
    columns = hidden_after_attention
    projection_rows = jnp.einsum(
        "yp,pma->yma",
        columns,
        lax.all_gather(w_qkv, "fsdp", axis=0, tiled=True),
        preferred_element_type=jnp.float32,
    )
    mid_qkv = (
        jnp.einsum(
            "td,sdjr->tsjr", hidden_after_attention, use_qkv_a, preferred_element_type=jnp.float32
        )
        * row_adapter_index[:, :, None, None]
    )
    projection_rows = projection_rows + ADAPTER_SCALE * jnp.einsum(
        "ladi,aidv->ldv", mid_qkv, use_qkv_b.astype(jnp.float32), precision=highest_precision
    )
    q_raw = projection_rows[:, 0]
    k_raw = projection_rows[:, 1]
    square_q, square_k = head_sum((jnp.sum(q_raw * q_raw, axis=1), jnp.sum(k_raw * k_raw, axis=1)))
    q_scale = lax.rsqrt(square_q / full_width + epsilon)[:, None]
    k_scale = lax.rsqrt(square_k / full_width + epsilon)[:, None]
    query_rows = rotate(
        (q_raw * q_scale * gain_q).reshape(row_count, local_heads, HEAD_DIM), cosine, sine_part
    ).astype(jnp.bfloat16)
    key_rows = rotate(
        (k_raw * k_scale * gain_k).reshape(row_count, local_heads, HEAD_DIM), cosine, sine_part
    ).astype(jnp.bfloat16)
    value_rows = (
        projection_rows[:, 2].reshape(row_count, local_heads, HEAD_DIM).astype(jnp.bfloat16)
    )
    prompt_keys, prompt_values = (
        lax.all_gather(key_rows[:prompt_rows], "ctx", axis=0, tiled=True),
        lax.all_gather(value_rows[:prompt_rows], "ctx", axis=0, tiled=True),
    )
    key_blocks = prompt_keys.reshape(key_blocks_n, key_width, local_heads, HEAD_DIM)
    value_blocks = prompt_values.reshape(key_blocks_n, key_width, local_heads, HEAD_DIM)
    block_starts = jnp.arange(key_blocks_n, dtype=jnp.int32) * key_width
    query_cont = query_rows[prompt_rows:].reshape(cont_count, CONT_LEN, local_heads, HEAD_DIM)
    key_cont = key_rows[prompt_rows:].reshape(cont_count, CONT_LEN, local_heads, HEAD_DIM)
    value_cont = value_rows[prompt_rows:].reshape(cont_count, CONT_LEN, local_heads, HEAD_DIM)
    cont_idx = jnp.arange(CONT_LEN, dtype=jnp.int32)
    self_mask = (cont_idx[:, None] >= cont_idx[None, :])[None, None]

    def block_scores(key_block, first_row):
        raw_scores = (
            jnp.einsum("thd,khd->htk", query_rows, key_block, preferred_element_type=jnp.float32)
            * score_scale
        )
        allowed = (first_row + jnp.arange(key_block.shape[0], dtype=jnp.int32))[
            None, :
        ] <= positions[:, None]
        return (raw_scores, allowed[None])

    def stat_step(acc_value, step_input):
        row_peak, row_total = acc_value
        key_block, first_row = step_input
        raw_scores, allowed = block_scores(key_block, first_row)
        raw_scores = jnp.where(allowed, raw_scores, masked_score)
        new_peak = jnp.maximum(row_peak, jnp.max(raw_scores, axis=2))
        row_total = row_total * jnp.exp(row_peak - new_peak) + jnp.sum(
            jnp.where(allowed, jnp.exp(raw_scores - new_peak[:, :, None]), 0.0), axis=2
        )
        return ((new_peak, row_total), None)

    (row_peak, row_total), unused = lax.scan(
        stat_step,
        (
            jnp.full((local_heads, row_count), masked_score, jnp.float32),
            jnp.zeros((local_heads, row_count), jnp.float32),
        ),
        (key_blocks, block_starts),
    )
    own_raw = (
        jnp.einsum("cqhd,ckhd->hcqk", query_cont, key_cont, preferred_element_type=jnp.float32)
        * score_scale
    )
    own_masked = jnp.where(self_mask, own_raw, masked_score)
    own_peak = jnp.max(own_masked, axis=3)
    own_total = jnp.sum(
        jnp.where(self_mask, jnp.exp(own_masked - own_peak[..., None]), 0.0), axis=3
    )
    pad_peak = jnp.concatenate(
        [
            jnp.full((local_heads, prompt_rows), masked_score, jnp.float32),
            own_peak.reshape(local_heads, -1),
        ],
        axis=1,
    )
    pad_total = jnp.concatenate(
        [jnp.zeros((local_heads, prompt_rows), jnp.float32), own_total.reshape(local_heads, -1)],
        axis=1,
    )
    new_peak = jnp.maximum(row_peak, pad_peak)
    whole_total = row_total * jnp.exp(row_peak - new_peak) + pad_total * jnp.exp(
        pad_peak - new_peak
    )
    log_total = new_peak + jnp.log(whole_total)
    log_cont = log_total[:, prompt_rows:].reshape(local_heads, cont_count, CONT_LEN)

    def out_step(acc_value, step_input):
        key_block, value_block, first_row = step_input
        raw_scores, allowed = block_scores(key_block, first_row)
        weights = jnp.where(allowed, jnp.exp(raw_scores - log_total[:, :, None]), 0.0).astype(
            jnp.bfloat16
        )
        return (
            acc_value
            + jnp.einsum("htk,khd->thd", weights, value_block, preferred_element_type=jnp.float32),
            None,
        )

    att_acc, unused = lax.scan(
        out_step,
        jnp.zeros((row_count, local_heads, HEAD_DIM), jnp.float32),
        (key_blocks, value_blocks, block_starts),
    )
    own_probs = jnp.where(self_mask, jnp.exp(own_raw - log_cont[..., None]), 0.0)
    own_out = jnp.einsum(
        "hcqk,ckhd->cqhd",
        own_probs.astype(jnp.bfloat16),
        value_cont,
        preferred_element_type=jnp.float32,
    )
    att_acc = att_acc + jnp.concatenate(
        [
            jnp.zeros((prompt_rows, local_heads, HEAD_DIM), jnp.float32),
            own_out.reshape(-1, local_heads, HEAD_DIM),
        ],
        axis=0,
    )
    attention_rows = att_acc.reshape(row_count, local_width).astype(jnp.bfloat16)
    branch_part = jnp.dot(
        attention_rows,
        lax.all_gather(w_out, "fsdp", axis=1, tiled=True),
        preferred_element_type=jnp.float32,
    )
    mid_out_part = jnp.einsum(
        "jd,cdi->jci", attention_rows, selected_output_down, preferred_element_type=jnp.float32
    )
    adapter_branch_sum, mid_out = head_sum((branch_part, mid_out_part))
    mid_out = mid_out * row_adapter_index[:, :, None]
    adapter_branch = adapter_branch_sum + ADAPTER_SCALE * jnp.einsum(
        "tsr,srd->td", mid_out, use_out_b.astype(jnp.float32), precision=highest_precision
    )
    x_mid = token_vals + adapter_branch
    mid_scale = lax.rsqrt(jnp.mean(x_mid * x_mid, axis=1, keepdims=True) + epsilon)
    hidden_after_experts = (x_mid * mid_scale * gain_mid).astype(jnp.bfloat16)
    mid_router = (
        jnp.einsum(
            "td,sdr->tsr", hidden_after_experts, use_router_a, preferred_element_type=jnp.float32
        )
        * row_adapter_index[:, :, None]
    )
    router_logits = jnp.dot(
        hidden_after_experts, w_router, preferred_element_type=jnp.float32
    ) + ADAPTER_SCALE * jnp.einsum(
        "tsr,sre->te", mid_router, use_router_b.astype(jnp.float32), precision=highest_precision
    )
    expert_probs = jax.nn.softmax(router_logits, axis=1)
    chosen = (routes[:, :, None] == jnp.arange(EXPERTS, dtype=jnp.int32)[None, None, :]).astype(
        jnp.float32
    )
    gates = jnp.sum(chosen * expert_probs[:, None, :], axis=2)
    pair_expert = routes.reshape(-1)
    pair_hot = (pair_expert[:, None] == jnp.arange(EXPERTS, dtype=jnp.int32)[None, :]).astype(
        jnp.int32
    )
    pair_rank = jnp.sum((jnp.cumsum(pair_hot, axis=0) - pair_hot) * pair_hot, axis=1)
    slot_of_pair = pair_expert * capacity + pair_rank
    pair_index = jnp.arange(row_count * TOPK, dtype=jnp.int32)
    slot_pair = jnp.zeros((EXPERTS * capacity,), jnp.int32).at[slot_of_pair].set(pair_index)
    slot_live = jnp.zeros((EXPERTS * capacity,), jnp.float32).at[slot_of_pair].set(1.0)
    slot_row_flat = slot_pair // TOPK
    slot_row = slot_row_flat.reshape(EXPERTS, capacity)
    slot_gate = (gates.reshape(-1)[slot_pair] * slot_live).reshape(EXPERTS, capacity)
    slot_sel = row_adapter_index[slot_row_flat].reshape(EXPERTS, capacity, use_count)
    slot_x = hidden_after_experts[slot_row_flat].reshape(EXPERTS, capacity, full_width)

    def run_experts(step_fn, initial):
        return run_piece(
            step_fn,
            initial,
            (
                lax.all_gather(w_gate_up, "fsdp", axis=0, tiled=True),
                lax.all_gather(w_down, "fsdp", axis=0, tiled=True),
            ),
        )

    def forward_step(acc_value, step_input):
        routed_sum, slot_dot, mid_keep, gu_keep = acc_value
        expert_gate_up_weight, expert_down_weight, expert_idx = step_input
        expert_rows = slot_x[expert_idx]
        expert_gate = slot_gate[expert_idx]
        expert_row = slot_row[expert_idx]
        expert_sel = slot_sel[expert_idx]
        mid_gu = (
            jnp.einsum(
                "cd,sdkr->cskr",
                expert_rows,
                use_gu_a[:, expert_idx],
                preferred_element_type=jnp.float32,
            )
            * expert_sel[:, :, None, None]
        )
        gate_up_rows = jnp.einsum(
            "cd,dko->cko", expert_rows, expert_gate_up_weight, preferred_element_type=jnp.float32
        ) + ADAPTER_SCALE * jnp.einsum(
            "cskr,srko->cko",
            mid_gu,
            use_gu_b[:, expert_idx].astype(jnp.float32),
            precision=highest_precision,
        )
        hidden_state = (jax.nn.silu(gate_up_rows[:, 0]) * gate_up_rows[:, 1]).astype(jnp.bfloat16)
        mid_down = (
            jnp.einsum(
                "cf,sfr->csr",
                hidden_state,
                use_down_a[:, expert_idx],
                preferred_element_type=jnp.float32,
            )
            * expert_sel[:, :, None]
        )
        expert_output_rows = jnp.dot(
            hidden_state, expert_down_weight, preferred_element_type=jnp.float32
        ) + ADAPTER_SCALE * jnp.einsum(
            "csr,srd->cd",
            mid_down,
            use_down_b[:, expert_idx].astype(jnp.float32),
            precision=highest_precision,
        )
        routed_sum = routed_sum.at[expert_row].add(expert_output_rows * expert_gate[:, None])
        slot_dot = slot_dot.at[expert_idx].set(
            jnp.sum(expert_output_rows * cot_vals[expert_row], axis=1)
        )
        mid_keep = mid_keep.at[expert_idx].set(mid_down)
        gu_keep = gu_keep.at[expert_idx].set(gate_up_rows)
        return ((routed_sum, slot_dot, mid_keep, gu_keep), None)

    forward_init = (
        jnp.zeros((row_count, full_width), jnp.float32),
        jnp.zeros((EXPERTS, capacity), jnp.float32),
        jnp.zeros((EXPERTS, capacity, use_count, RANK), jnp.float32),
        jnp.zeros((EXPERTS, capacity, 2, ff_local), jnp.float32),
    )
    routed_part, slot_dot_part, mid_keep_part, gu_keep = run_experts(forward_step, forward_init)
    routed_sum, slot_dot, mid_keep = head_sum((routed_part, slot_dot_part, mid_keep_part))
    mixed = (x_mid + routed_sum).astype(jnp.bfloat16)
    pair_dot = (
        jnp.zeros((row_count * TOPK,), jnp.float32)
        .at[slot_pair]
        .add(slot_dot.reshape(-1) * slot_live)
    )
    d_gates = pair_dot.reshape(row_count, TOPK)
    d_probs = jnp.sum(chosen * d_gates[:, :, None], axis=1)
    d_logits = (
        expert_probs * (d_probs - jnp.sum(expert_probs * d_probs, axis=1, keepdims=True))
    ).astype(jnp.bfloat16)
    d_mid_router = (
        ADAPTER_SCALE
        * jnp.einsum("te,sre->tsr", d_logits, use_router_b, preferred_element_type=jnp.float32)
        * row_adapter_index[:, :, None]
    )
    grad_router_b = spread(
        ADAPTER_SCALE
        * jnp.einsum(
            "tsr,te->sre", mid_router, d_logits.astype(jnp.float32), precision=highest_precision
        ),
        full_router_b,
    )
    grad_router_a = spread(
        jnp.einsum(
            "td,tsr->sdr",
            hidden_after_experts.astype(jnp.float32),
            d_mid_router,
            precision=highest_precision,
        ),
        full_router_a,
    )
    d_second = jnp.einsum(
        "te,de->td", d_logits, w_router, preferred_element_type=jnp.float32
    ) + jnp.einsum(
        "tsr,sdr->td", d_mid_router, use_router_a.astype(jnp.float32), precision=highest_precision
    )

    def backward_step(acc_value, step_input):
        d_rows, d_mid_gu, grad_gub, grad_dna, grad_dnb = acc_value
        expert_gate_up_weight, expert_down_weight, expert_idx = step_input
        expert_rows = slot_x[expert_idx]
        expert_gate = slot_gate[expert_idx]
        expert_row = slot_row[expert_idx]
        expert_sel = slot_sel[expert_idx]
        d_out = (expert_gate[:, None] * cot_vals[expert_row]).astype(jnp.bfloat16)
        d_mid_down = (
            ADAPTER_SCALE
            * jnp.einsum(
                "cd,srd->csr", d_out, use_down_b[:, expert_idx], preferred_element_type=jnp.float32
            )
            * expert_sel[:, :, None]
        )
        d_hidden = jnp.einsum(
            "cd,fd->cf", d_out, expert_down_weight, preferred_element_type=jnp.float32
        ) + jnp.einsum(
            "csr,sfr->cf",
            d_mid_down,
            use_down_a[:, expert_idx].astype(jnp.float32),
            precision=highest_precision,
        )
        gate_up_rows = gu_keep[expert_idx]
        gate_part = gate_up_rows[:, 0]
        up_part = gate_up_rows[:, 1]
        sigmoid_gate = jax.nn.sigmoid(gate_part)
        silu_gate = jax.nn.silu(gate_part)
        hidden_state = (silu_gate * up_part).astype(jnp.bfloat16)
        d_gate_part = d_hidden * up_part * sigmoid_gate * (1.0 + gate_part * (1.0 - sigmoid_gate))
        d_up_part = d_hidden * silu_gate
        d_gu = jnp.stack([d_gate_part, d_up_part], axis=1).astype(jnp.bfloat16)
        d_rows_e = jnp.einsum(
            "cko,dko->cd", d_gu, expert_gate_up_weight, preferred_element_type=jnp.float32
        )
        d_mid_part = (
            ADAPTER_SCALE
            * jnp.einsum(
                "cko,srko->cskr", d_gu, use_gu_b[:, expert_idx], preferred_element_type=jnp.float32
            )
            * expert_sel[:, :, None, None]
        )
        mid_gu = (
            jnp.einsum(
                "cd,sdkr->cskr",
                expert_rows,
                use_gu_a[:, expert_idx],
                preferred_element_type=jnp.float32,
            )
            * expert_sel[:, :, None, None]
        )
        grad_gub = grad_gub.at[:, expert_idx].set(
            ADAPTER_SCALE
            * jnp.einsum(
                "cskr,cko->srko", mid_gu, d_gu.astype(jnp.float32), precision=highest_precision
            )
        )
        grad_dna = grad_dna.at[:, expert_idx].set(
            jnp.einsum(
                "cf,csr->sfr",
                hidden_state.astype(jnp.float32),
                d_mid_down,
                precision=highest_precision,
            )
        )
        grad_dnb = grad_dnb.at[:, expert_idx].set(
            ADAPTER_SCALE
            * jnp.einsum(
                "csr,cd->srd",
                mid_keep[expert_idx],
                d_out.astype(jnp.float32),
                precision=highest_precision,
            )
        )
        d_rows = d_rows.at[expert_row].add(d_rows_e)
        d_mid_gu = d_mid_gu.at[expert_idx].set(d_mid_part)
        return ((d_rows, d_mid_gu, grad_gub, grad_dna, grad_dnb), None)

    backward_init = (
        jnp.zeros((row_count, full_width), jnp.float32),
        jnp.zeros((EXPERTS, capacity, use_count, 2, RANK), jnp.float32),
        jnp.zeros(use_gu_b.shape, jnp.float32),
        jnp.zeros(use_down_a.shape, jnp.float32),
        jnp.zeros(use_down_b.shape, jnp.float32),
    )
    d_rows_part, d_mid_gu_part, grad_gub_used, grad_dna_used, grad_dnb_used = run_experts(
        backward_step, backward_init
    )
    grad_gu_b = spread(grad_gub_used, full_gu_b)
    grad_down_a = spread(grad_dna_used, full_down_a)
    grad_down_b = spread(grad_dnb_used, full_down_b)
    d_rows_sum, d_mid_gu = head_sum((d_rows_part, d_mid_gu_part))

    def adapter_step(acc_value, expert_idx):
        d_rows, grad_gua = acc_value
        d_mid_rows = d_mid_gu[expert_idx]
        gate_up_first_factor = use_gu_a[:, expert_idx].astype(jnp.float32)
        d_rows = d_rows.at[slot_row[expert_idx]].add(
            jnp.einsum(
                "cskr,sdkr->cd", d_mid_rows, gate_up_first_factor, precision=highest_precision
            )
        )
        grad_gua = grad_gua.at[:, expert_idx].set(
            jnp.einsum(
                "cd,cskr->sdkr",
                slot_x[expert_idx].astype(jnp.float32),
                d_mid_rows,
                precision=highest_precision,
            )
        )
        return ((d_rows, grad_gua), None)

    (d_rows_sum, grad_gua_used), unused = lax.scan(
        adapter_step,
        (d_rows_sum, jnp.zeros(use_gu_a.shape, jnp.float32)),
        jnp.arange(EXPERTS, dtype=jnp.int32),
    )
    grad_gu_a = spread(grad_gua_used, full_gu_a)
    d_second = d_second + d_rows_sum
    d_x_mid = cot_vals + rms_back(x_mid, gain_mid, d_second, mid_scale, full_width)
    d_branch = d_x_mid.astype(jnp.bfloat16)
    columns = d_branch
    d_att = jnp.einsum(
        "tc,oc->to",
        columns,
        lax.all_gather(w_out, "fsdp", axis=1, tiled=True),
        preferred_element_type=jnp.float32,
    )
    gradient_output_middle = (
        ADAPTER_SCALE
        * jnp.einsum("td,srd->tsr", d_branch, use_out_b, preferred_element_type=jnp.float32)
        * row_adapter_index[:, :, None]
    )
    d_att = d_att + jnp.einsum(
        "fqd,qgd->fg",
        gradient_output_middle,
        selected_output_down.astype(jnp.float32),
        precision=highest_precision,
    )
    grad_out_b = spread(
        ADAPTER_SCALE
        * jnp.einsum(
            "tsr,td->srd", mid_out, d_branch.astype(jnp.float32), precision=highest_precision
        ),
        full_out_b,
    )
    grad_out_a = spread(
        jnp.einsum(
            "ia,ihu->hau",
            attention_rows.astype(jnp.float32),
            gradient_output_middle,
            precision=highest_precision,
        ),
        full_out_a,
    )
    d_att_rows = d_att.reshape(row_count, local_heads, HEAD_DIM).astype(jnp.bfloat16)
    d_att_cont = d_att_rows[prompt_rows:].reshape(cont_count, CONT_LEN, local_heads, HEAD_DIM)

    def delta_step(acc_value, step_input):
        key_block, value_block, first_row = step_input
        raw_scores, allowed = block_scores(key_block, first_row)
        weights = jnp.where(allowed, jnp.exp(raw_scores - log_total[:, :, None]), 0.0)
        d_weights = jnp.einsum(
            "thd,khd->htk", d_att_rows, value_block, preferred_element_type=jnp.float32
        )
        return (acc_value + jnp.sum(weights * d_weights, axis=2), None)

    delta, unused = lax.scan(
        delta_step,
        jnp.zeros((local_heads, row_count), jnp.float32),
        (key_blocks, value_blocks, block_starts),
    )
    own_dw = jnp.einsum(
        "cqhd,ckhd->hcqk", d_att_cont, value_cont, preferred_element_type=jnp.float32
    )
    own_delta = jnp.sum(own_probs * own_dw, axis=3).reshape(local_heads, -1)
    delta = delta + jnp.concatenate(
        [jnp.zeros((local_heads, prompt_rows), jnp.float32), own_delta], axis=1
    )
    delta_cont = delta[:, prompt_rows:].reshape(local_heads, cont_count, CONT_LEN)

    def grad_step(d_query, step_input):
        key_block, value_block, first_row = step_input
        raw_scores, allowed = block_scores(key_block, first_row)
        weights = jnp.where(allowed, jnp.exp(raw_scores - log_total[:, :, None]), 0.0)
        d_weights = jnp.einsum(
            "thd,khd->htk", d_att_rows, value_block, preferred_element_type=jnp.float32
        )
        d_scores = (weights * (d_weights - delta[:, :, None])).astype(jnp.bfloat16)
        d_query = (
            d_query
            + jnp.einsum("htk,khd->thd", d_scores, key_block, preferred_element_type=jnp.float32)
            * score_scale
        )
        d_key = (
            jnp.einsum("htk,thd->khd", d_scores, query_rows, preferred_element_type=jnp.float32)
            * score_scale
        )
        d_value = jnp.einsum(
            "htk,thd->khd",
            weights.astype(jnp.bfloat16),
            d_att_rows,
            preferred_element_type=jnp.float32,
        )
        return (d_query, (d_key, d_value))

    d_query, (d_key_blocks, d_value_blocks) = lax.scan(
        grad_step,
        jnp.zeros((row_count, local_heads, HEAD_DIM), jnp.float32),
        (key_blocks, value_blocks, block_starts),
    )
    own_ds = (own_probs * (own_dw - delta_cont[..., None])).astype(jnp.bfloat16)
    own_dq = (
        jnp.einsum("hcqk,ckhd->cqhd", own_ds, key_cont, preferred_element_type=jnp.float32)
        * score_scale
    )
    own_dk = (
        jnp.einsum("hcqk,cqhd->ckhd", own_ds, query_cont, preferred_element_type=jnp.float32)
        * score_scale
    )
    own_dv = jnp.einsum(
        "hcqk,cqhd->ckhd",
        own_probs.astype(jnp.bfloat16),
        d_att_cont,
        preferred_element_type=jnp.float32,
    )
    d_query = d_query + jnp.concatenate(
        [
            jnp.zeros((prompt_rows, local_heads, HEAD_DIM), jnp.float32),
            own_dq.reshape(-1, local_heads, HEAD_DIM),
        ],
        axis=0,
    )
    prompt_dk, prompt_dv = (
        lax.psum_scatter(
            d_key_blocks.reshape(PROMPT, local_heads, HEAD_DIM).astype(jnp.bfloat16),
            "ctx",
            scatter_dimension=0,
            tiled=True,
        ).astype(jnp.float32),
        lax.psum_scatter(
            d_value_blocks.reshape(PROMPT, local_heads, HEAD_DIM).astype(jnp.bfloat16),
            "ctx",
            scatter_dimension=0,
            tiled=True,
        ).astype(jnp.float32),
    )
    d_key = jnp.concatenate([prompt_dk, own_dk.reshape(-1, local_heads, HEAD_DIM)], axis=0)
    d_value = jnp.concatenate([prompt_dv, own_dv.reshape(-1, local_heads, HEAD_DIM)], axis=0)
    d_q_norm = rotate(d_query, cosine, -sine_part).reshape(row_count, local_width)
    d_k_norm = rotate(d_key, cosine, -sine_part).reshape(row_count, local_width)
    dot_q, dot_k = head_sum(
        (jnp.sum(gain_q * q_raw * d_q_norm, axis=1), jnp.sum(gain_k * k_raw * d_k_norm, axis=1))
    )
    d_q_raw = (
        q_scale * gain_q * d_q_norm
        - q_raw * (q_scale * q_scale * q_scale) * dot_q[:, None] / full_width
    )
    d_k_raw = (
        k_scale * gain_k * d_k_norm
        - k_raw * (k_scale * k_scale * k_scale) * dot_k[:, None] / full_width
    )
    d_proj = jnp.stack([d_q_raw, d_k_raw, d_value.reshape(row_count, local_width)], axis=1).astype(
        jnp.bfloat16
    )
    d_first_part = jnp.einsum(
        "tjo,djo->td",
        d_proj,
        lax.all_gather(w_qkv, "fsdp", axis=0, tiled=True),
        preferred_element_type=jnp.float32,
    )
    d_mid_qkv_part = jnp.einsum(
        "tjo,srjo->tsjr", d_proj, use_qkv_b, preferred_element_type=jnp.float32
    )
    d_first_sum, gradient_projection_middle = head_sum((d_first_part, d_mid_qkv_part))
    gradient_projection_middle = (
        ADAPTER_SCALE * gradient_projection_middle * row_adapter_index[:, :, None, None]
    )
    d_first = d_first_sum + jnp.einsum(
        "tsjr,sdjr->td",
        gradient_projection_middle,
        use_qkv_a.astype(jnp.float32),
        precision=highest_precision,
    )
    grad_qkv_b = spread(
        ADAPTER_SCALE
        * jnp.einsum(
            "tsjr,tjo->srjo", mid_qkv, d_proj.astype(jnp.float32), precision=highest_precision
        ),
        full_qkv_b,
    )
    grad_qkv_a = spread(
        jnp.einsum(
            "td,tsjr->sdjr",
            hidden_after_attention.astype(jnp.float32),
            gradient_projection_middle,
            precision=highest_precision,
        ),
        full_qkv_a,
    )
    grad_input = d_x_mid + rms_back(token_vals, gain_in, d_first, first_scale, full_width)
    (
        share_qkv_a,
        share_qkv_b,
        share_out_a,
        share_out_b,
        share_router_a,
        share_router_b,
        share_gu_a,
        share_gu_b,
        share_down_a,
        share_down_b,
    ) = (
        lax.psum_scatter(
            grad_qkv_a.astype(jnp.bfloat16), "fsdp", scatter_dimension=0, tiled=True
        ).astype(jnp.float32),
        lax.psum_scatter(
            grad_qkv_b.astype(jnp.bfloat16), "fsdp", scatter_dimension=0, tiled=True
        ).astype(jnp.float32),
        lax.psum_scatter(
            grad_out_a.astype(jnp.bfloat16), "fsdp", scatter_dimension=0, tiled=True
        ).astype(jnp.float32),
        lax.psum_scatter(
            grad_out_b.astype(jnp.bfloat16), "fsdp", scatter_dimension=0, tiled=True
        ).astype(jnp.float32),
        lax.psum_scatter(
            grad_router_a.astype(jnp.bfloat16), "fsdp", scatter_dimension=0, tiled=True
        ).astype(jnp.float32),
        lax.psum_scatter(
            grad_router_b.astype(jnp.bfloat16), "fsdp", scatter_dimension=0, tiled=True
        ).astype(jnp.float32),
        lax.psum_scatter(
            grad_gu_a.astype(jnp.bfloat16), "fsdp", scatter_dimension=0, tiled=True
        ).astype(jnp.float32),
        lax.psum_scatter(
            grad_gu_b.astype(jnp.bfloat16), "fsdp", scatter_dimension=0, tiled=True
        ).astype(jnp.float32),
        lax.psum_scatter(
            grad_down_a.astype(jnp.bfloat16), "fsdp", scatter_dimension=0, tiled=True
        ).astype(jnp.float32),
        lax.psum_scatter(
            grad_down_b.astype(jnp.bfloat16), "fsdp", scatter_dimension=0, tiled=True
        ).astype(jnp.float32),
    )
    (
        total_qkv_a,
        total_qkv_b,
        total_out_a,
        total_out_b,
        total_router_a,
        total_router_b,
        total_gu_a,
        total_gu_b,
        total_down_a,
        total_down_b,
    ) = (
        lax.psum(share_qkv_a.astype(jnp.bfloat16), "ctx").astype(jnp.float32),
        lax.psum(share_qkv_b.astype(jnp.bfloat16), "ctx").astype(jnp.float32),
        lax.psum(share_out_a.astype(jnp.bfloat16), "ctx").astype(jnp.float32),
        lax.psum(share_out_b.astype(jnp.bfloat16), "ctx").astype(jnp.float32),
        lax.psum(share_router_a.astype(jnp.bfloat16), "ctx").astype(jnp.float32),
        lax.psum(share_router_b.astype(jnp.bfloat16), "ctx").astype(jnp.float32),
        lax.psum(share_gu_a.astype(jnp.bfloat16), "ctx").astype(jnp.float32),
        lax.psum(share_gu_b.astype(jnp.bfloat16), "ctx").astype(jnp.float32),
        lax.psum(share_down_a.astype(jnp.bfloat16), "ctx").astype(jnp.float32),
        lax.psum(share_down_b.astype(jnp.bfloat16), "ctx").astype(jnp.float32),
    )
    return (
        mixed,
        grad_input,
        total_qkv_a,
        total_qkv_b,
        total_out_a,
        total_out_b,
        total_router_a,
        total_router_b,
        total_gu_a,
        total_gu_b,
        total_down_a,
        total_down_b,
    )


def solution(mesh):
    return jax.shard_map(
        per_device,
        mesh=mesh,
        in_specs=(
            P(("fsdp", "ctx"), None),
            P(("fsdp", "ctx"), None),
            P(("fsdp", "ctx"), None),
            P("fsdp", None),
            P(),
            P(),
            P("tp"),
            P("tp"),
            P("fsdp", None, "tp"),
            P("tp", "fsdp"),
            P(),
            P("fsdp", None, None, "tp"),
            P("fsdp", "tp", None),
            P("fsdp", None, None, None),
            P("fsdp", None, None, "tp"),
            P("fsdp", "tp", None),
            P("fsdp", None, None),
            P("fsdp", None, None),
            P("fsdp", None, None),
            P("fsdp", None, None, None, None),
            P("fsdp", None, None, None, "tp"),
            P("fsdp", None, "tp", None),
            P("fsdp", None, None, None),
        ),
        out_specs=(
            P(("fsdp", "ctx"), None),
            P(("fsdp", "ctx"), None),
            P("fsdp", None, None, None),
            P("fsdp", None, None, "tp"),
            P("fsdp", "tp", None),
            P("fsdp", None, None),
            P("fsdp", None, None),
            P("fsdp", None, None),
            P("fsdp", None, None, None, None),
            P("fsdp", None, None, None, "tp"),
            P("fsdp", None, "tp", None),
            P("fsdp", None, None, None),
        ),
        check_vma=False,
    )
```

profile of v0, /device:TPU:0, one launch (start us, length us, event | category | flops | bytes accessed | tf_op | source)
XLA Modules:
  0.0 7150.0 jit_solution(13652431195613193092)
XLA Ops:
  14.1 31.0 all_gather.53
  65.7 212.9 %all-gather.12.cloned.1.call-done = bf16[2048,3,1024]{0,2,1:T(8,128)(2,1)} async-done(((bf16[512,3,1024]{0,2,1:T(8,128)(2,1)}), bf16[2048,3,1024]{0,2,1:T(8,128)(2,1)}) %all-gather.12.cloned.1.call-update) | async-done | bytes 12582928 | tf_op jit(solution)/shard_map/all_gather | solution.py:162
  403.5 73.2 %while.107 = (s32[]{:T(128)}, f32[8,1024]{1,0:T(8,128)S(1)}, f32[8,1024]{1,0:T(8,128)S(1)}, s32[4]{0:T(128)S(1)}, bf16[4,512,8,128]{3,1,2,0:T(8,128)(2,1)}, /*in...) while((s32[]{:T(128)}, f32[8,1024]{1,0:T(8,128)S(1)}, ...), condition=%wide.region_8.9_spmd.clone, body=%wide.region_5.8_spmd.clone.sunk | while | flops 1107874304 | bytes 38711428 | solution.py:222
  476.8 59.1 while.108
  604.0 30.5 scatter_custom_fusion.3
  635.8 31.2 gather_fusion.8
  691.1 22.2 all_gather.66
  720.6 31.0 scatter_custom_fusion.4
  760.1 61.1 all-gather.32.cloned.1.call-done
  827.7 279.9 %all-gather.26.cloned.1.call-done = bf16[8,16,2048,2,16]{2,4,3,1,0:T(8,128)(2,1)} async-done(((bf16[2,16,2048,2,16]{2,4,3,1,0:T(8,128)(2,1)}), bf16[8,16,2048,2,16]{2,4,3,1,0:T(8,128)(2,1)}) %all-gather.26.cloned.1.call-update) | async-done | bytes 16777232 | tf_op jit(solution)/shard_map/all_gather | solution.py:128
  1164.6 72.3 %gather_fusion.6 = bf16[9216,2048]{1,0:T(8,128)(2,1)} fusion(bf16[1024,2048]{1,0:T(8,128)(2,1)} %multiply_convert_fusion.4, s32[9216]{0:T(1024)S(1)} %get-tuple-element.1277), kind=kCustom, calls=%fused_computation.6 | custom fusion | bytes 75534336 | tf_op jit(solution)/shard_map/gather | solution.py:334
  1243.5 51.2 gather_fusion.13
  1294.8 417.0 %all-gather.28.cloned.1.call-done = bf16[16,512,2048]{2,1,0:T(8,128)(2,1)} async-done(((bf16[4,512,2048]{2,1,0:T(8,128)(2,1)}), bf16[16,512,2048]{2,1,0:T(8,128)(2,1)}) %all-gather.28.cloned.1.call-update) | async-done | bytes 33554448 | tf_op jit(solution)/shard_map/all_gather | solution.py:342
  1711.7 1110.3 %all-gather.22.cloned.1.call-done = bf16[16,2048,2,512]{3,1,2,0:T(8,128)(2,1)} async-done(((bf16[4,2048,2,512]{3,1,2,0:T(8,128)(2,1)}), bf16[16,2048,2,512]{3,1,2,0:T(8,128)(2,1)}) %all-gather.22.cloned.1.call-update) | async-done | bytes 67108880 | tf_op jit(solution)/shard_map/all_gather | solution.py:341
  2839.3 1008.0 %while.104 = (s32[]{:T(128)}, f32[1024,2048]{1,0:T(8,128)}, f32[16,576]{1,0:T(8,128)S(1)}, f32[16,576,3,16]{1,3,2,0:T(8,128)S(1)}, f32[16,576,2,512]{3,1,2,0:T(8...) while((s32[]{:T(128)}, f32[1024,2048]{1,0:T(8,128)}, ...), condition=%wide.region_29.30_spmd, body=%wide.region_24.29_spmd.sunk | while | flops 4908656128 | bytes 84455304 | solution.py:55
  2879.4 22.2 scatter_custom_fusion.29
  2942.4 22.2 scatter_custom_fusion.29
  3005.4 22.2 scatter_custom_fusion.29
  3068.4 22.2 scatter_custom_fusion.29
  3131.3 22.2 scatter_custom_fusion.29
  3194.3 22.2 scatter_custom_fusion.29
  3257.2 22.2 scatter_custom_fusion.29
  3320.2 22.2 scatter_custom_fusion.29
  3383.1 22.2 scatter_custom_fusion.29
  3446.1 22.2 scatter_custom_fusion.29
  3509.1 22.2 scatter_custom_fusion.29
  3572.0 22.2 scatter_custom_fusion.29
  3634.9 22.2 scatter_custom_fusion.29
  3697.9 22.2 scatter_custom_fusion.29
  3760.9 22.2 scatter_custom_fusion.29
  3823.9 22.2 scatter_custom_fusion.29
  3881.6 1182.7 %while.105 = (s32[]{:T(128)}, f32[1024,2048]{1,0:T(8,128)}, f32[16,576,3,2,16]{1,4,2,3,0:T(8,128)}, f32[3,16,16,2,512]{4,2,3,1,0:T(8,128)}, f32[3,16,512,16]{2,3...) while((s32[]{:T(128)}, f32[1024,2048]{1,0:T(8,128)}, ...), condition=%wide.region_41.42_spmd, body=%wide.region_36.41_spmd.sunk | while | flops 5392688640 | bytes 95125888 | solution.py:55
  3915.8 21.9 scatter_custom_fusion.31
  3989.8 21.9 scatter_custom_fusion.31
  4063.7 21.9 scatter_custom_fusion.31
  4137.6 21.9 scatter_custom_fusion.31
  4211.5 21.9 scatter_custom_fusion.31
  4285.4 21.9 scatter_custom_fusion.31
  4359.3 21.9 scatter_custom_fusion.31
  4433.3 21.9 scatter_custom_fusion.31
  4507.2 21.9 scatter_custom_fusion.31
  4581.1 21.9 scatter_custom_fusion.31
  4654.9 21.9 scatter_custom_fusion.31
  4728.8 21.9 scatter_custom_fusion.31
  4802.7 21.9 scatter_custom_fusion.31
  4876.6 21.9 scatter_custom_fusion.31
  4950.5 21.9 scatter_custom_fusion.31
  5024.4 21.9 scatter_custom_fusion.31
  5074.3 63.7 scatter_custom_fusion.5
  5149.7 595.9 %while.106 = (s32[]{:T(128)}, f32[1024,2048]{1,0:T(8,128)}, f32[3,16,2048,2,16]{2,4,3,1,0:T(8,128)}, s32[16]{0:T(128)S(1)}, s32[16,576]{1,0:T(8,128)}, /*index=5...) while((s32[]{:T(128)}, f32[1024,2048]{1,0:T(8,128)}, ...), condition=%wide.region_47.48_spmd, body=%wide.region_44.47_spmd.sunk | while | flops 2719287040 | bytes 24223500 | solution.py:554
  5270.1 21.8 scatter_custom_fusion.33
  5381.9 21.8 scatter_custom_fusion.33
  5530.9 21.8 scatter_custom_fusion.33
  5784.3 50.5 while.109
  5840.5 193.5 %while.110 = (s32[]{:T(128)}, f32[1024,8,128]{0,2,1:T(8,128)}, bf16[4,512,8,128]{3,2,1,0:T(8,128)(2,1)}, bf16[4,512,8,128]{3,2,1,0:T(8,128)(2,1)}, bf16[4,512,8,...) while((s32[]{:T(128)}, f32[1024,8,128]{0,2,1:T(8,128)}, ...), condition=%wide.region_54.55_spmd.clone, body=%wide.region_53.54_spmd.clone.sunk | while | flops 5415383552 | bytes 111784152 | solution.py:648
  6325.3 54.4 reduce-scatter.31.cloned.1.call-done
  6379.7 23.4 reduce-scatter.21.cloned.1.call-done
  6403.2 22.4 reduce-scatter.23.cloned.1.call-done
  6425.5 145.2 %reduce-scatter.35.cloned.1.call-done = bf16[2,16,16,2048]{3,2,1,0:T(8,128)(2,1)} async-done(((bf16[8,16,16,2048]{3,2,1,0:T(8,128)(2,1)}), bf16[2,16,16,2048]{3,2,1,0:T(8,128)(2,1)}) %reduce-scatter.35.cloned.1.call-update) | async-done | bytes 2097168 | tf_op jit(solution)/shard_map/reduce_scatter | solution.py:782
  6570.8 26.5 reduce-scatter.19.cloned.1.call-done
  6597.3 37.9 reduce-scatter.17.cloned.1.call-done
  6635.2 281.5 %reduce-scatter.29.cloned.1.call-done = bf16[2,16,2048,2,16]{2,4,3,1,0:T(8,128)(2,1)} async-done(((bf16[8,16,2048,2,16]{2,4,3,1,0:T(8,128)(2,1)}), bf16[2,16,2048,2,16]{2,4,3,1,0:T(8,128)(2,1)}) %reduce-scatter.29.cloned.1.call-update) | async-done | bytes 4194320 | tf_op jit(solution)/shard_map/reduce_scatter | solution.py:773
  6916.7 22.5 reduce-scatter.27.cloned.1.call-done
  6972.1 149.4 %all-reduce.25.cloned.1.call-done = (bf16[2,16,16,2,512]{4,2,3,1,0:T(8,128)(2,1)}, bf16[2,2048,3,16]{1,3,2,0:T(8,128)(2,1)}, bf16[2,16,3,1024]{3,1,2,0:T(8,128)(...) async-done(((bf16[2,16,16,2,512]{4,2,3,1,0:T(8,128)(2,1)}, ...) | async-done | bytes 8781840 | tf_op jit(solution)/shard_map/psum | solution.py:805
  (1737 shorter events, 3085.1 us)
Async XLA Ops:
  7.2 1229.8 %copy-start = (bf16[2048,16]{0,1:T(8,128)(2,1)S(1)}, bf16[2048,16]{0,1:T(8,128)(2,1)}, u32[]{:S(2)}) copy-start(bf16[2048,16]{0,1:T(8,128)(2,1)} %param.63) | copy-start | bytes 196612
  7.2 51.7 all-gather.14.cloned.1.call-start
  8.0 270.6 %all-gather.12.cloned.1.call-start = ((), (), s32[]{:S(2)}) async-start(), calls=%async_computation.12 | async-start | bytes 15728640 | tf_op jit(solution)/shard_map/all_gather | solution.py:162
  12.7 36.7 copy-start.136
  12.7 36.7 copy-start.137
  12.7 385.6 %all-gather.18.cloned.1.call-start = ((), (), s32[]{:S(2)}) async-start(), calls=%async_computation.15 | async-start | bytes 5242880 | tf_op jit(solution)/shard_map/all_gather | solution.py:189
  12.8 265.8 %copy-start.118 = (f32[2048]{0:T(1024)}, f32[2048]{0:T(1024)S(1)}, u32[]{:S(2)}) copy-start(f32[2048]{0:T(1024)S(1)} %convert_element_type.229) | copy-start | bytes 24580
  13.6 47.3 copy-start.3
  13.8 284.1 %copy-start.64 = (f32[1024,3]{0,1:T(4,128)}, f32[1024,3]{0,1:T(4,128)S(1)}, u32[]{:S(2)}) copy-start(f32[1024,3]{0,1:T(4,128)S(1)} %copy.267) | copy-start | bytes 36868
  14.0 39.0 copy-start.106
  14.1 359.8 %copy-start.120 = (s32[1024]{0:T(1024)}, s32[1024]{0:T(1024)S(1)}, u32[]{:S(2)}) copy-start(s32[1024]{0:T(1024)S(1)} %pad_clamp_fusion.2) | copy-start | bytes 12292
  45.6 252.4 %copy-start.37 = (bf16[3,16,3,1024]{3,1,2,0:T(8,128)(2,1)}, bf16[3,16,3,1024]{3,1,2,0:T(8,128)(2,1)S(1)}, u32[]{:S(2)}) copy-start(bf16[3,16,3,1024]{3,1,2,0:T(8,128)(2,1)S(1)} %gather_fusion.2) | copy-start | bytes 884740
  45.7 329.8 %copy-start.93 = (pred[3]{0:T(512)(128)(4,1)}, pred[3]{0:T(512)(128)(4,1)S(1)}, u32[]{:S(2)}) copy-start(pred[3]{0:T(512)(128)(4,1)S(1)} %compare_and_fusion) | copy-start | bytes 13
  49.5 229.1 %copy-start.123 = (f32[1024]{0:T(1024)}, f32[1024]{0:T(1024)S(1)}, u32[]{:S(2)}) copy-start(f32[1024]{0:T(1024)S(1)} %get-tuple-element.1284) | copy-start | bytes 12292
  53.0 288.1 %copy-start.31 = (f32[1024,64]{1,0:T(8,128)}, f32[1024,64]{1,0:T(8,128)S(1)}, u32[]{:S(2)}) copy-start(f32[1024,64]{1,0:T(8,128)S(1)} %get-tuple-element.1282) | copy-start | bytes 786436
  65.7 232.3 %copy-start.63 = (f32[1024,144]{0,1}, f32[1024,144]{0,1:S(1)}, u32[]{:S(2)}) copy-start(f32[1024,144]{0,1:S(1)} %fusion.391) | copy-start | bytes 1769476
  345.3 30.3 copy-start.16
  347.4 33.5 copy-start.26
  347.4 129.4 %all-gather.16.cloned.1.call-start = ((), (), s32[]{:S(2)}) async-start(), calls=%async_computation.14 | async-start | bytes 5242880 | tf_op jit(solution)/shard_map/all_gather | solution.py:190
  353.2 198.8 %all-gather.20.cloned.1.call-start = ((), (), s32[]{:S(2)}) async-start(), calls=%async_computation.16 | async-start | bytes 5242880 | tf_op jit(solution)/shard_map/all_gather | solution.py:291
  353.8 398.6 %all-gather.30.cloned.1.call-start = ((), (), s32[]{:S(2)}) async-start(), calls=%async_computation.21 | async-start | bytes 2621440 | tf_op jit(solution)/shard_map/all_gather | solution.py:130
  354.4 401.3 %all-gather.24.cloned.1.call-start = ((), (), s32[]{:S(2)}) async-start(), calls=%async_computation.18 | async-start | bytes 5242880 | tf_op jit(solution)/shard_map/all_gather | solution.py:129
  357.1 464.1 %all-gather.32.cloned.1.call-start = ((), (), s32[]{:S(2)}) async-start(), calls=%async_computation.22 | async-start | bytes 10485760 | tf_op jit(solution)/shard_map/all_gather | solution.py:131
  357.9 749.8 %all-gather.26.cloned.1.call-start = ((), (), s32[]{:S(2)}) async-start(), calls=%async_computation.19 | async-start | bytes 20971520 | tf_op jit(solution)/shard_map/all_gather | solution.py:128
  358.6 788.9 %all-reduce.23.cloned.1.call-start = ((), (), s32[]{:S(2)}) async-start(), calls=%async_computation.38 | async-start | bytes 17170432 | tf_op jit(solution)/shard_map/psum | solution.py:23
  375.5 166.6 %copy-start.54 = (pred[256,256]{0,1:T(8,128)(4,1)}, pred[256,256]{0,1:T(8,128)(4,1)S(1)}, u32[]{:S(2)}) copy-start(pred[256,256]{0,1:T(8,128)(4,1)S(1)} %iota_compare_fusion.8) | copy-start | bytes 196612
  375.6 174.9 %copy-start.78 = (bf16[3,1024,16]{1,2,0:T(8,128)(2,1)}, bf16[3,1024,16]{1,2,0:T(8,128)(2,1)S(1)}, u32[]{:S(2)}) copy-start(bf16[3,1024,16]{1,2,0:T(8,128)(2,1)S(1)} %broadcast_select_fusion.8) | copy-start | bytes 294916
  561.1 1150.7 %all-gather.28.cloned.1.call-start = ((), (), s32[]{:S(2)}) async-start(), calls=%async_computation.20 | async-start | bytes 41943040 | tf_op jit(solution)/shard_map/all_gather | solution.py:342
  561.8 2260.2 %all-gather.22.cloned.1.call-start = ((), (), s32[]{:S(2)}) async-start(), calls=%async_computation.17 | async-start | bytes 83886080 | tf_op jit(solution)/shard_map/all_gather | solution.py:341
  577.8 58.0 copy-start.135
  577.8 58.0 copy-start.4
  577.8 3290.2 %all-reduce.17.cloned.1.call-start = ((), (), s32[]{:S(2)}) async-start(), calls=%async_computation.23 | async-start | bytes 3932160 | tf_op jit(solution)/shard_map/psum | solution.py:23
  597.2 550.4 %copy-start.50 = (bf16[3,16,2048]{2,1,0:T(8,128)(2,1)}, bf16[3,16,2048]{2,1,0:T(8,128)(2,1)S(1)}, u32[]{:S(2)}) copy-start(bf16[3,16,2048]{2,1,0:T(8,128)(2,1)S(1)} %gather_fusion.5) | copy-start | bytes 589828
  635.8 520.7 %copy-start.89 = (f32[2048]{0:T(1024)}, f32[2048]{0:T(1024)S(1)}, u32[]{:S(2)}) copy-start(f32[2048]{0:T(1024)S(1)} %convert_element_type.240) | copy-start | bytes 24580
  713.9 37.8 copy-start.94
  1243.5 51.2 copy-start.80
  3848.6 1295.0 %all-reduce.21.cloned.1.call-start = ((), (), s32[]{:S(2)}) async-start(), calls=%async_computation.37 | async-start | bytes 24641536 | tf_op jit(solution)/shard_map/psum | solution.py:23
  5064.3 1023.7 %reduce-scatter.13.cloned.1.call-start = ((), (), s32[]{:S(2)}) async-start(), calls=%async_computation.24 | async-start | bytes 5242880 | tf_op jit(solution)/shard_map/reduce_scatter | solution.py:676
  5065.4 700.5 %copy-start.76 = (f32[1024,3]{0,1:T(4,128)}, f32[1024,3]{0,1:T(4,128)S(1)}, u32[]{:S(2)}) copy-start(f32[1024,3]{0,1:T(4,128)S(1)} %copy.297) | copy-start | bytes 36868
  5065.4 73.1 %copy-start.75 = (s32[1024,8]{0,1:T(8,128)S(1)}, s32[1024,8]{0,1:T(8,128)}, u32[]{:S(2)}) copy-start(s32[1024,8]{0,1:T(8,128)} %param.55) | copy-start | bytes 98308
  5065.4 73.2 %copy-start.58 = (f32[1024,16]{0,1:T(8,128)S(1)}, f32[1024,16]{0,1:T(8,128)}, u32[]{:S(2)}) copy-start(f32[1024,16]{0,1:T(8,128)} %copy-done.57) | copy-start | bytes 196612
  5065.4 73.2 %copy-start.100 = (f32[1024]{0:T(1024)S(1)}, f32[1024]{0:T(1024)}, u32[]{:S(2)}) copy-start(f32[1024]{0:T(1024)} %copy-done.99) | copy-start | bytes 12292
  5065.4 73.2 %copy-start.105 = (f32[1024]{0:T(1024)S(1)}, f32[1024]{0:T(1024)}, u32[]{:S(2)}) copy-start(f32[1024]{0:T(1024)} %copy-done.104) | copy-start | bytes 12292
  5065.4 73.3 %copy-start.95 = (pred[3]{0:T(512)(128)(4,1)S(1)}, pred[3]{0:T(512)(128)(4,1)}, u32[]{:S(2)}) copy-start(pred[3]{0:T(512)(128)(4,1)} %copy-done.93) | copy-start | bytes 13
  5065.4 73.3 %copy-start.98 = (bf16[3,16,16]{2,1,0:T(8,128)(2,1)S(1)}, bf16[3,16,16]{2,1,0:T(8,128)(2,1)}, u32[]{:S(2)}) copy-start(bf16[3,16,16]{2,1,0:T(8,128)(2,1)} %gather_fusion.12) | copy-start | bytes 4612
  5138.9 606.7 %copy-start.44 = (f32[1024,3,16]{0,2,1:T(8,128)}, f32[1024,3,16]{0,2,1:T(8,128)S(1)}, u32[]{:S(2)}) copy-start(f32[1024,3,16]{0,2,1:T(8,128)S(1)} %convolution_multiply_fusion) | copy-start | bytes 589828
  5149.7 595.9 %copy-start.49 = (bf16[3,2048,16]{1,2,0:T(8,128)(2,1)S(1)}, bf16[3,2048,16]{1,2,0:T(8,128)(2,1)}, u32[]{:S(2)}) copy-start(bf16[3,2048,16]{1,2,0:T(8,128)(2,1)} %broadcast_select_fusion.6) | copy-start | bytes 589828
  5149.7 595.9 %copy-start.90 = (f32[2048]{0:T(1024)S(1)}, f32[2048]{0:T(1024)}, u32[]{:S(2)}) copy-start(f32[2048]{0:T(1024)} %copy-done.89) | copy-start | bytes 24580
  5784.2 50.5 copy-start.34
  5784.2 50.5 copy-start.55
  5784.2 50.5 copy-start.86
  6034.1 109.5 %reduce-scatter.15.cloned.1.call-start = ((), (), s32[]{:S(2)}) async-start(), calls=%async_computation.25 | async-start | bytes 5242880 | tf_op jit(solution)/shard_map/reduce_scatter | solution.py:682
  6034.6 230.2 %all-reduce.19.cloned.1.call-start = ((), (), s32[]{:S(2)}) async-start(), calls=%async_computation.36 | async-start | bytes 34734080 | tf_op jit(solution)/shard_map/psum | solution.py:23
  6169.2 156.1 %reduce-scatter.25.cloned.1.call-start = ((), (), s32[]{:S(2)}) async-start(), calls=%async_computation.30 | async-start | bytes 655360 | tf_op jit(solution)/shard_map/reduce_scatter | solution.py:767
  6176.4 148.9 %reduce-scatter.33.cloned.1.call-start = ((), (), s32[]{:S(2)}) async-start(), calls=%async_computation.34 | async-start | bytes 2621440 | tf_op jit(solution)/shard_map/reduce_scatter | solution.py:779
  6188.3 191.4 %reduce-scatter.31.cloned.1.call-start = ((), (), s32[]{:S(2)}) async-start(), calls=%async_computation.33 | async-start | bytes 5242880 | tf_op jit(solution)/shard_map/reduce_scatter | solution.py:776
  6208.3 194.9 %reduce-scatter.21.cloned.1.call-start = ((), (), s32[]{:S(2)}) async-start(), calls=%async_computation.28 | async-start | bytes 327680 | tf_op jit(solution)/shard_map/reduce_scatter | solution.py:761
  6214.2 211.3 %reduce-scatter.23.cloned.1.call-start = ((), (), s32[]{:S(2)}) async-start(), calls=%async_computation.29 | async-start | bytes 655360 | tf_op jit(solution)/shard_map/reduce_scatter | solution.py:764
  6223.0 347.8 %reduce-scatter.35.cloned.1.call-start = ((), (), s32[]{:S(2)}) async-start(), calls=%async_computation.35 | async-start | bytes 10485760 | tf_op jit(solution)/shard_map/reduce_scatter | solution.py:782
  6253.3 344.0 %reduce-scatter.19.cloned.1.call-start = ((), (), s32[]{:S(2)}) async-start(), calls=%async_computation.27 | async-start | bytes 983040 | tf_op jit(solution)/shard_map/reduce_scatter | solution.py:758
  6264.8 370.4 %reduce-scatter.17.cloned.1.call-start = ((), (), s32[]{:S(2)}) async-start(), calls=%async_computation.26 | async-start | bytes 1966080 | tf_op jit(solution)/shard_map/reduce_scatter | solution.py:755
  6275.4 641.3 %reduce-scatter.29.cloned.1.call-start = ((), (), s32[]{:S(2)}) async-start(), calls=%async_computation.32 | async-start | bytes 20971520 | tf_op jit(solution)/shard_map/reduce_scatter | solution.py:773
  6322.8 616.5 %reduce-scatter.27.cloned.1.call-start = ((), (), s32[]{:S(2)}) async-start(), calls=%async_computation.31 | async-start | bytes 40960 | tf_op jit(solution)/shard_map/reduce_scatter | solution.py:770
  6325.2 796.2 %all-reduce.25.cloned.1.call-start = ((), (), s32[]{:S(2)}) async-start(), calls=%async_computation.39 | async-start | bytes 17563648 | tf_op jit(solution)/shard_map/psum | solution.py:805
  (208 other events, 1165.3 us)
Sparse Core Ops, SparseCore 0:
  9.6 49.2 all-gather.13
  61.0 217.4 all-gather.11
  347.5 50.7 all-gather.17
  400.6 52.5 all-gather.15
  454.6 80.7 all-gather.19
  536.8 44.1 all-gather.29
  582.5 80.6 all-gather.23
  664.8 156.3 all-gather.31
  822.8 284.8 all-gather.25
  1111.2 36.2 all-reduce.22
  1149.1 562.5 all-gather.27
  1713.2 1108.7 all-gather.21
  3848.7 19.2 all-reduce.16
  5064.5 47.9 all-reduce.20
  6034.2 53.8 reduce-scatter.12
  6090.9 52.5 reduce-scatter.14
  6169.3 62.2 all-reduce.18
  6233.8 23.0 reduce-scatter.24
  6259.1 41.8 reduce-scatter.32
  6303.8 75.9 reduce-scatter.30
  6382.6 20.5 reduce-scatter.20
  6405.4 20.0 reduce-scatter.22
  6427.9 142.8 reduce-scatter.34
  6573.5 23.7 reduce-scatter.18
  6600.2 34.9 reduce-scatter.16
  6637.4 279.2 reduce-scatter.28
  6919.4 19.8 reduce-scatter.26
  6944.4 176.9 all-reduce.24
where the time goes:
time: 7180 us; the launch traced here: 7150 us
  waiting for transfers between devices  2920 us (41%)
  other arithmetic  1590 us (22%)
  matrix products  1400 us (19%)
  local copies, waits for them, and re-layouts  1000 us (14%)
  blocking collectives  123 us (2%)
  loops' own time  98.8 us (1%)
    all_gather x1, waiting for transfers between devices, run_experts(): lax.all_gather(w_gate_up, 'fsdp', axis=0, tiled=True)  1110 us
    all_gather x1, waiting for transfers between devices, run_experts(): lax.all_gather(w_down, 'fsdp', axis=0, tiled=True)  417 us
    scatter-add x16, other arithmetic, forward_step(): routed_sum.at[expert_row].add(expert_output_rows * expert_gate[:, None])  356 us
    scatter-add x16, other arithmetic, backward_step(): d_rows = d_rows.at[expert_row].add(d_rows_e)  350 us
    scatter-add x16, other arithmetic, adapter_step(): d_rows.at[slot_row[expert_idx]]  349 us
    reduce_scatter x1, waiting for transfers between devices, per_device(): lax.psum_scatter(grad_gu_a.astype(jnp.bfloat16), 'fsdp', scatter_dimensio...  282 us
    all_gather x1, waiting for transfers between devices, per_device(): lax.all_gather(gu_a, 'fsdp', axis=0, tiled=True)  280 us
    all_gather x1, waiting for transfers between devices, per_device(): lax.all_gather(w_qkv, 'fsdp', axis=0, tiled=True)  213 us
  transfers between devices with their start and end apart: 28, of which 20 were waited for; matrix products, arithmetic and copies ran while one was open for 12% of the time, Pallas kernels for 0%

commit v1 on v0

v1 whole, which is shorter than its diff:
```python
import jax
import jax.numpy as jnp
from jax import lax
from jax.experimental import pallas as pl
from jax.experimental.pallas import tpu as pltpu
from jax.sharding import PartitionSpec as P

HEAD_DIM = 128
TOPK = 8
EXPERTS = 16
RANK = 16
PROMPT = 2048
CONT_LEN = 256
CONTS = 8
SETS = 8

epsilon = 1e-05
ADAPTER_SCALE = 0.5
ROPE_BASE = 10000.0
masked_score = -1e30
TILE = CONT_LEN
SCORE_SCALE = HEAD_DIM ** (-0.5)
f32 = jnp.float32
bf16 = jnp.bfloat16


def dot_nn(a, b):
    return lax.dot_general(a, b, (((1,), (0,)), ((), ())), preferred_element_type=f32)


def dot_nt(a, b):
    return lax.dot_general(a, b, (((1,), (1,)), ((), ())), preferred_element_type=f32)


def dot_tn(a, b):
    return lax.dot_general(a, b, (((0,), (0,)), ((), ())), preferred_element_type=f32)


def rms_back(value, gain, grad, scale_col, full_width):
    inner = jnp.sum(gain * value * grad, axis=-1, keepdims=True)
    return (
        scale_col * gain * grad - value * (scale_col * scale_col * scale_col) * inner / full_width
    )


def angles(positions):
    freqs = ROPE_BASE ** (-(2.0 * jnp.arange(HEAD_DIM // 2, dtype=f32)) / HEAD_DIM)
    turned = positions.astype(f32)[:, None] * freqs[None, :]
    return (jnp.cos(turned)[:, None, :], jnp.sin(turned)[:, None, :])


def rotate(value, cosine, sine_part):
    half_dim = value.shape[-1] // 2
    first_half = value[..., :half_dim]
    second_half = value[..., half_dim:]
    return jnp.concatenate(
        [
            first_half * cosine - second_half * sine_part,
            second_half * cosine + first_half * sine_part,
        ],
        axis=-1,
    )


def attention_scores(k_ref, q, slab_ref, tile, prompt_rows, is_prompt):
    scores = dot_nt(k_ref[...], q) * SCORE_SCALE
    if not is_prompt:
        return scores
    key_at = lax.broadcasted_iota(jnp.int32, scores.shape, 0)
    query_at = (
        slab_ref[0] * prompt_rows + tile * TILE + lax.broadcasted_iota(jnp.int32, scores.shape, 1)
    )
    return jnp.where(key_at <= query_at, scores, masked_score)


def own_scores(ko_ref, q):
    scores = dot_nt(ko_ref[...], q) * SCORE_SCALE
    key_at = lax.broadcasted_iota(jnp.int32, scores.shape, 0)
    query_at = lax.broadcasted_iota(jnp.int32, scores.shape, 1)
    return jnp.where(key_at <= query_at, scores, masked_score)


def attention_forward(slab, q, k, v, ko, vo, prompt_rows):
    rows, width = q.shape
    heads, tiles, prompt_tiles = width // HEAD_DIM, rows // TILE, prompt_rows // TILE
    keys = k.shape[0]

    def body(slab_ref, q_ref, k_ref, v_ref, ko_ref, vo_ref, att_ref, lse_ref, vt_ref):
        tile = pl.program_id(1)

        @pl.when(tile == 0)
        def _():
            vt_ref[...] = v_ref[...].T

        query = q_ref[...]

        def finish(total, peak, out_t):
            att_ref[...] = (out_t / total).T.astype(bf16)
            lse_ref[0] = peak + jnp.log(total)

        @pl.when(tile < prompt_tiles)
        def _():
            scores = attention_scores(k_ref, query, slab_ref, tile, prompt_rows, True)
            peak = jnp.max(scores, axis=0, keepdims=True)
            probs = jnp.exp(scores - peak)
            total = jnp.sum(probs, axis=0, keepdims=True)
            finish(total, peak, dot_nn(vt_ref[...], probs.astype(bf16)))

        @pl.when(tile >= prompt_tiles)
        def _():
            scores = attention_scores(k_ref, query, slab_ref, tile, prompt_rows, False)
            own = own_scores(ko_ref, query)
            peak = jnp.maximum(
                jnp.max(scores, axis=0, keepdims=True), jnp.max(own, axis=0, keepdims=True)
            )
            probs = jnp.exp(scores - peak)
            own_probs = jnp.exp(own - peak)
            total = jnp.sum(probs, axis=0, keepdims=True) + jnp.sum(
                own_probs, axis=0, keepdims=True
            )
            out_t = dot_nn(vt_ref[...], probs.astype(bf16)) + dot_nn(
                vo_ref[...].T, own_probs.astype(bf16)
            )
            finish(total, peak, out_t)

    tile_spec = pl.BlockSpec((TILE, HEAD_DIM), lambda h, t, s: (t, h))
    key_spec = pl.BlockSpec((keys, HEAD_DIM), lambda h, t, s: (0, h))
    own_spec = pl.BlockSpec(
        (TILE, HEAD_DIM), lambda h, t, s: (jnp.maximum(t - prompt_tiles, 0), h)
    )
    return pl.pallas_call(
        body,
        grid_spec=pltpu.PrefetchScalarGridSpec(
            num_scalar_prefetch=1,
            grid=(heads, tiles),
            in_specs=[tile_spec, key_spec, key_spec, own_spec, own_spec],
            out_specs=[tile_spec, pl.BlockSpec((1, 1, TILE), lambda h, t, s: (h, 0, t))],
            scratch_shapes=[pltpu.VMEM((HEAD_DIM, keys), bf16)],
        ),
        out_shape=[
            jax.ShapeDtypeStruct((rows, width), bf16),
            jax.ShapeDtypeStruct((heads, 1, rows), f32),
        ],
        compiler_params=pltpu.CompilerParams(
            dimension_semantics=("arbitrary", "arbitrary"), vmem_limit_bytes=56 << 20
        ),
        name="attention_forward",
    )(slab, q, k, v, ko, vo)


def attention_backward(slab, q, k, v, ko, vo, att, d_att, lse, prompt_rows):
    rows, width = q.shape
    heads, tiles, prompt_tiles = width // HEAD_DIM, rows // TILE, prompt_rows // TILE
    keys = k.shape[0]

    def body(
        slab_ref, q_ref, k_ref, v_ref, ko_ref, vo_ref, att_ref, da_ref, lse_ref,
        dq_ref, dk_ref, dv_ref, dko_ref, dvo_ref, kt_ref, dka_ref, dva_ref,
    ):
        tile = pl.program_id(1)

        @pl.when(tile == 0)
        def _():
            kt_ref[...] = k_ref[...].T
            dka_ref[...] = jnp.zeros_like(dka_ref)
            dva_ref[...] = jnp.zeros_like(dva_ref)

        query = q_ref[...]
        d_out = da_ref[...]
        delta = jnp.sum(
            (d_out.astype(f32) * att_ref[...].astype(f32)).T, axis=0, keepdims=True
        )
        log_total = lse_ref[0]

        def prompt_keys(is_prompt):
            scores = attention_scores(k_ref, query, slab_ref, tile, prompt_rows, is_prompt)
            probs = jnp.exp(scores - log_total)
            d_probs = dot_nt(v_ref[...], d_out)
            d_scores = (probs * (d_probs - delta)).astype(bf16)
            dka_ref[...] += dot_nn(d_scores, query)
            dva_ref[...] += dot_nn(probs.astype(bf16), d_out)
            return dot_nn(kt_ref[...], d_scores)

        @pl.when(tile < prompt_tiles)
        def _():
            dq_ref[...] = prompt_keys(True).T * SCORE_SCALE

        @pl.when(tile >= prompt_tiles)
        def _():
            dq_t = prompt_keys(False)
            probs = jnp.exp(own_scores(ko_ref, query) - log_total)
            d_probs = dot_nt(vo_ref[...], d_out)
            d_scores = (probs * (d_probs - delta)).astype(bf16)
            dko_ref[...] = dot_nn(d_scores, query) * SCORE_SCALE
            dvo_ref[...] = dot_nn(probs.astype(bf16), d_out)
            dq_ref[...] = (dq_t + dot_nn(ko_ref[...].T, d_scores)).T * SCORE_SCALE

        @pl.when(tile == tiles - 1)
        def _():
            dk_ref[...] = (dka_ref[...] * SCORE_SCALE).astype(bf16)
            dv_ref[...] = dva_ref[...].astype(bf16)

    tile_spec = pl.BlockSpec((TILE, HEAD_DIM), lambda h, t, s: (t, h))
    key_spec = pl.BlockSpec((keys, HEAD_DIM), lambda h, t, s: (0, h))
    own_spec = pl.BlockSpec(
        (TILE, HEAD_DIM), lambda h, t, s: (jnp.maximum(t - prompt_tiles, 0), h)
    )
    return pl.pallas_call(
        body,
        grid_spec=pltpu.PrefetchScalarGridSpec(
            num_scalar_prefetch=1,
            grid=(heads, tiles),
            in_specs=[
                tile_spec, key_spec, key_spec, own_spec, own_spec, tile_spec, tile_spec,
                pl.BlockSpec((1, 1, TILE), lambda h, t, s: (h, 0, t)),
            ],
            out_specs=[tile_spec, key_spec, key_spec, own_spec, own_spec],
            scratch_shapes=[
                pltpu.VMEM((HEAD_DIM, keys), bf16),
                pltpu.VMEM((keys, HEAD_DIM), f32),
                pltpu.VMEM((keys, HEAD_DIM), f32),
            ],
        ),
        out_shape=[
            jax.ShapeDtypeStruct((rows, width), f32),
            jax.ShapeDtypeStruct((keys, width), bf16),
            jax.ShapeDtypeStruct((keys, width), bf16),
            jax.ShapeDtypeStruct((rows - prompt_rows, width), f32),
            jax.ShapeDtypeStruct((rows - prompt_rows, width), f32),
        ],
        compiler_params=pltpu.CompilerParams(
            dimension_semantics=("arbitrary", "arbitrary"), vmem_limit_bytes=56 << 20
        ),
        name="attention_backward",
    )(slab, q, k, v, ko, vo, att, d_att, lse)


def expert_pass(order, order_sets, h, cot, gates, w_gu, w_dn, gu_a, gu_b, dn_a, dn_b):
    shards, parts, rows, part_width = h.shape
    width = parts * part_width
    locals_n = gates.shape[2]
    ff = w_dn.shape[1]
    tiles = rows // TILE
    gu_rank = 2 * RANK

    def body(
        order_ref, set_ref, h_ref, cot_ref, gate_ref, wgu_ref, wdn_ref, gua_ref, gub_ref,
        dna_ref, dnb_ref, y_ref, dh_ref, dgate_ref, ggua_ref, ggub_ref, gdna_ref, gdnb_ref,
        y_acc, dh_acc,
    ):
        step = pl.program_id(0)
        fresh = jnp.logical_or(
            step == 0, set_ref[step] != set_ref[jnp.maximum(step - 1, 0)]
        )

        @pl.when(fresh)
        def _():
            ggua_ref[...] = jnp.zeros_like(ggua_ref)
            ggub_ref[...] = jnp.zeros_like(ggub_ref)
            gdna_ref[...] = jnp.zeros_like(gdna_ref)
            gdnb_ref[...] = jnp.zeros_like(gdnb_ref)

        x = jnp.concatenate([h_ref[0, i] for i in range(parts)], axis=1)
        ct = jnp.concatenate([cot_ref[0, i] for i in range(parts)], axis=1)
        gu_a_rows = gua_ref[0]
        gu_b_rows = gub_ref[0]
        dn_a_rows = dna_ref[0]
        dn_b_rows = dnb_ref[0]
        mid_gu = (ADAPTER_SCALE * dot_nt(x, gu_a_rows)).astype(bf16)
        d_mid_dn = (ADAPTER_SCALE * dot_nt(ct, dn_b_rows)).astype(bf16)
        gu_lane = lax.broadcasted_iota(jnp.int32, mid_gu.shape, 1)
        dn_lane = lax.broadcasted_iota(jnp.int32, d_mid_dn.shape, 1)
        n_all = jnp.zeros(mid_gu.shape, f32)
        mid_dn_all = jnp.zeros(d_mid_dn.shape, f32)
        gate_block = gate_ref[0, 0]
        d_gate_cols = []
        for e in range(locals_n):
            gate_lanes = (gu_lane // RANK) == 2 * e
            up_lanes = (gu_lane // RANK) == 2 * e + 1
            dn_lanes = (dn_lane // RANK) == e
            zero_gu = jnp.zeros_like(mid_gu)
            mid_gate = jnp.where(gate_lanes, mid_gu, zero_gu)
            mid_up = jnp.where(up_lanes, mid_gu, zero_gu)
            d_mid_e = jnp.where(dn_lanes, d_mid_dn, jnp.zeros_like(d_mid_dn))
            g = dot_nn(x, wgu_ref[e, 0]) + dot_nn(mid_gate, gu_b_rows)
            u = dot_nn(x, wgu_ref[e, 1]) + dot_nn(mid_up, gu_b_rows)
            c = dot_nt(ct, wdn_ref[e]) + dot_nn(d_mid_e, dn_a_rows)
            gate = gate_block[:, e : e + 1]
            sig = jax.nn.sigmoid(g)
            silu = g * sig
            hidden = silu * u
            hidden_b = hidden.astype(bf16)
            d_gate_cols.append(jnp.sum(hidden_b.astype(f32) * c, axis=1, keepdims=True))
            d_hidden = gate * c
            d_g = (d_hidden * u * sig * (1.0 + g * (1.0 - sig))).astype(bf16)
            d_u = (d_hidden * silu).astype(bf16)
            gated = (gate * hidden).astype(bf16)
            y_e = dot_nn(gated, wdn_ref[e])
            dh_e = dot_nt(d_g, wgu_ref[e, 0]) + dot_nt(d_u, wgu_ref[e, 1])
            if e == 0:
                y_acc[...] = y_e
                dh_acc[...] = dh_e
            else:
                y_acc[...] += y_e
                dh_acc[...] += dh_e
            mid_dn_all = jnp.where(dn_lanes, dot_nt(gated, dn_a_rows), mid_dn_all)
            n_all = jnp.where(gate_lanes, dot_nt(d_g, gu_b_rows), n_all)
            n_all = jnp.where(up_lanes, dot_nt(d_u, gu_b_rows), n_all)
            ggub_ref[0] += dot_tn(mid_gate, d_g) + dot_tn(mid_up, d_u)
            gdna_ref[0] += dot_tn((gate * d_mid_e.astype(f32)).astype(bf16), hidden_b)
        n_b = (ADAPTER_SCALE * n_all).astype(bf16)
        mid_dn_b = (ADAPTER_SCALE * mid_dn_all).astype(bf16)
        y = (y_acc[...] + dot_nn(mid_dn_b, dn_b_rows)).astype(bf16)
        dh = (dh_acc[...] + dot_nn(n_b, gu_a_rows)).astype(bf16)
        for i in range(parts):
            y_ref[0, i] = y[:, i * part_width : (i + 1) * part_width]
            dh_ref[0, i] = dh[:, i * part_width : (i + 1) * part_width]
        dgate_ref[0, 0] = jnp.concatenate(d_gate_cols, axis=1)
        ggua_ref[0] += dot_tn(n_b, x)
        gdnb_ref[0] += dot_tn(mid_dn_b, ct)

    row_spec = pl.BlockSpec(
        (1, parts, TILE, part_width), lambda i, o, s: (o[i] // tiles, 0, o[i] % tiles, 0)
    )
    gate_spec = pl.BlockSpec(
        (1, 1, TILE, locals_n), lambda i, o, s: (o[i] // tiles, o[i] % tiles, 0, 0)
    )
    gates = gates.reshape(shards, tiles, TILE, locals_n)

    def whole(a):
        zeros = (0,) * a.ndim
        return pl.BlockSpec(a.shape, lambda i, o, s: zeros, pipeline_mode=pl.Buffered(1))

    def of_set(a):
        return pl.BlockSpec((1,) + a.shape[1:], lambda i, o, s: (s[i], 0, 0))

    grads = [jax.ShapeDtypeStruct(a.shape, f32) for a in (gu_a, gu_b, dn_a, dn_b)]
    return pl.pallas_call(
        body,
        grid_spec=pltpu.PrefetchScalarGridSpec(
            num_scalar_prefetch=2,
            grid=(shards * tiles,),
            in_specs=[row_spec, row_spec, gate_spec, whole(w_gu), whole(w_dn)]
            + [of_set(a) for a in (gu_a, gu_b, dn_a, dn_b)],
            out_specs=[row_spec, row_spec, gate_spec] + [of_set(a) for a in grads],
            scratch_shapes=[pltpu.VMEM((TILE, width), f32), pltpu.VMEM((TILE, width), f32)],
        ),
        out_shape=[
            jax.ShapeDtypeStruct(h.shape, bf16),
            jax.ShapeDtypeStruct(h.shape, bf16),
            jax.ShapeDtypeStruct(gates.shape, f32),
        ]
        + grads,
        compiler_params=pltpu.CompilerParams(
            dimension_semantics=("arbitrary",), vmem_limit_bytes=60 << 20
        ),
        name="expert_pass",
    )(order, order_sets, h, cot, gates, w_gu, w_dn, gu_a, gu_b, dn_a, dn_b)


def per_device(
    tokens, cotangent, routes, adapter_ids, norm_in, norm_mid, q_gain, k_gain, w_qkv, w_out,
    w_router, w_gate_up, w_down, qkv_a, qkv_b, out_a, out_b, router_a, router_b, gu_a, gu_b,
    down_a, down_b,
):
    row_count, full_width = tokens.shape
    local_width = q_gain.shape[0]
    local_heads = local_width // HEAD_DIM
    locals_n, ff_local = w_gate_up.shape[0], w_gate_up.shape[3]
    shard_count, slab_count, part_count = (
        lax.axis_size("fsdp"), lax.axis_size("ctx"), lax.axis_size("tp"),
    )
    shard_index, slab_index, part_index = (
        lax.axis_index("fsdp"), lax.axis_index("ctx"), lax.axis_index("tp"),
    )
    part_width = full_width // part_count
    prompt_rows = PROMPT // slab_count
    cont_count = CONTS // slab_count
    tiles, prompt_tiles = row_count // TILE, prompt_rows // TILE
    row_index = jnp.arange(row_count, dtype=jnp.int32)
    tail_offset = jnp.maximum(row_index - prompt_rows, 0)
    leading = row_index < prompt_rows
    positions = jnp.where(
        leading, slab_index * prompt_rows + row_index, PROMPT + tail_offset % CONT_LEN
    )
    cosine, sine_part = angles(positions)
    slab = slab_index.reshape(1).astype(jnp.int32)

    def my_part(x):
        return lax.dynamic_slice_in_dim(x, part_index * part_width, part_width, axis=1)

    def tile_rows(x):
        return x.reshape(tiles, TILE, x.shape[1])

    cont_sets = lax.dynamic_slice_in_dim(adapter_ids[0], 1 + slab_index * cont_count, cont_count)
    tile_sets = jnp.concatenate([jnp.broadcast_to(adapter_ids[0, :1], (prompt_tiles,)), cont_sets])
    all_sets = lax.all_gather(tile_sets, "fsdp", axis=0, tiled=True)
    count_all = all_sets.shape[0]
    tile_at = jnp.arange(count_all, dtype=jnp.int32)
    ahead = (all_sets[None, :] < all_sets[:, None]) | (
        (all_sets[None, :] == all_sets[:, None]) & (tile_at[None, :] < tile_at[:, None])
    )
    rank_of = jnp.sum(ahead.astype(jnp.int32), axis=1)
    at_rank = (rank_of[None, :] == tile_at[:, None]).astype(jnp.int32)
    order = jnp.sum(at_rank * tile_at[None, :], axis=1)
    order_sets = jnp.sum(at_rank * all_sets[None, :], axis=1)
    set_at = jnp.arange(SETS, dtype=jnp.int32)
    present = jnp.any(set_at[:, None] == all_sets[None, :], axis=1)
    tile_hot = (set_at[:, None] == tile_sets[None, :]).astype(f32)

    sets_local = qkv_a.shape[0]

    def as_rows(x):
        return x.reshape(x.shape[0], -1, local_width)

    def router_rows(x):
        flat = x.reshape(x.shape[0], 1, -1)
        return jnp.pad(flat, ((0, 0), (0, 0), (0, local_width - flat.shape[2])))

    pieces = [
        as_rows(qkv_a.transpose(0, 2, 3, 1)),
        as_rows(qkv_b.transpose(0, 2, 1, 3)),
        as_rows(out_a.transpose(0, 2, 1)),
        as_rows(out_b),
        as_rows(router_a.transpose(0, 2, 1)),
        router_rows(router_b),
    ]
    sizes = [p.shape[1] for p in pieces]
    packed = lax.all_gather(jnp.concatenate(pieces, axis=1), "fsdp", axis=0, tiled=True)
    picked = jnp.take(packed, tile_sets, axis=0)
    cuts = [sum(sizes[:i]) for i in range(len(sizes) + 1)]

    def piece(i, shape):
        return picked[:, cuts[i] : cuts[i + 1]].reshape((tiles,) + shape)

    t_qkv_a = piece(0, (3, RANK, full_width))
    t_qkv_b = piece(1, (3, RANK, local_width))
    t_out_a = piece(2, (RANK, local_width))
    t_out_b = piece(3, (RANK, full_width))
    t_router_a = piece(4, (RANK, full_width))
    t_router_b = picked[:, cuts[5], : RANK * EXPERTS].reshape(tiles, RANK, EXPERTS)

    token_vals = tokens.astype(f32)
    cot_vals = cotangent.astype(f32)
    gain_in = norm_in.astype(f32)
    gain_mid = norm_mid.astype(f32)
    gain_q = q_gain.astype(f32)
    gain_k = k_gain.astype(f32)
    first_scale = lax.rsqrt(jnp.mean(token_vals * token_vals, axis=1, keepdims=True) + epsilon)
    h_first = (token_vals * first_scale * gain_in).astype(bf16)
    whole_qkv = lax.all_gather(w_qkv, "fsdp", axis=0, tiled=True)
    proj = jnp.einsum("nd,djo->jno", h_first, whole_qkv, preferred_element_type=f32)
    mid_qkv = (
        ADAPTER_SCALE
        * jnp.einsum("tnd,tjrd->tnjr", tile_rows(h_first), t_qkv_a, preferred_element_type=f32)
    ).astype(bf16)
    proj = proj + jnp.einsum(
        "tnjr,tjro->jtno", mid_qkv, t_qkv_b, preferred_element_type=f32
    ).reshape(3, row_count, local_width)
    q_raw, k_raw = proj[0], proj[1]
    squares = lax.psum(
        jnp.stack([jnp.sum(q_raw * q_raw, axis=1), jnp.sum(k_raw * k_raw, axis=1)]), "tp"
    )
    q_scale = lax.rsqrt(squares[0] / full_width + epsilon)[:, None]
    k_scale = lax.rsqrt(squares[1] / full_width + epsilon)[:, None]

    def heads_of(x):
        return x.reshape(x.shape[0], local_heads, HEAD_DIM)

    query_rows = (
        rotate(heads_of(q_raw * q_scale * gain_q), cosine, sine_part)
        .reshape(row_count, local_width)
        .astype(bf16)
    )
    key_rows = (
        rotate(heads_of(k_raw * k_scale * gain_k), cosine, sine_part)
        .reshape(row_count, local_width)
        .astype(bf16)
    )
    value_rows = proj[2].astype(bf16)
    prompt_keys = lax.all_gather(key_rows[:prompt_rows], "ctx", axis=0, tiled=True)
    prompt_values = lax.all_gather(value_rows[:prompt_rows], "ctx", axis=0, tiled=True)
    key_own, value_own = key_rows[prompt_rows:], value_rows[prompt_rows:]
    attention_rows, log_total = attention_forward(
        slab, query_rows, prompt_keys, prompt_values, key_own, value_own, prompt_rows
    )
    whole_out = lax.all_gather(w_out, "fsdp", axis=1, tiled=True)
    mid_out = (
        ADAPTER_SCALE
        * jnp.einsum("tnd,trd->tnr", tile_rows(attention_rows), t_out_a, preferred_element_type=f32)
    ).astype(bf16)
    branch = lax.psum(
        jnp.dot(attention_rows, whole_out, preferred_element_type=f32)
        + jnp.einsum("tnr,trd->tnd", mid_out, t_out_b, preferred_element_type=f32).reshape(
            row_count, full_width
        ),
        "tp",
    )
    x_mid = token_vals + branch
    mid_scale = lax.rsqrt(jnp.mean(x_mid * x_mid, axis=1, keepdims=True) + epsilon)
    h_second = (x_mid * mid_scale * gain_mid).astype(bf16)
    h_tiles = tile_rows(h_second)
    mid_router = (
        ADAPTER_SCALE
        * jnp.einsum("tnd,trd->tnr", h_tiles, t_router_a, preferred_element_type=f32)
    ).astype(bf16)
    router_logits = jnp.dot(h_second, w_router, preferred_element_type=f32) + jnp.einsum(
        "tnr,tre->tne", mid_router, t_router_b, preferred_element_type=f32
    ).reshape(row_count, EXPERTS)
    expert_probs = jax.nn.softmax(router_logits, axis=1)
    chosen = jnp.any(
        routes[:, :, None] == jnp.arange(EXPERTS, dtype=jnp.int32)[None, None, :], axis=1
    )
    gates = jnp.where(chosen, expert_probs, 0.0)

    def gather_rows(x):
        return lax.all_gather(my_part(x), ("fsdp", "tp"), axis=0, tiled=False).reshape(
            shard_count, part_count, row_count, part_width
        )

    def experts_of_sets(x):
        return lax.all_to_all(x, "fsdp", split_axis=1, concat_axis=0, tiled=True)

    e_gu_a = experts_of_sets(gu_a.transpose(0, 1, 3, 4, 2)).reshape(SETS, -1, full_width)
    e_gu_b = experts_of_sets(gu_b.transpose(0, 1, 3, 2, 4)).reshape(SETS, -1, ff_local)
    e_dn_a = experts_of_sets(down_a.transpose(0, 1, 3, 2)).reshape(SETS, -1, ff_local)
    e_dn_b = experts_of_sets(down_b).reshape(SETS, -1, full_width)
    cot_all = gather_rows(cotangent)
    h_all = gather_rows(h_second)
    gates_all = lax.all_gather(gates, "fsdp", axis=0, tiled=False)
    my_gates = lax.dynamic_slice_in_dim(gates_all, shard_index * locals_n, locals_n, axis=2)
    y_part, dh_part, d_gates_part, g_gu_a, g_gu_b, g_dn_a, g_dn_b = expert_pass(
        order, order_sets, h_all, cot_all, my_gates, w_gate_up.transpose(0, 2, 1, 3), w_down,
        e_gu_a, e_gu_b, e_dn_a, e_dn_b,
    )

    def return_rows(x):
        own = lax.psum_scatter(
            x.reshape(shard_count * part_count, row_count, part_width),
            ("fsdp", "tp"), scatter_dimension=0, tiled=False,
        )
        return own

    d_gates_wide = lax.dynamic_update_slice_in_dim(
        jnp.zeros((shard_count, row_count, EXPERTS), f32),
        d_gates_part.reshape(shard_count, row_count, locals_n),
        shard_index * locals_n, axis=2,
    )
    d_gates = lax.psum(
        lax.psum_scatter(d_gates_wide, "fsdp", scatter_dimension=0, tiled=False), "tp"
    )
    d_second_routed = lax.all_gather(return_rows(dh_part), "tp", axis=1, tiled=True).astype(f32)
    mixed = lax.all_gather(
        (my_part(x_mid) + return_rows(y_part).astype(f32)).astype(bf16), "tp", axis=1, tiled=True
    )

    d_probs = jnp.where(chosen, d_gates, 0.0)
    d_logits = (
        expert_probs * (d_probs - jnp.sum(expert_probs * d_probs, axis=1, keepdims=True))
    ).astype(bf16)
    dl_tiles = tile_rows(d_logits)
    d_mid_router = (
        ADAPTER_SCALE
        * jnp.einsum("tne,tre->tnr", dl_tiles, t_router_b, preferred_element_type=f32)
    ).astype(bf16)
    g_router_b = jnp.einsum("tnr,tne->tre", mid_router, dl_tiles, preferred_element_type=f32)
    g_router_a = jnp.einsum("tnr,tnd->trd", d_mid_router, h_tiles, preferred_element_type=f32)
    d_second = (
        d_second_routed
        + jnp.einsum("ne,de->nd", d_logits, w_router, preferred_element_type=f32)
        + jnp.einsum("tnr,trd->tnd", d_mid_router, t_router_a, preferred_element_type=f32).reshape(
            row_count, full_width
        )
    )
    d_x_mid = cot_vals + rms_back(x_mid, gain_mid, d_second, mid_scale, full_width)
    d_branch = d_x_mid.astype(bf16)
    db_tiles = tile_rows(d_branch)
    d_mid_out = (
        ADAPTER_SCALE
        * jnp.einsum("tnd,trd->tnr", db_tiles, t_out_b, preferred_element_type=f32)
    ).astype(bf16)
    d_att = jnp.einsum("nc,oc->no", d_branch, whole_out, preferred_element_type=f32) + jnp.einsum(
        "tnr,tro->tno", d_mid_out, t_out_a, preferred_element_type=f32
    ).reshape(row_count, local_width)
    g_out_b = jnp.einsum("tnr,tnd->trd", mid_out, db_tiles, preferred_element_type=f32)
    g_out_a = jnp.einsum(
        "tnr,tno->tro", d_mid_out, tile_rows(attention_rows), preferred_element_type=f32
    )
    d_att_rows = d_att.astype(bf16)
    d_query, d_key_all, d_value_all, d_key_own, d_value_own = attention_backward(
        slab, query_rows, prompt_keys, prompt_values, key_own, value_own, attention_rows,
        d_att_rows, log_total, prompt_rows,
    )
    d_key_prompt = lax.psum_scatter(d_key_all, "ctx", scatter_dimension=0, tiled=True)
    d_value_prompt = lax.psum_scatter(d_value_all, "ctx", scatter_dimension=0, tiled=True)
    d_key = jnp.concatenate([d_key_prompt.astype(f32), d_key_own], axis=0)
    d_value = jnp.concatenate([d_value_prompt.astype(f32), d_value_own], axis=0)
    d_q_norm = rotate(heads_of(d_query), cosine, -sine_part).reshape(row_count, local_width)
    d_k_norm = rotate(heads_of(d_key), cosine, -sine_part).reshape(row_count, local_width)
    dots = lax.psum(
        jnp.stack(
            [jnp.sum(gain_q * q_raw * d_q_norm, axis=1), jnp.sum(gain_k * k_raw * d_k_norm, axis=1)]
        ),
        "tp",
    )
    d_q_raw = (
        q_scale * gain_q * d_q_norm
        - q_raw * (q_scale * q_scale * q_scale) * dots[0][:, None] / full_width
    )
    d_k_raw = (
        k_scale * gain_k * d_k_norm
        - k_raw * (k_scale * k_scale * k_scale) * dots[1][:, None] / full_width
    )
    d_proj = jnp.stack([d_q_raw, d_k_raw, d_value], axis=0).astype(bf16)
    dp_tiles = d_proj.reshape(3, tiles, TILE, local_width)
    d_mid_qkv = (
        ADAPTER_SCALE
        * jnp.einsum("jtno,tjro->tnjr", dp_tiles, t_qkv_b, preferred_element_type=f32)
    ).astype(bf16)
    d_first = lax.psum(
        jnp.einsum("jno,djo->nd", d_proj, whole_qkv, preferred_element_type=f32)
        + jnp.einsum("tnjr,tjrd->tnd", d_mid_qkv, t_qkv_a, preferred_element_type=f32).reshape(
            row_count, full_width
        ),
        "tp",
    )
    grad_input = d_x_mid + rms_back(token_vals, gain_in, d_first, first_scale, full_width)
    g_qkv_b = jnp.einsum("tnjr,jtno->tjro", mid_qkv, dp_tiles, preferred_element_type=f32)
    g_qkv_a = jnp.einsum(
        "tnjr,tnd->tjrd", d_mid_qkv, tile_rows(h_first), preferred_element_type=f32
    )

    def to_sets(pieces_):
        rows_ = jnp.concatenate(pieces_, axis=1)
        return jnp.sum(tile_hot[:, :, None, None] * rows_[None], axis=1).astype(bf16)

    def reduced(x, axes):
        mine = lax.psum_scatter(x, "fsdp", scatter_dimension=0, tiled=True)
        return lax.psum(mine, axes).astype(f32)

    both = reduced(to_sets([as_rows(g_qkv_a), as_rows(g_out_b)]), ("ctx", "tp"))
    one = reduced(
        to_sets(
            [as_rows(g_qkv_b), as_rows(g_out_a), as_rows(g_router_a), router_rows(g_router_b)]
        ),
        "ctx",
    )
    n0, n1, n2, n3, n4 = sizes[0], sizes[1], sizes[2], sizes[3], sizes[4]
    grad_qkv_a = both[:, :n0].reshape(sets_local, 3, RANK, full_width).transpose(0, 3, 1, 2)
    grad_out_b = both[:, n0 : n0 + n3].reshape(out_b.shape)
    grad_qkv_b = one[:, :n1].reshape(sets_local, 3, RANK, local_width).transpose(0, 2, 1, 3)
    grad_out_a = one[:, n1 : n1 + n2].reshape(sets_local, RANK, local_width).transpose(0, 2, 1)
    grad_router_a = (
        one[:, n1 + n2 : n1 + n2 + n4].reshape(sets_local, RANK, full_width).transpose(0, 2, 1)
    )
    grad_router_b = one[:, n1 + n2 + n4, : RANK * EXPERTS].reshape(router_b.shape)

    def expert_grad(g, axes):
        g = jnp.where(present[:, None, None], g, 0.0).astype(bf16)
        g = lax.psum(g, axes)
        g = g.reshape(SETS, locals_n, -1, g.shape[2])
        return lax.all_to_all(g, "fsdp", split_axis=0, concat_axis=1, tiled=True).astype(f32)

    grad_gu_a = (
        expert_grad(g_gu_a, ("ctx", "tp"))
        .reshape(sets_local, EXPERTS, 2, RANK, full_width)
        .transpose(0, 1, 4, 2, 3)
    )
    grad_gu_b = (
        expert_grad(g_gu_b, "ctx")
        .reshape(sets_local, EXPERTS, 2, RANK, ff_local)
        .transpose(0, 1, 3, 2, 4)
    )
    grad_down_a = expert_grad(g_dn_a, "ctx").transpose(0, 1, 3, 2)
    grad_down_b = expert_grad(g_dn_b, ("ctx", "tp"))
    return (
        mixed, grad_input, grad_qkv_a, grad_qkv_b, grad_out_a, grad_out_b, grad_router_a,
        grad_router_b, grad_gu_a, grad_gu_b, grad_down_a, grad_down_b,
    )


def solution(mesh):
    return jax.shard_map(
        per_device,
        mesh=mesh,
        in_specs=(
            P(("fsdp", "ctx"), None),
            P(("fsdp", "ctx"), None),
            P(("fsdp", "ctx"), None),
            P("fsdp", None),
            P(),
            P(),
            P("tp"),
            P("tp"),
            P("fsdp", None, "tp"),
            P("tp", "fsdp"),
            P(),
            P("fsdp", None, None, "tp"),
            P("fsdp", "tp", None),
            P("fsdp", None, None, None),
            P("fsdp", None, None, "tp"),
            P("fsdp", "tp", None),
            P("fsdp", None, None),
            P("fsdp", None, None),
            P("fsdp", None, None),
            P("fsdp", None, None, None, None),
            P("fsdp", None, None, None, "tp"),
            P("fsdp", None, "tp", None),
            P("fsdp", None, None, None),
        ),
        out_specs=(
            P(("fsdp", "ctx"), None),
            P(("fsdp", "ctx"), None),
            P("fsdp", None, None, None),
            P("fsdp", None, None, "tp"),
            P("fsdp", "tp", None),
            P("fsdp", None, None),
            P("fsdp", None, None),
            P("fsdp", None, None),
            P("fsdp", None, None, None, None),
            P("fsdp", None, None, None, "tp"),
            P("fsdp", None, "tp", None),
            P("fsdp", None, None, None),
        ),
        check_vma=False,
    )
```

time: 7180 us -> 2420 us (0.34)
  waiting for transfers between devices: 2920 us -> 1290 us
  other arithmetic: 1590 us -> 128 us
  matrix products: 1400 us -> 119 us
  local copies, waits for them, and re-layouts: 1000 us -> 145 us
  Pallas kernels: 0 us -> 414 us
  blocking collectives: 123 us -> 259 us
  loops' own time: 98.8 us -> 0 us
    all_gather x9 -> x7, waiting for transfers between devices: 2090 us -> 299 us  [the longest x1 203 us: per_device(): whole_qkv = lax.all_gather(w_qkv, 'fsdp', axis=0, tiled=True)]
    dot_general x319 -> x24, matrix products: 1390 us -> 119 us  [the longest x1 22.9 us: per_device(): jnp.einsum('nd,djo->jno', h_first, whole_qkv, preferred_element_type=f32)]
    scatter-add x59 -> x0, other arithmetic: 1170 us -> none  [the longest x16 356 us: forward_step(): routed_sum.at[expert_row].add(expert_output_rows * expert_gate[:, None])]
    gather x47 -> x1, local copies, waits for them, and re-layouts: 518 us -> 2.74 us  [per_device(): picked = jnp.take(packed, tile_sets, axis=0)]
    pallas_call x0 -> x3, Pallas kernels: none -> 414 us  [the longest x1 292 us: expert_pass(): pl.pallas_call(body, grid_spec=pltpu.PrefetchScalarGridSpec(num_scalar_pr...]
    all_to_all x0 -> x7, waiting for transfers between devices: none -> 225 us  [the longest x4 156 us: experts_of_sets(): return lax.all_to_all(x, 'fsdp', split_axis=1, concat_axis=0, tiled=True)]
    reduce_scatter x12 -> x6, waiting for transfers between devices: 640 us -> 440 us  [the longest x2 338 us: return_rows(): lax.psum_scatter(x.reshape(shard_count * part_count, row_count, part_widt...]
    unnamed x0 -> x1, blocking collectives: none -> 183 us
  transfers between devices with their start and end apart: 28 -> 28, of which waited for: 20 -> 23; matrix products, arithmetic and copies ran while one was open for 12% -> 11% of each run, Pallas kernels for 0% -> 2%
where the time goes in v1:
time: 2420 us; the launch traced here: 2400 us
  waiting for transfers between devices  1290 us (53%)
  Pallas kernels  414 us (17%)
  blocking collectives  259 us (11%)
  local copies, waits for them, and re-layouts  145 us (6%)
  other arithmetic  128 us (5%)
  matrix products  119 us (5%)
  starting transfers between devices  31.7 us (1%)
    reduce_scatter x2, waiting for transfers between devices, return_rows(): lax.psum_scatter(x.reshape(shard_count * part_count, row_count, part_widt...  338 us
    pallas_call x1, Pallas kernels, expert_pass(): pl.pallas_call(body, grid_spec=pltpu.PrefetchScalarGridSpec(num_scalar_pr...  292 us
    all_gather x1, waiting for transfers between devices, per_device(): whole_qkv = lax.all_gather(w_qkv, 'fsdp', axis=0, tiled=True)  203 us
    unnamed x1, blocking collectives  183 us
    all_to_all x4, waiting for transfers between devices, experts_of_sets(): return lax.all_to_all(x, 'fsdp', split_axis=1, concat_axis=0, tiled=True)  156 us
    psum x2, waiting for transfers between devices, reduced(): return lax.psum(mine, axes).astype(f32)  132 us
    unnamed x139, local copies, waits for them, and re-layouts  75.5 us
    pallas_call x1, Pallas kernels, attention_backward(): pl.pallas_call(body, grid_spec=pltpu.PrefetchScalarGridSpec(num_scalar_pr...  70.6 us
  transfers between devices with their start and end apart: 28, of which 23 were waited for; matrix products, arithmetic and copies ran while one was open for 11% of the time, Pallas kernels for 2%

profile of v1, /device:TPU:0, one launch (start us, length us, event | category | flops | bytes accessed | tf_op | source)
XLA Modules:
  0.0 2404.2 jit_solution(7719759728568655567)
XLA Ops:
  34.1 62.6 %all-gather.17.cloned.1.call-done = bf16[8,225,1024]{2,1,0:T(8,128)(2,1)} async-done(((bf16[2,225,1024]{2,1,0:T(8,128)(2,1)}), bf16[8,225,1024]{2,1,0:T(8,128)(2,1)}) %all-gather.17.cloned.1.call-update) | async-done | bytes 3686416 | tf_op jit(solution)/shard_map/all_gather | solution.py:429
  101.4 3.9 fusion.27
  105.3 7.4 fusion.35
  112.7 202.9 %all-gather.15.cloned.1.call-done = bf16[2048,3,1024]{0,2,1:T(8,128)(2,1)} async-done(((bf16[512,3,1024]{0,2,1:T(8,128)(2,1)}), bf16[2048,3,1024]{0,2,1:T(8,128)(2,1)}) %all-gather.15.cloned.1.call-update) | async-done | bytes 12582928 | tf_op jit(solution)/shard_map/all_gather | solution.py:451
  315.7 22.9 fusion.73
  338.6 7.2 multiply_reduce_fusion.7
  357.0 3.9 add_convert_fusion
  377.2 38.0 %all-gather.19.cloned.1.call-done.k_ref = bf16[2048,1024]{1,0:T(8,128)(2,1)} async-done(((bf16[512,1024]{1,0:T(8,128)(2,1)}), bf16[2048,1024]{1,0:T(8,128)(2,1)}) %all-gather.19.cloned.1.call-update) | async-done | bytes 4194320 | tf_op jit(solution)/shard_map/all_gather | solution.py:481
  415.2 54.9 %all-gather.25.cloned.1.call-done = bf16[1,2048,1024]{2,1,0:T(8,128)(2,1)} async-done(((bf16[1,512,1024]{2,1,0:T(8,128)(2,1)}), bf16[1,2048,1024]{2,1,0:T(8,128)(2,1)}) %all-gather.25.cloned.1.call-update) | async-done | bytes 4194320 | tf_op jit(solution)/shard_map/all_gather | solution.py:482
  470.1 51.2 %attention_forward.1 = (bf16[1024,1024]{1,0:T(8,128)(2,1)}, f32[8,1,1024]{2,1,0:T(1,128)}) custom-call(s32[1]{0:T(128)} %bitcast.slab_ref, bf16[1024,1024]{1,0:T(8,128)(2,1)} %bitcast.249, bf16[2048,1024]{1,0:T(8,128)(2,1)} %all-gather.19.cloned.1.call-done.k_ref, bf16[2048,1024]{1,0:T(8,128)(2,1)} %bitcast.255, bf16[512,1024]{1,0:T(8,128)(2,1)} %bitcast.262, ...), custom_call_target="tpu_custom_call" | custom-call | tf_op jit(solution)/shard_map/attention_forward/pallas_call | solution.py:131
  523.5 4.7 fusion.75
  528.2 24.1 %all-gather.21.cloned.1.call-done = bf16[1024,2048]{1,0:T(8,128)(2,1)} async-done(((bf16[1024,512]{1,0:T(8,128)(2,1)}), bf16[1024,2048]{1,0:T(8,128)(2,1)}) %all-gather.21.cloned.1.call-update) | async-done | bytes 4194320 | tf_op jit(solution)/shard_map/all_gather | solution.py:487
  552.3 10.2 bitcast_add_fusion.2
  565.8 33.1 %all-reduce.14.cloned.1.call-done = f32[1024,2048]{1,0:T(8,128)} async-done(((f32[1024,2048]{1,0:T(8,128)}), f32[1024,2048]{1,0:T(8,128)}) %all-reduce.14.cloned.1.call-update) | async-done | bytes 8388624 | tf_op jit(solution)/shard_map/psum | solution.py:492
  598.8 5.9 multiply_reduce_fusion.3
  612.6 4.9 all-to-all-start.2
  619.4 30.7 %all-to-all-done.2 = bf16[2,16,16,512]{3,2,0,1:T(8,128)(2,1)S(1)} async-done(((bf16[2,16,16,512]{3,2,0,1:T(8,128)(2,1)}), bf16[2,16,16,512]{3,2,0,1:T(8,128)(2,1)S(1)}, u32[]{:S(2)}, u32[]{:S(2)}) %all-to-all-start.2) | async-done | bytes 524320 | tf_op jit(solution)/shard_map/all_to_all | solution.py:522
  657.5 52.9 %all-to-all-done.1 = bf16[2,16,2,16,512]{4,2,3,0,1:T(2,128)(2,1)S(1)} async-done(((bf16[2,16,2,16,512]{4,2,3,0,1:T(2,128)(2,1)}), bf16[2,16,2,16,512]{4,2,3,0,1:T(2,128)(2,1)S(1)}, u32[]{:S(2)}, u32[]{:S(2)}) %all-to-all-start.1) | async-done | bytes 1048608 | tf_op jit(solution)/shard_map/all_to_all | solution.py:522
  715.2 4.8 copy.314
  720.0 71.9 %all-to-all-done.3 = bf16[2,16,16,2048]{3,2,0,1:T(8,128)(2,1)S(1)} async-done(((bf16[2,16,16,2048]{3,2,0,1:T(8,128)(2,1)}), bf16[2,16,16,2048]{3,2,0,1:T(8,128)(2,1)S(1)}, u32[]{:S(2)}, u32[]{:S(2)}) %all-to-all-start.3) | async-done | bytes 2097184 | tf_op jit(solution)/shard_map/all_to_all | solution.py:522
  791.9 4.9 all-to-all-start
  796.9 16.5 copy.313
  814.8 182.9 %all-reduce.3 = s32[16]{0:T(128)S(1)} all-reduce(s32[16]{0:T(128)S(1)} %pad_dynamic-update-slice_fusion), channel_id=1, replica_groups=mesh['fsdp'=4,'ctx'=4,'tp'=2] {'fsdp'}, use_global_device_ids=true, to_apply=%add.3 | all-reduce | flops 16 | bytes 128
  1006.5 4.9 copy.251
  1014.1 18.4 all-gather.3
  1036.1 292.0 %expert_pass.1 = (bf16[4,2,1024,1024]{3,2,1,0:T(8,128)(2,1)}, bf16[4,2,1024,1024]{3,2,1,0:T(8,128)(2,1)}, f32[4,4,256,4]{3,2,1,0:T(8,128)}, f32[8,128,2048]{2,1,...) custom-call(s32[16]{0:T(128)} %get-tuple-element.129.order_ref, ...), custom_call_target="tpu_custom_call" | custom-call | tf_op jit(solution)/shard_map/expert_pass/pallas_call | solution.py:338
  1331.9 20.1 reduce-scatter.12.cloned.1.call-done
  1352.0 168.7 %reduce-scatter.10.cloned.1.call-done = bf16[1,1024,1024]{2,1,0:T(8,128)(2,1)} async-done(((bf16[8,1024,1024]{2,1,0:T(8,128)(2,1)}), bf16[1,1024,1024]{2,1,0:T(8,128)(2,1)}) %reduce-scatter.10.cloned.1.call-update) | async-done | bytes 2097168 | tf_op jit(solution)/shard_map/reduce_scatter | solution.py:538
  1520.8 18.4 all-reduce.16.cloned.1.call-done
  1541.1 4.6 fusion.76
  1545.7 9.8 all-gather.31.cloned.1.call-done
  1555.6 8.3 multiply_reduce_fusion.2
  1563.9 7.2 fusion.67
  1575.4 6.1 fusion.21.da_ref
  1581.5 70.6 %attention_backward.1 = (f32[1024,1024]{1,0:T(8,128)}, bf16[2048,1024]{1,0:T(8,128)(2,1)}, bf16[2048,1024]{1,0:T(8,128)(2,1)}, f32[512,1024]{1,0:T(8,128)}, f32[512,1024]{1,0:T(8,128)}) custom-call(s32[1]{0:T(128)} %bitcast.slab_ref, bf16[1024,1024]{1,0:T(8,128)(2,1)} %bitcast.250, bf16[2048,1024]{1,0:T(8,128)(2,1)} %all-gather.19.cloned.1.call-done.k_ref, ...), custom_call_target="tpu_custom_call" | custom-call | tf_op jit(solution)/shard_map/attention_backward/pallas_call | solution.py:208
  1657.1 5.4 copy.291
  1662.9 43.2 %reduce-scatter.14.cloned.1.call-done = bf16[512,1024]{1,0:T(8,128)(2,1)} async-done(((bf16[2048,1024]{1,0:T(8,128)(2,1)}), bf16[512,1024]{1,0:T(8,128)(2,1)}) %reduce-scatter.14.cloned.1.call-update) | async-done | bytes 1048592 | tf_op jit(solution)/shard_map/reduce_scatter | solution.py:594
  1710.3 5.5 multiply_subtract_fusion.1
  1719.0 5.0 concatenate.43
  1724.0 6.9 pad_maximum_fusion.1
  1730.9 4.9 reshape.620
  1735.8 6.9 multiply_reduce_fusion.5
  1745.3 9.8 subtract_convert_fusion.1
  1755.1 6.4 reduce-scatter.16.cloned.1.call-done
  1771.2 5.1 fusion.28
  1790.7 47.4 %all-reduce.20.cloned.1.call-done = bf16[8,97,1024]{2,0,1:T(8,128)(2,1)} async-done(((bf16[8,97,1024]{2,0,1:T(8,128)(2,1)}), bf16[8,97,1024]{2,0,1:T(8,128)(2,1)}) %all-reduce.20.cloned.1.call-update) | async-done | bytes 1589264
  1840.7 4.0 select_convert_fusion.1
  1844.7 7.0 select_convert_fusion
  1851.7 31.8 %reduce-scatter.18.cloned.1.call-done = bf16[2,128,1024]{2,1,0:T(8,128)(2,1)} async-done(((bf16[8,128,1024]{2,1,0:T(8,128)(2,1)}), bf16[2,128,1024]{2,1,0:T(8,128)(2,1)}) %reduce-scatter.18.cloned.1.call-update) | async-done | bytes 524304 | tf_op jit(solution)/shard_map/reduce_scatter | solution.py:638
  1883.7 169.5 %reduce-scatter.8.cloned.1.call-done = bf16[1,1024,1024]{2,1,0:T(8,128)(2,1)} async-done(((bf16[8,1024,1024]{2,1,0:T(8,128)(2,1)}), bf16[1,1024,1024]{2,1,0:T(8,128)(2,1)}) %reduce-scatter.8.cloned.1.call-update) | async-done | bytes 2097168 | tf_op jit(solution)/shard_map/reduce_scatter | solution.py:538
  2053.2 5.0 fusion.20
  2058.2 65.8 %all-reduce.24.cloned.1.call-done = (bf16[2,97,1024]{2,0,1:T(2,128)(2,1)}, bf16[8,4,32,512]{3,2,1,0:T(8,128)(2,1)}, bf16[8,4,16,512]{3,2,1,0:T(8,128)(2,1)}) async-done(((bf16[2,97,1024]{2,0,1:T(2,128)(2,1)}, bf16[8,4,32,512]{3,2,1,0:T(8,128)(2,1)}, bf16[8,4,16,512]{3,2,1,0:T(8,128)(2,1)}), (bf16[2,97,1024]{2,0,1:T(2,128)(2,1)}, bf16[8,4,32,512]{3,2,1,0:T(8,128)(2,1)}, ...) | async-done | bytes 1970192 | tf_op jit(solution)/shard_map/psum | solution.py:639
  2124.0 4.6 all-to-all-start.6
  2131.4 5.7 fusion.77
  2137.1 5.8 all-to-all-done.6
  2147.5 20.9 bitcast_add_fusion.1
  2168.4 4.1 all-to-all-done.5
  2172.5 65.7 %all-reduce.22.cloned.1.call-done = (bf16[2,128,1024]{2,1,0:T(8,128)(2,1)}, bf16[8,4,32,2048]{3,2,1,0:T(8,128)(2,1)}, bf16[8,4,16,2048]{3,2,1,0:T(8,128)(2,1)}) async-done(((bf16[2,128,1024]{2,1,0:T(8,128)(2,1)}, bf16[8,4,32,2048]{3,2,1,0:T(8,128)(2,1)}, bf16[8,4,16,2048]{3,2,1,0:T(8,128)(2,1)}), (bf16[2,128,1024]{2,1,0:T(8,128)(2,1)}, bf16[8,4,32,2048]{3,2,1,0:T(8,128)(2,1)}, ...) | async-done | bytes 6815760 | tf_op jit(solution)/shard_map/psum | solution.py:639
  2238.2 52.5 %all_to_all.96 = bf16[8,4,16,2048]{3,2,1,0:T(8,128)(2,1)S(1)} all-to-all(bf16[8,4,16,2048]{3,2,1,0:T(8,128)(2,1)} %get-tuple-element.132), channel_id=1, replica_groups=mesh['fsdp'=4,'ctx'=4,'tp'=2] {'fsdp'}, dimensions={0} | all-to-all | bytes 4194304 | tf_op jit(solution)/shard_map/all_to_all | solution.py:662
  2290.7 5.0 all-to-all-start.4
  2310.5 5.9 fusion.8
  2318.7 6.9 fusion.6
  2328.2 59.7 %all-to-all-done.4 = bf16[8,4,32,2048]{3,2,1,0:T(8,128)(2,1)} async-done(((bf16[8,4,32,2048]{3,2,1,0:T(8,128)(2,1)}), bf16[8,4,32,2048]{3,2,1,0:T(8,128)(2,1)}, u32[]{:S(2)}, u32[]{:S(2)}) %all-to-all-start.4) | async-done | bytes 4194336 | tf_op jit(solution)/shard_map/all_to_all | solution.py:662
  2387.8 6.8 copy.269
  (295 shorter events, 181.5 us)
Async XLA Ops:
  8.0 1004.8 %copy-start = (bf16[2048,16]{0,1:T(8,128)(2,1)S(1)}, bf16[2048,16]{0,1:T(8,128)(2,1)}, u32[]{:S(2)}) copy-start(bf16[2048,16]{0,1:T(8,128)(2,1)} %param.33) | copy-start | bytes 196612
  8.0 11.7 copy-start.21
  8.0 88.7 %all-gather.17.cloned.1.call-start = ((), (), s32[]{:S(2)}) async-start(), calls=%async_computation.15 | async-start | bytes 4751360 | tf_op jit(solution)/shard_map/all_gather | solution.py:429
  19.6 3.5 copy-start.52
  19.7 4.1 copy-start.53
  19.7 296.0 %all-gather.15.cloned.1.call-start = ((), (), s32[]{:S(2)}) async-start(), calls=%async_computation.14 | async-start | bytes 15728640 | tf_op jit(solution)/shard_map/all_gather | solution.py:451
  22.7 392.6 %all-gather.19.cloned.1.call-start = ((), (), s32[]{:S(2)}) async-start(), calls=%async_computation.16 | async-start | bytes 5242880 | tf_op jit(solution)/shard_map/all_gather | solution.py:481
  22.8 11.4 copy-start.42
  22.8 8.3 copy-start.5
  28.0 6.1 copy-start.44
  101.1 11.6 copy-start.32
  101.4 11.3 copy-start.17
  105.3 7.4 copy-start.39
  353.2 3.8 copy-start.27
  364.3 105.8 %all-gather.25.cloned.1.call-start = ((), (), s32[]{:S(2)}) async-start(), calls=%async_computation.28 | async-start | bytes 5242880 | tf_op jit(solution)/shard_map/all_gather | solution.py:482
  367.4 184.9 %all-gather.21.cloned.1.call-start = ((), (), s32[]{:S(2)}) async-start(), calls=%async_computation.17 | async-start | bytes 5242880 | tf_op jit(solution)/shard_map/all_gather | solution.py:487
  368.0 230.8 %all-reduce.14.cloned.1.call-start = ((), (), s32[]{:S(2)}) async-start(), calls=%async_computation.18 | async-start | bytes 16777216 | tf_op jit(solution)/shard_map/psum | solution.py:492
  523.5 4.7 copy-start.37
  523.5 28.8 %copy-start.11 = (bf16[1024,1024]{1,0:T(8,128)(2,1)S(1)}, bf16[1024,1024]{1,0:T(8,128)(2,1)}, u32[]{:S(2)}) copy-start(bf16[1024,1024]{1,0:T(8,128)(2,1)} %get-tuple-element.26.att_ref) | copy-start | bytes 6291460
  562.5 473.5 %all-gather.29.cloned.1.call-start = ((), (), s32[]{:S(2)}) async-start(), calls=%async_computation.30 | async-start | bytes 18874368 | tf_op jit(solution)/shard_map/all_gather | solution.py:517
  565.7 470.4 %all-gather.27.cloned.1.call-start = ((), (), s32[]{:S(2)}) async-start(), calls=%async_computation.29 | async-start | bytes 18874368 | tf_op jit(solution)/shard_map/all_gather | solution.py:517
  610.1 7.4 copy-start.33
  612.6 37.5 %all-to-all-start.2 = ((bf16[2,16,16,512]{3,2,0,1:T(8,128)(2,1)}), bf16[2,16,16,512]{3,2,0,1:T(8,128)(2,1)S(1)}, u32[]{:S(2)}, u32[]{:S(2)}) async-start(bf16[2,16,16,512]{3,2,0,1:T(8,128)(2,1)} %bitcast.237), calls=%async_computation.2 | async-start | bytes 1048576 | tf_op jit(solution)/shard_map/all_to_all | solution.py:522
  650.9 59.6 %all-to-all-start.1 = ((bf16[2,16,2,16,512]{4,2,3,0,1:T(2,128)(2,1)}), bf16[2,16,2,16,512]{4,2,3,0,1:T(2,128)(2,1)S(1)}, u32[]{:S(2)}, u32[]{:S(2)}) async-start(bf16[2,16,2,16,512]{4,2,3,0,1:T(2,128)(2,1)} %bitcast.236), calls=%async_computation.1 | async-start | bytes 2097152 | tf_op jit(solution)/shard_map/all_to_all | solution.py:522
  711.4 80.5 %all-to-all-start.3 = ((bf16[2,16,16,2048]{3,2,0,1:T(8,128)(2,1)}), bf16[2,16,16,2048]{3,2,0,1:T(8,128)(2,1)S(1)}, u32[]{:S(2)}, u32[]{:S(2)}) async-start(bf16[2,16,16,2048]{3,2,0,1:T(8,128)(2,1)} %copy.256), calls=%async_computation.3 | async-start | bytes 4194304 | tf_op jit(solution)/shard_map/all_to_all | solution.py:522
  791.9 214.5 %all-to-all-start = ((bf16[2,16,2,16,2048]{4,3,2,0,1:T(8,128)(2,1)}), bf16[2,16,2,16,2048]{4,3,2,0,1:T(8,128)(2,1)}, u32[]{:S(2)}, u32[]{:S(2)}) async-start(bf16[2,16,2,16,2048]{4,3,2,0,1:T(8,128)(2,1)} %bitcast.260), calls=%async_computation | async-start | bytes 8388608 | tf_op jit(solution)/shard_map/all_to_all | solution.py:522
  796.8 555.1 %reduce-scatter.12.cloned.1.call-start = ((), (), s32[]{:S(2)}) async-start(), calls=%async_computation.22 | async-start | bytes 327680 | tf_op jit(solution)/shard_map/reduce_scatter | solution.py:550
  796.9 16.5 copy-start.54
  796.9 201.7 %copy-start.48 = (s32[1024,8]{0,1:T(8,128)S(1)}, s32[1024,8]{0,1:T(8,128)}, u32[]{:S(2)}) copy-start(s32[1024,8]{0,1:T(8,128)} %param.25) | copy-start | bytes 98308
  1006.5 4.9 copy-start.4
  1331.1 189.7 %reduce-scatter.10.cloned.1.call-start = ((), (), s32[]{:S(2)}) async-start(), calls=%async_computation.21 | async-start | bytes 18874368 | tf_op jit(solution)/shard_map/reduce_scatter | solution.py:538
  1331.8 207.4 %all-reduce.16.cloned.1.call-start = ((), (), s32[]{:S(2)}) async-start(), calls=%async_computation.23 | async-start | bytes 131072 | tf_op jit(solution)/shard_map/psum | solution.py:549
  1351.9 203.6 %all-gather.31.cloned.1.call-start = ((), (), s32[]{:S(2)}) async-start(), calls=%async_computation.31 | async-start | bytes 6291456 | tf_op jit(solution)/shard_map/all_gather | solution.py:552
  1520.8 185.3 %reduce-scatter.14.cloned.1.call-start = ((), (), s32[]{:S(2)}) async-start(), calls=%async_computation.24 | async-start | bytes 5242880 | tf_op jit(solution)/shard_map/reduce_scatter | solution.py:594
  1555.5 8.3 copy-start.14
  1571.1 4.3 copy-start.7
  1571.1 4.3 copy-start.56
  1652.1 109.4 %reduce-scatter.16.cloned.1.call-start = ((), (), s32[]{:S(2)}) async-start(), calls=%async_computation.25 | async-start | bytes 5242880 | tf_op jit(solution)/shard_map/reduce_scatter | solution.py:595
  1652.7 185.3 %all-reduce.20.cloned.1.call-start = ((), (), s32[]{:S(2)}) async-start(), calls=%async_computation.32 | async-start | bytes 3178496
  1657.1 5.4 copy-start.12
  1662.5 45.1 %copy-start.31 = (f32[512,1024]{1,0:T(8,128)S(1)}, f32[512,1024]{1,0:T(8,128)}, u32[]{:S(2)}) copy-start(f32[512,1024]{1,0:T(8,128)} %get-tuple-element.33) | copy-start | bytes 6291460
  1730.9 4.9 copy-start.46
  1730.9 4.9 copy-start.47
  1745.3 16.2 copy-start.15
  1755.1 8.1 copy-start.40
  1768.0 115.6 %reduce-scatter.18.cloned.1.call-start = ((), (), s32[]{:S(2)}) async-start(), calls=%async_computation.27 | async-start | bytes 2621440 | tf_op jit(solution)/shard_map/reduce_scatter | solution.py:638
  1771.2 5.2 copy-start.8
  1776.4 4.6 copy-start.41
  1785.4 267.8 %reduce-scatter.8.cloned.1.call-start = ((), (), s32[]{:S(2)}) async-start(), calls=%async_computation.19 | async-start | bytes 18874368 | tf_op jit(solution)/shard_map/reduce_scatter | solution.py:538
  1786.0 338.0 %all-reduce.24.cloned.1.call-start = ((), (), s32[]{:S(2)}) async-start(), calls=%async_computation.34 | async-start | bytes 3940352 | tf_op jit(solution)/shard_map/psum | solution.py:639
  1840.7 397.5 %all-reduce.22.cloned.1.call-start = ((), (), s32[]{:S(2)}) async-start(), calls=%async_computation.33 | async-start | bytes 13631488 | tf_op jit(solution)/shard_map/psum | solution.py:639
  1883.6 412.1 %all-gather.23.cloned.1.call-start = ((), (), s32[]{:S(2)}) async-start(), calls=%async_computation.20 | async-start | bytes 6291456 | tf_op jit(solution)/shard_map/all_gather | solution.py:553
  2058.1 73.3 %copy-start.18 = (bf16[4,3,16,2048]{3,2,1,0:T(8,128)(2,1)S(1)}, bf16[4,3,16,2048]{3,2,1,0:T(8,128)(2,1)}, u32[]{:S(2)}) copy-start(bf16[4,3,16,2048]{3,2,1,0:T(8,128)(2,1)} %copy-done.17) | copy-start | bytes 2359300
  2124.0 18.9 all-to-all-start.6
  2131.4 16.1 copy-start.23
  2143.7 28.8 %all-to-all-start.5 = ((bf16[8,4,32,512]{3,2,1,0:T(8,128)(2,1)}), bf16[8,4,32,512]{3,2,1,0:T(8,128)(2,1)S(1)}, u32[]{:S(2)}, u32[]{:S(2)}) async-start(bf16[8,4,32,512]{3,2,1,0:T(8,128)(2,1)} %get-tuple-element.134), calls=%async_computation.11 | async-start | bytes 2097152 | tf_op jit(solution)/shard_map/all_to_all | solution.py:662
  2147.2 163.3 %all-reduce.18.cloned.1.call-start = ((), (), s32[]{:S(2)}) async-start(), calls=%async_computation.26 | async-start | bytes 16777216 | tf_op jit(solution)/shard_map/psum | solution.py:620
  2290.7 97.1 %all-to-all-start.4 = ((bf16[8,4,32,2048]{3,2,1,0:T(8,128)(2,1)}), bf16[8,4,32,2048]{3,2,1,0:T(8,128)(2,1)}, u32[]{:S(2)}, u32[]{:S(2)}) async-start(bf16[8,4,32,2048]{3,2,1,0:T(8,128)(2,1)} %get-tuple-element.131), calls=%async_computation.10 | async-start | bytes 8388608 | tf_op jit(solution)/shard_map/all_to_all | solution.py:662
  2305.5 5.0 copy-start.43
  2310.5 5.9 copy-start.45
  2310.5 5.9 copy-start.49
  2310.5 5.9 copy-start.6
  2310.5 8.2 copy-start.10
  2387.8 6.8 copy-start.19
  (21 other events, 44.3 us)
Sparse Core Ops, SparseCore 0:
  19.7 76.9 all-gather.16
  98.9 216.7 all-gather.14
  364.4 50.7 all-gather.18
  417.5 52.5 all-gather.24
  471.5 80.7 all-gather.20
  562.6 36.1 all-reduce.13
  1331.2 20.7 reduce-scatter.11
  1354.3 166.4 reduce-scatter.9
  1523.0 16.1 all-reduce.15
  1540.6 14.8 all-gather.30
  1652.3 53.7 reduce-scatter.13
  1708.9 52.5 reduce-scatter.15
  1768.1 69.8 all-reduce.19
  1840.8 42.7 reduce-scatter.17
  1885.8 167.3 reduce-scatter.7
  2057.7 66.2 all-reduce.23
  2128.0 110.1 all-reduce.21
  2240.1 13.7 all-gather.22
  2257.0 38.8 all-reduce.17
Sparse Core Ops, SparseCore 1:
  565.8 224.8 all-gather.28
  792.1 238.5 all-gather.26

commit v2 on v1

--- a/solution.py
+++ b/solution.py
@@ -66,7 +66,14 @@
     scores = dot_nt(k_ref[...], q) * SCORE_SCALE
     if not is_prompt:
         return scores
-    key_at = lax.broadcasted_iota(jnp.int32, scores.shape, 0)
+    block_at = lax.broadcasted_iota(jnp.int32, (prompt_rows, scores.shape[1]), 0)
+    key_at = jnp.concatenate(
+        [
+            block_at + jnp.bitwise_xor(slab_ref[0], b) * prompt_rows
+            for b in range(scores.shape[0] // prompt_rows)
+        ],
+        axis=0,
+    )
     query_at = (
         slab_ref[0] * prompt_rows + tile * TILE + lax.broadcasted_iota(jnp.int32, scores.shape, 1)
     )
@@ -235,18 +242,19 @@
     )(slab, q, k, v, ko, vo, att, d_att, lse)
 
 
-def expert_pass(order, order_sets, h, cot, gates, w_gu, w_dn, gu_a, gu_b, dn_a, dn_b):
-    shards, parts, rows, part_width = h.shape
-    width = parts * part_width
-    locals_n = gates.shape[2]
-    ff = w_dn.shape[1]
+def expert_pass(order, order_sets, part, h, cot, gates, w_gu, w_dn, adapters, sums):
+    halved = isinstance(h, tuple)
+    rows = h[0].shape[0] if halved else h.shape[0]
+    width = w_gu.shape[2]
+    part_width = width // 2
+    locals_n = gates.shape[1]
     tiles = rows // TILE
-    gu_rank = 2 * RANK
 
     def body(
-        order_ref, set_ref, h_ref, cot_ref, gate_ref, wgu_ref, wdn_ref, gua_ref, gub_ref,
-        dna_ref, dnb_ref, y_ref, dh_ref, dgate_ref, ggua_ref, ggub_ref, gdna_ref, gdnb_ref,
-        y_acc, dh_acc,
+        order_ref, set_ref, part_ref, h0_ref, h1_ref, cot0_ref, cot1_ref, gate_ref, wgu_ref,
+        wdn_ref, wide_ref, slim_ref, swide_ref, sslim_ref,
+        yk_ref, ys_ref, dhk_ref, dhs_ref, dgate_ref, gwide_ref, gslim_ref,
+        y_acc, dh_acc, x_ref, ct_ref, n_ref, mid_ref,
     ):
         step = pl.program_id(0)
         fresh = jnp.logical_or(
@@ -255,107 +263,129 @@
 
         @pl.when(fresh)
         def _():
-            ggua_ref[...] = jnp.zeros_like(ggua_ref)
-            ggub_ref[...] = jnp.zeros_like(ggub_ref)
-            gdna_ref[...] = jnp.zeros_like(gdna_ref)
-            gdnb_ref[...] = jnp.zeros_like(gdnb_ref)
-
-        x = jnp.concatenate([h_ref[0, i] for i in range(parts)], axis=1)
-        ct = jnp.concatenate([cot_ref[0, i] for i in range(parts)], axis=1)
-        gu_a_rows = gua_ref[0]
-        gu_b_rows = gub_ref[0]
-        dn_a_rows = dna_ref[0]
-        dn_b_rows = dnb_ref[0]
-        mid_gu = (ADAPTER_SCALE * dot_nt(x, gu_a_rows)).astype(bf16)
-        d_mid_dn = (ADAPTER_SCALE * dot_nt(ct, dn_b_rows)).astype(bf16)
-        gu_lane = lax.broadcasted_iota(jnp.int32, mid_gu.shape, 1)
-        dn_lane = lax.broadcasted_iota(jnp.int32, d_mid_dn.shape, 1)
-        n_all = jnp.zeros(mid_gu.shape, f32)
-        mid_dn_all = jnp.zeros(d_mid_dn.shape, f32)
-        gate_block = gate_ref[0, 0]
-        d_gate_cols = []
-        for e in range(locals_n):
-            gate_lanes = (gu_lane // RANK) == 2 * e
-            up_lanes = (gu_lane // RANK) == 2 * e + 1
-            dn_lanes = (dn_lane // RANK) == e
-            zero_gu = jnp.zeros_like(mid_gu)
-            mid_gate = jnp.where(gate_lanes, mid_gu, zero_gu)
-            mid_up = jnp.where(up_lanes, mid_gu, zero_gu)
-            d_mid_e = jnp.where(dn_lanes, d_mid_dn, jnp.zeros_like(d_mid_dn))
-            g = dot_nn(x, wgu_ref[e, 0]) + dot_nn(mid_gate, gu_b_rows)
-            u = dot_nn(x, wgu_ref[e, 1]) + dot_nn(mid_up, gu_b_rows)
-            c = dot_nt(ct, wdn_ref[e]) + dot_nn(d_mid_e, dn_a_rows)
-            gate = gate_block[:, e : e + 1]
+            gwide_ref[...] = swide_ref[...]
+            gslim_ref[...] = sslim_ref[...]
+
+        low_first = part_ref[0] == 0
+
+        def join(first, second):
+            x_ref[:, :part_width] = h0_ref[...] if first else h1_ref[...]
+            x_ref[:, part_width:] = h1_ref[...] if first else h0_ref[...]
+            ct_ref[:, :part_width] = cot0_ref[...] if first else cot1_ref[...]
+            ct_ref[:, part_width:] = cot1_ref[...] if first else cot0_ref[...]
+
+        if halved:
+            pl.when(low_first)(lambda: join(True, False))
+            pl.when(jnp.logical_not(low_first))(lambda: join(False, True))
+        else:
+            join(True, False)
+        x = x_ref[...]
+        ct = ct_ref[...]
+        wide = wide_ref[0]
+        slim = slim_ref[0]
+        lane = lax.broadcasted_iota(jnp.int32, (TILE, wide.shape[0]), 1)
+        mid_gu = (ADAPTER_SCALE * dot_nt(x, wide)).astype(bf16)
+        d_mid_dn = (ADAPTER_SCALE * dot_nt(ct, wide)).astype(bf16)
+        zero_mid = jnp.zeros_like(mid_gu)
+        n_ref[...] = jnp.zeros_like(n_ref)
+        mid_ref[...] = jnp.zeros_like(mid_ref)
+        y_acc[...] = jnp.zeros_like(y_acc)
+        dh_acc[...] = jnp.zeros_like(dh_acc)
+        gate_block = gate_ref[...]
+        gate_lane = lax.broadcasted_iota(jnp.int32, gate_block.shape, 1)
+
+        def expert(e, d_gates):
+            gate_lanes = (lane // RANK) == 3 * e
+            up_lanes = (lane // RANK) == 3 * e + 1
+            dn_lanes = (lane // RANK) == 3 * e + 2
+            mid_gate = jnp.where(gate_lanes, mid_gu, zero_mid)
+            mid_up = jnp.where(up_lanes, mid_gu, zero_mid)
+            d_mid_e = jnp.where(dn_lanes, d_mid_dn, zero_mid)
+            g = dot_nn(x_ref[...], wgu_ref[e, 0]) + dot_nn(mid_gate, slim)
+            u = dot_nn(x_ref[...], wgu_ref[e, 1]) + dot_nn(mid_up, slim)
+            c = dot_nt(ct_ref[...], wdn_ref[e]) + dot_nn(d_mid_e, slim)
+            gate = jnp.sum(jnp.where(gate_lane == e, gate_block, 0.0), axis=1, keepdims=True)
             sig = jax.nn.sigmoid(g)
             silu = g * sig
             hidden = silu * u
             hidden_b = hidden.astype(bf16)
-            d_gate_cols.append(jnp.sum(hidden_b.astype(f32) * c, axis=1, keepdims=True))
+            d_gate = jnp.sum(hidden_b.astype(f32) * c, axis=1, keepdims=True)
             d_hidden = gate * c
             d_g = (d_hidden * u * sig * (1.0 + g * (1.0 - sig))).astype(bf16)
             d_u = (d_hidden * silu).astype(bf16)
             gated = (gate * hidden).astype(bf16)
-            y_e = dot_nn(gated, wdn_ref[e])
-            dh_e = dot_nt(d_g, wgu_ref[e, 0]) + dot_nt(d_u, wgu_ref[e, 1])
-            if e == 0:
-                y_acc[...] = y_e
-                dh_acc[...] = dh_e
-            else:
-                y_acc[...] += y_e
-                dh_acc[...] += dh_e
-            mid_dn_all = jnp.where(dn_lanes, dot_nt(gated, dn_a_rows), mid_dn_all)
-            n_all = jnp.where(gate_lanes, dot_nt(d_g, gu_b_rows), n_all)
-            n_all = jnp.where(up_lanes, dot_nt(d_u, gu_b_rows), n_all)
-            ggub_ref[0] += dot_tn(mid_gate, d_g) + dot_tn(mid_up, d_u)
-            gdna_ref[0] += dot_tn((gate * d_mid_e.astype(f32)).astype(bf16), hidden_b)
-        n_b = (ADAPTER_SCALE * n_all).astype(bf16)
-        mid_dn_b = (ADAPTER_SCALE * mid_dn_all).astype(bf16)
-        y = (y_acc[...] + dot_nn(mid_dn_b, dn_b_rows)).astype(bf16)
-        dh = (dh_acc[...] + dot_nn(n_b, gu_a_rows)).astype(bf16)
-        for i in range(parts):
-            y_ref[0, i] = y[:, i * part_width : (i + 1) * part_width]
-            dh_ref[0, i] = dh[:, i * part_width : (i + 1) * part_width]
-        dgate_ref[0, 0] = jnp.concatenate(d_gate_cols, axis=1)
-        ggua_ref[0] += dot_tn(n_b, x)
-        gdnb_ref[0] += dot_tn(mid_dn_b, ct)
-
-    row_spec = pl.BlockSpec(
-        (1, parts, TILE, part_width), lambda i, o, s: (o[i] // tiles, 0, o[i] % tiles, 0)
-    )
-    gate_spec = pl.BlockSpec(
-        (1, 1, TILE, locals_n), lambda i, o, s: (o[i] // tiles, o[i] % tiles, 0, 0)
-    )
-    gates = gates.reshape(shards, tiles, TILE, locals_n)
+            y_acc[...] += dot_nn(gated, wdn_ref[e])
+            dh_acc[...] += dot_nt(d_g, wgu_ref[e, 0]) + dot_nt(d_u, wgu_ref[e, 1])
+            mid_ref[...] = jnp.where(dn_lanes, dot_nt(gated, slim), mid_ref[...])
+            n_e = jnp.where(gate_lanes, dot_nt(d_g, slim), n_ref[...])
+            n_ref[...] = jnp.where(up_lanes, dot_nt(d_u, slim), n_e)
+            gslim_ref[0] += (
+                dot_tn(mid_gate, d_g)
+                + dot_tn(mid_up, d_u)
+                + dot_tn((gate * d_mid_e.astype(f32)).astype(bf16), hidden_b)
+            )
+            return jnp.where(gate_lane == e, d_gate, d_gates)
+
+        dgate_ref[...] = lax.fori_loop(0, locals_n, expert, jnp.zeros(gate_block.shape, f32))
+        n_b = (ADAPTER_SCALE * n_ref[...]).astype(bf16)
+        mid_dn_b = (ADAPTER_SCALE * mid_ref[...]).astype(bf16)
+        y = (y_acc[...] + dot_nn(mid_dn_b, wide)).astype(bf16)
+        dh = (dh_acc[...] + dot_nn(n_b, wide)).astype(bf16)
+
+        def part_out(keep_low):
+            low, high = slice(0, part_width), slice(part_width, width)
+            keep, send = (low, high) if keep_low else (high, low)
+            yk_ref[...] = y[:, keep]
+            ys_ref[...] = y[:, send]
+            dhk_ref[...] = dh[:, keep]
+            dhs_ref[...] = dh[:, send]
+
+        pl.when(low_first)(lambda: part_out(True))
+        pl.when(jnp.logical_not(low_first))(lambda: part_out(False))
+        gwide_ref[0] += dot_tn(n_b, x) + dot_tn(mid_dn_b, ct)
+
+    def row_spec(column):
+        return pl.BlockSpec((TILE, part_width), lambda i, o, s, p: (o[i], column))
+
+    gate_spec = pl.BlockSpec((TILE, locals_n), lambda i, o, s, p: (o[i], 0))
 
     def whole(a):
         zeros = (0,) * a.ndim
-        return pl.BlockSpec(a.shape, lambda i, o, s: zeros, pipeline_mode=pl.Buffered(1))
+        return pl.BlockSpec(a.shape, lambda i, o, s, p: zeros, pipeline_mode=pl.Buffered(1))
 
     def of_set(a):
-        return pl.BlockSpec((1,) + a.shape[1:], lambda i, o, s: (s[i], 0, 0))
-
-    grads = [jax.ShapeDtypeStruct(a.shape, f32) for a in (gu_a, gu_b, dn_a, dn_b)]
+        return pl.BlockSpec((1,) + a.shape[1:], lambda i, o, s, p: (s[i], 0, 0))
+
+    if halved:
+        row_args = h + cot
+        row_specs = [row_spec(0)] * 4
+    else:
+        row_args = (h, h, cot, cot)
+        row_specs = [row_spec(0), row_spec(1)] * 2
+    half = jax.ShapeDtypeStruct((rows, part_width), bf16)
     return pl.pallas_call(
         body,
         grid_spec=pltpu.PrefetchScalarGridSpec(
-            num_scalar_prefetch=2,
-            grid=(shards * tiles,),
-            in_specs=[row_spec, row_spec, gate_spec, whole(w_gu), whole(w_dn)]
-            + [of_set(a) for a in (gu_a, gu_b, dn_a, dn_b)],
-            out_specs=[row_spec, row_spec, gate_spec] + [of_set(a) for a in grads],
-            scratch_shapes=[pltpu.VMEM((TILE, width), f32), pltpu.VMEM((TILE, width), f32)],
+            num_scalar_prefetch=3,
+            grid=(tiles,),
+            in_specs=row_specs + [gate_spec, whole(w_gu), whole(w_dn)]
+            + [of_set(a) for a in adapters] + [of_set(a) for a in sums],
+            out_specs=[row_spec(0)] * 4 + [gate_spec] + [of_set(a) for a in sums],
+            scratch_shapes=[
+                pltpu.VMEM((TILE, width), f32), pltpu.VMEM((TILE, width), f32),
+                pltpu.VMEM((TILE, width), bf16), pltpu.VMEM((TILE, width), bf16),
+                pltpu.VMEM((TILE, adapters[0].shape[1]), f32),
+                pltpu.VMEM((TILE, adapters[0].shape[1]), f32),
+            ],
         ),
-        out_shape=[
-            jax.ShapeDtypeStruct(h.shape, bf16),
-            jax.ShapeDtypeStruct(h.shape, bf16),
-            jax.ShapeDtypeStruct(gates.shape, f32),
-        ]
-        + grads,
+        out_shape=[half] * 4 + [jax.ShapeDtypeStruct(gates.shape, f32)]
+        + [jax.ShapeDtypeStruct(a.shape, f32) for a in sums],
+        input_output_aliases={12 + i: 5 + i for i in range(2)},
         compiler_params=pltpu.CompilerParams(
             dimension_semantics=("arbitrary",), vmem_limit_bytes=60 << 20
         ),
         name="expert_pass",
-    )(order, order_sets, h, cot, gates, w_gu, w_dn, gu_a, gu_b, dn_a, dn_b)
+    )(order, order_sets, part, *row_args, gates, w_gu, w_dn, *adapters, *sums)
 
 
 def per_device(
@@ -392,23 +422,58 @@
     def tile_rows(x):
         return x.reshape(tiles, TILE, x.shape[1])
 
+    def from_shard(x, s):
+        return lax.ppermute(
+            x, "fsdp", [(i, (i - s) % shard_count) for i in range(shard_count)]
+        )
+
+    def to_shard(x, s):
+        return lax.ppermute(
+            x, "fsdp", [(i, (i + s) % shard_count) for i in range(shard_count)]
+        )
+
+    def swap(x):
+        return lax.ppermute(x, "tp", [(0, 1), (1, 0)])
+
+    def across(x, bit):
+        return lax.ppermute(x, "ctx", [(i, i ^ bit) for i in range(slab_count)])
+
+    def sum_parts(x):
+        return x + swap(x)
+
+    def join_parts(mine, other):
+        low_first = part_index == 0
+        return jnp.concatenate(
+            [jnp.where(low_first, mine, other), jnp.where(low_first, other, mine)], axis=1
+        )
+
+    def my_slab(x, axis):
+        size = x.shape[axis] // slab_count
+        return lax.dynamic_slice_in_dim(x, slab_index * size, size, axis=axis)
+
+    def by_shard(pieces_, index):
+        return jnp.take(jnp.stack(pieces_), index % shard_count, axis=0)
+
+    shard_at = jnp.arange(shard_count, dtype=jnp.int32)
+    slab_bits = [1 << i for i in range(slab_count.bit_length() - 1)]
+
     cont_sets = lax.dynamic_slice_in_dim(adapter_ids[0], 1 + slab_index * cont_count, cont_count)
     tile_sets = jnp.concatenate([jnp.broadcast_to(adapter_ids[0, :1], (prompt_tiles,)), cont_sets])
-    all_sets = lax.all_gather(tile_sets, "fsdp", axis=0, tiled=True)
-    count_all = all_sets.shape[0]
-    tile_at = jnp.arange(count_all, dtype=jnp.int32)
-    ahead = (all_sets[None, :] < all_sets[:, None]) | (
-        (all_sets[None, :] == all_sets[:, None]) & (tile_at[None, :] < tile_at[:, None])
-    )
-    rank_of = jnp.sum(ahead.astype(jnp.int32), axis=1)
-    at_rank = (rank_of[None, :] == tile_at[:, None]).astype(jnp.int32)
-    order = jnp.sum(at_rank * tile_at[None, :], axis=1)
-    order_sets = jnp.sum(at_rank * all_sets[None, :], axis=1)
+    step_sets = jnp.stack([tile_sets] + [from_shard(tile_sets, s) for s in range(1, shard_count)])
+    sets_local = qkv_a.shape[0]
+    step_sets = (
+        (step_sets // sets_local - shard_index) % shard_count * sets_local + step_sets % sets_local
+    )
+    tile_at = jnp.arange(tiles, dtype=jnp.int32)
+    left, right = step_sets[:, None, :], step_sets[:, :, None]
+    ahead = (left < right) | ((left == right) & (tile_at[None, None, :] < tile_at[None, :, None]))
+    rank_of = jnp.sum(ahead.astype(jnp.int32), axis=2)
+    at_rank = (rank_of[:, None, :] == tile_at[None, :, None]).astype(jnp.int32)
+    step_order = jnp.sum(at_rank * tile_at[None, None, :], axis=2)
+    step_order_sets = jnp.sum(at_rank * left, axis=2)
     set_at = jnp.arange(SETS, dtype=jnp.int32)
-    present = jnp.any(set_at[:, None] == all_sets[None, :], axis=1)
     tile_hot = (set_at[:, None] == tile_sets[None, :]).astype(f32)
 
-    sets_local = qkv_a.shape[0]
 
     def as_rows(x):
         return x.reshape(x.shape[0], -1, local_width)
@@ -426,7 +491,14 @@
         router_rows(router_b),
     ]
     sizes = [p.shape[1] for p in pieces]
-    packed = lax.all_gather(jnp.concatenate(pieces, axis=1), "fsdp", axis=0, tiled=True)
+    rows_n = sum(sizes)
+    rows_pad = -rows_n % (16 * slab_count)
+    packed = my_slab(
+        jnp.pad(jnp.concatenate(pieces, axis=1), ((0, 0), (0, rows_pad), (0, 0))), 1
+    )
+    packed = lax.all_gather(packed, ("fsdp", "ctx"), axis=0, tiled=False)
+    packed = packed.reshape((shard_count, slab_count) + packed.shape[1:]).transpose(0, 2, 1, 3, 4)
+    packed = packed.reshape(SETS, rows_n + rows_pad, local_width)
     picked = jnp.take(packed, tile_sets, axis=0)
     cuts = [sum(sizes[:i]) for i in range(len(sizes) + 1)]
 
@@ -448,21 +520,59 @@
     gain_k = k_gain.astype(f32)
     first_scale = lax.rsqrt(jnp.mean(token_vals * token_vals, axis=1, keepdims=True) + epsilon)
     h_first = (token_vals * first_scale * gain_in).astype(bf16)
-    whole_qkv = lax.all_gather(w_qkv, "fsdp", axis=0, tiled=True)
-    proj = jnp.einsum("nd,djo->jno", h_first, whole_qkv, preferred_element_type=f32)
+
+    def exchange(x, bits):
+        blocks = {0: x}
+        for bit in bits:
+            names = sorted(blocks)
+            got = across(jnp.stack([blocks[i] for i in names]), bit)
+            blocks.update({i ^ bit: got[at] for at, i in enumerate(names)})
+        return [blocks[i] for i in range(slab_count)]
+
+    half_n = shard_count // 2
+    near_at = jnp.bitwise_xor(jnp.arange(slab_count, dtype=jnp.int32), slab_index)[None, :]
+    step_at = ((shard_at - shard_index) % shard_count)[:, None]
+    row_at = (step_at // half_n) * (half_n * slab_count) + near_at * half_n + step_at % half_n
+    row_at = row_at.reshape(-1)
+
+    def fetch(x):
+        mine = my_slab(x, 0)
+        return [mine] + [from_shard(mine, s) for s in range(1, shard_count)]
+
+    def spread(got):
+        near = exchange(jnp.stack(got[:half_n]), slab_bits)
+        far = exchange(jnp.stack(got[half_n:]), slab_bits[::-1])
+        rows_ = jnp.concatenate(near + far, axis=0)
+        return jnp.take(rows_, row_at, axis=0).reshape(full_width, local_width)
+
+    got_k = fetch(w_qkv[:, 1])
+    got_k, w_v, w_q = lax.optimization_barrier((got_k, w_qkv[:, 2], w_qkv[:, 0]))
+    got_v = fetch(w_v)
+    got_v, w_q = lax.optimization_barrier((got_v, w_q))
+    got_q = fetch(w_q)
+    got_q, w_out, cot_mine, gu_a, gu_b, down_a, down_b = lax.optimization_barrier(
+        (got_q, w_out, my_part(cotangent), gu_a, gu_b, down_a, down_b)
+    )
+    weights = [spread(got_q), spread(got_k), spread(got_v)]
     mid_qkv = (
         ADAPTER_SCALE
         * jnp.einsum("tnd,tjrd->tnjr", tile_rows(h_first), t_qkv_a, preferred_element_type=f32)
     ).astype(bf16)
-    proj = proj + jnp.einsum(
-        "tnjr,tjro->jtno", mid_qkv, t_qkv_b, preferred_element_type=f32
-    ).reshape(3, row_count, local_width)
-    q_raw, k_raw = proj[0], proj[1]
-    squares = lax.psum(
-        jnp.stack([jnp.sum(q_raw * q_raw, axis=1), jnp.sum(k_raw * k_raw, axis=1)]), "tp"
-    )
-    q_scale = lax.rsqrt(squares[0] / full_width + epsilon)[:, None]
-    k_scale = lax.rsqrt(squares[1] / full_width + epsilon)[:, None]
+
+    def project(j):
+        return jnp.dot(h_first, weights[j], preferred_element_type=f32) + jnp.einsum(
+            "tnr,tro->tno", mid_qkv[:, :, j], t_qkv_b[:, j], preferred_element_type=f32
+        ).reshape(row_count, local_width)
+
+    def scale_of(raw):
+        squares = sum_parts(jnp.sum(raw * raw, axis=1))
+        return lax.rsqrt(squares / full_width + epsilon)[:, None]
+
+    k_raw = project(1)
+    k_scale = scale_of(k_raw)
+    value_rows = project(2).astype(bf16)
+    q_raw = project(0)
+    q_scale = scale_of(q_raw)
 
     def heads_of(x):
         return x.reshape(x.shape[0], local_heads, HEAD_DIM)
@@ -477,24 +587,73 @@
         .reshape(row_count, local_width)
         .astype(bf16)
     )
-    value_rows = proj[2].astype(bf16)
-    prompt_keys = lax.all_gather(key_rows[:prompt_rows], "ctx", axis=0, tiled=True)
-    prompt_values = lax.all_gather(value_rows[:prompt_rows], "ctx", axis=0, tiled=True)
+
+    def exchange_back(x, bits):
+        blocks = {i: x[i * prompt_rows : (i + 1) * prompt_rows] for i in range(slab_count)}
+        for bit in bits:
+            sent = sorted(i for i in blocks if i & bit)
+            got = across(jnp.stack([blocks[i].astype(bf16) for i in sent]), bit)
+            for at, i in enumerate(sent):
+                blocks[i ^ bit] = blocks[i ^ bit].astype(f32) + got[at].astype(f32)
+                del blocks[i]
+        return blocks[0]
+
+    prompt_keys = jnp.concatenate(exchange(key_rows[:prompt_rows], slab_bits), axis=0)
+    prompt_values = jnp.concatenate(exchange(value_rows[:prompt_rows], slab_bits[::-1]), axis=0)
     key_own, value_own = key_rows[prompt_rows:], value_rows[prompt_rows:]
+    def experts_of_sets(x, axes):
+        count, width_x = lax.axis_size(axes), x.shape[3]
+        x = x.reshape(sets_local, shard_count, -1, width_x).transpose(1, 0, 2, 3)
+        x = x.reshape(shard_count, count, -1, width_x)
+        got = []
+        for s in range(shard_count):
+            at = ((shard_index - s) % shard_count, lax.axis_index(axes), 0, 0)
+            block = lax.dynamic_slice(x, at, (1, 1) + x.shape[2:])[0, 0]
+            got.append(from_shard(block, s) if s else block)
+        return jnp.stack(got)
+
+    def gather_adapters(x, axes):
+        whole = lax.all_gather(x, axes, axis=1, tiled=True)
+        return whole.reshape(SETS, -1, x.shape[2])
+
+    def sets_of_experts(x, axes):
+        width_x = x.shape[2]
+        x = x.astype(bf16).reshape(shard_count, -1, width_x)
+        mine = lax.psum_scatter(x, axes, scatter_dimension=1, tiled=True)
+        got = [to_shard(mine[s], s) if s else mine[s] for s in range(shard_count)]
+        whole = lax.all_gather(by_shard(got, shard_index - shard_at), axes, axis=1, tiled=True)
+        return whole.reshape(shard_count, sets_local, locals_n, -1, width_x).transpose(1, 0, 2, 3, 4)
+
+    wide = jnp.concatenate(
+        [gu_a.transpose(0, 1, 3, 4, 2).reshape(sets_local, EXPERTS, -1, full_width), down_b], axis=2
+    )
+    slim = jnp.concatenate(
+        [
+            gu_b.transpose(0, 1, 3, 2, 4).reshape(sets_local, EXPERTS, -1, ff_local),
+            down_a.transpose(0, 1, 3, 2),
+        ],
+        axis=2,
+    )
+    wide = experts_of_sets(wide, ("ctx", "tp"))
+    slim = experts_of_sets(slim, ("ctx",))
+    cot_got = [from_shard(cot_mine, s) for s in range(1, shard_count)]
+    query_rows, wide, slim = lax.optimization_barrier((query_rows, wide, slim))
+    wide = gather_adapters(wide, ("ctx", "tp"))
+    slim = gather_adapters(slim, ("ctx",))
     attention_rows, log_total = attention_forward(
         slab, query_rows, prompt_keys, prompt_values, key_own, value_own, prompt_rows
     )
-    whole_out = lax.all_gather(w_out, "fsdp", axis=1, tiled=True)
+    attention_rows, cot_got = lax.optimization_barrier((attention_rows, cot_got))
+    whole_out = lax.all_gather(my_slab(w_out, 1), ("fsdp", "ctx"), axis=1, tiled=True)
     mid_out = (
         ADAPTER_SCALE
         * jnp.einsum("tnd,trd->tnr", tile_rows(attention_rows), t_out_a, preferred_element_type=f32)
     ).astype(bf16)
-    branch = lax.psum(
+    branch = sum_parts(
         jnp.dot(attention_rows, whole_out, preferred_element_type=f32)
         + jnp.einsum("tnr,trd->tnd", mid_out, t_out_b, preferred_element_type=f32).reshape(
             row_count, full_width
-        ),
-        "tp",
+        )
     )
     x_mid = token_vals + branch
     mid_scale = lax.rsqrt(jnp.mean(x_mid * x_mid, axis=1, keepdims=True) + epsilon)
@@ -513,46 +672,51 @@
     )
     gates = jnp.where(chosen, expert_probs, 0.0)
 
-    def gather_rows(x):
-        return lax.all_gather(my_part(x), ("fsdp", "tp"), axis=0, tiled=False).reshape(
-            shard_count, part_count, row_count, part_width
-        )
-
-    def experts_of_sets(x):
-        return lax.all_to_all(x, "fsdp", split_axis=1, concat_axis=0, tiled=True)
-
-    e_gu_a = experts_of_sets(gu_a.transpose(0, 1, 3, 4, 2)).reshape(SETS, -1, full_width)
-    e_gu_b = experts_of_sets(gu_b.transpose(0, 1, 3, 2, 4)).reshape(SETS, -1, ff_local)
-    e_dn_a = experts_of_sets(down_a.transpose(0, 1, 3, 2)).reshape(SETS, -1, ff_local)
-    e_dn_b = experts_of_sets(down_b).reshape(SETS, -1, full_width)
-    cot_all = gather_rows(cotangent)
-    h_all = gather_rows(h_second)
-    gates_all = lax.all_gather(gates, "fsdp", axis=0, tiled=False)
-    my_gates = lax.dynamic_slice_in_dim(gates_all, shard_index * locals_n, locals_n, axis=2)
-    y_part, dh_part, d_gates_part, g_gu_a, g_gu_b, g_dn_a, g_dn_b = expert_pass(
-        order, order_sets, h_all, cot_all, my_gates, w_gate_up.transpose(0, 2, 1, 3), w_down,
-        e_gu_a, e_gu_b, e_dn_a, e_dn_b,
-    )
-
-    def return_rows(x):
-        own = lax.psum_scatter(
-            x.reshape(shard_count * part_count, row_count, part_width),
-            ("fsdp", "tp"), scatter_dimension=0, tiled=False,
-        )
-        return own
-
-    d_gates_wide = lax.dynamic_update_slice_in_dim(
-        jnp.zeros((shard_count, row_count, EXPERTS), f32),
-        d_gates_part.reshape(shard_count, row_count, locals_n),
-        shard_index * locals_n, axis=2,
-    )
-    d_gates = lax.psum(
-        lax.psum_scatter(d_gates_wide, "fsdp", scatter_dimension=0, tiled=False), "tp"
-    )
-    d_second_routed = lax.all_gather(return_rows(dh_part), "tp", axis=1, tiled=True).astype(f32)
-    mixed = lax.all_gather(
-        (my_part(x_mid) + return_rows(y_part).astype(f32)).astype(bf16), "tp", axis=1, tiled=True
-    )
+    gu_rank = 2 * RANK
+    adapters = (wide, slim)
+    sums = tuple(jnp.zeros(a.shape, f32) for a in adapters)
+    w_gu = w_gate_up.transpose(0, 2, 1, 3)
+    part = part_index.reshape(1).astype(jnp.int32)
+    h_mine = my_part(h_second)
+    cot_steps = [cotangent] + [(x, swap(x)) for x in cot_got]
+    gates_t = gates.T
+    gate_steps = []
+    for s in range(shard_count):
+        block = lax.dynamic_slice_in_dim(
+            gates_t, ((shard_index - s) % shard_count) * locals_n, locals_n, axis=0
+        )
+        gate_steps.append((from_shard(block, s) if s else block).T)
+    y_steps, dh_steps, d_gate_steps = [], [], []
+    h_step = h_second
+    h_next = from_shard(h_mine, 1)
+    for s in range(shard_count):
+        y_keep, y_send, dh_keep, dh_send, d_gate, *sums = expert_pass(
+            step_order[s], step_order_sets[s], part, h_step, cot_steps[s], gate_steps[s], w_gu,
+            w_down, adapters, tuple(sums),
+        )
+        dh = dh_keep.astype(f32) + swap(dh_send).astype(f32)
+        if s:
+            dh = dh.astype(bf16)
+        if s + 1 < shard_count:
+            h_step = (h_next, swap(h_next))
+            sums, h_step, h_mine, dh, dh_steps = lax.optimization_barrier(
+                (sums, h_step, h_mine, dh, dh_steps)
+            )
+            if s + 2 < shard_count:
+                h_next = from_shard(h_mine, s + 2)
+        dh_steps.append(to_shard(dh, s) if s else dh)
+        d_gate = d_gate.T
+        d_gate_steps.append(to_shard(d_gate, s) if s else d_gate)
+        y_steps.append((y_keep, y_send))
+    d_gates = sum_parts(
+        by_shard(d_gate_steps, shard_index - shard_at).reshape(EXPERTS, row_count)
+    ).T
+    d_second_mine = sum(dh.astype(f32) for dh in dh_steps).astype(bf16)
+    y_steps = [keep.astype(f32) + swap(send).astype(f32) for keep, send in y_steps]
+    y_steps = [y.astype(bf16) if s else y for s, y in enumerate(y_steps)]
+    d_second_mine, y_steps = lax.optimization_barrier((d_second_mine, y_steps))
+    d_second_routed = join_parts(d_second_mine, swap(d_second_mine)).astype(f32)
+    y_odd = [to_shard(y_steps[s], s) for s in range(1, shard_count, 2)]
 
     d_probs = jnp.where(chosen, d_gates, 0.0)
     d_logits = (
@@ -591,17 +755,18 @@
         slab, query_rows, prompt_keys, prompt_values, key_own, value_own, attention_rows,
         d_att_rows, log_total, prompt_rows,
     )
-    d_key_prompt = lax.psum_scatter(d_key_all, "ctx", scatter_dimension=0, tiled=True)
-    d_value_prompt = lax.psum_scatter(d_value_all, "ctx", scatter_dimension=0, tiled=True)
-    d_key = jnp.concatenate([d_key_prompt.astype(f32), d_key_own], axis=0)
-    d_value = jnp.concatenate([d_value_prompt.astype(f32), d_value_own], axis=0)
+    d_query, y_odd, y_steps = lax.optimization_barrier((d_query, y_odd, y_steps))
+    y_even = [to_shard(y_steps[s], s) for s in range(2, shard_count, 2)]
+    d_key_prompt = exchange_back(d_key_all, slab_bits)
+    d_value_prompt = exchange_back(d_value_all, slab_bits[::-1])
+    d_key = jnp.concatenate([d_key_prompt, d_key_own], axis=0)
+    d_value = jnp.concatenate([d_value_prompt, d_value_own], axis=0)
     d_q_norm = rotate(heads_of(d_query), cosine, -sine_part).reshape(row_count, local_width)
     d_k_norm = rotate(heads_of(d_key), cosine, -sine_part).reshape(row_count, local_width)
-    dots = lax.psum(
+    dots = sum_parts(
         jnp.stack(
             [jnp.sum(gain_q * q_raw * d_q_norm, axis=1), jnp.sum(gain_k * k_raw * d_k_norm, axis=1)]
-        ),
-        "tp",
+        )
     )
     d_q_raw = (
         q_scale * gain_q * d_q_norm
@@ -612,17 +777,21 @@
         - k_raw * (k_scale * k_scale * k_scale) * dots[1][:, None] / full_width
     )
     d_proj = jnp.stack([d_q_raw, d_k_raw, d_value], axis=0).astype(bf16)
+    d_proj, y_even = lax.optimization_barrier((d_proj, y_even))
+    mixed_mine = sum(
+        [y.astype(f32) for y in y_steps[:1] + y_odd + y_even], my_part(x_mid)
+    ).astype(bf16)
+    mixed = join_parts(mixed_mine, swap(mixed_mine))
     dp_tiles = d_proj.reshape(3, tiles, TILE, local_width)
     d_mid_qkv = (
         ADAPTER_SCALE
         * jnp.einsum("jtno,tjro->tnjr", dp_tiles, t_qkv_b, preferred_element_type=f32)
     ).astype(bf16)
-    d_first = lax.psum(
-        jnp.einsum("jno,djo->nd", d_proj, whole_qkv, preferred_element_type=f32)
+    d_first = sum_parts(
+        sum(dot_nt(d_proj[j], weights[j]) for j in range(3))
         + jnp.einsum("tnjr,tjrd->tnd", d_mid_qkv, t_qkv_a, preferred_element_type=f32).reshape(
             row_count, full_width
-        ),
-        "tp",
+        )
     )
     grad_input = d_x_mid + rms_back(token_vals, gain_in, d_first, first_scale, full_width)
     g_qkv_b = jnp.einsum("tnjr,jtno->tjro", mid_qkv, dp_tiles, preferred_element_type=f32)
@@ -632,47 +801,50 @@
 
     def to_sets(pieces_):
         rows_ = jnp.concatenate(pieces_, axis=1)
-        return jnp.sum(tile_hot[:, :, None, None] * rows_[None], axis=1).astype(bf16)
-
-    def reduced(x, axes):
-        mine = lax.psum_scatter(x, "fsdp", scatter_dimension=0, tiled=True)
-        return lax.psum(mine, axes).astype(f32)
-
-    both = reduced(to_sets([as_rows(g_qkv_a), as_rows(g_out_b)]), ("ctx", "tp"))
-    one = reduced(
-        to_sets(
-            [as_rows(g_qkv_b), as_rows(g_out_a), as_rows(g_router_a), router_rows(g_router_b)]
-        ),
-        "ctx",
-    )
-    n0, n1, n2, n3, n4 = sizes[0], sizes[1], sizes[2], sizes[3], sizes[4]
-    grad_qkv_a = both[:, :n0].reshape(sets_local, 3, RANK, full_width).transpose(0, 3, 1, 2)
-    grad_out_b = both[:, n0 : n0 + n3].reshape(out_b.shape)
-    grad_qkv_b = one[:, :n1].reshape(sets_local, 3, RANK, local_width).transpose(0, 2, 1, 3)
-    grad_out_a = one[:, n1 : n1 + n2].reshape(sets_local, RANK, local_width).transpose(0, 2, 1)
+        return jnp.sum(tile_hot[:, :, None, None] * rows_[None], axis=1)
+
+    def reduced(x):
+        n_rows = x.shape[1]
+        pad = -n_rows % (16 * slab_count)
+        x = jnp.pad(x.astype(bf16), ((0, 0), (0, pad), (0, 0)))
+        x = x.reshape(shard_count, sets_local, slab_count, -1, local_width)
+        x = x.transpose(0, 2, 1, 3, 4).reshape((shard_count * slab_count, sets_local, -1, local_width))
+        mine = lax.psum_scatter(x, ("fsdp", "ctx"), scatter_dimension=0, tiled=False)
+        return lax.all_gather(mine, "ctx", axis=1, tiled=True)[:, :n_rows].astype(f32)
+
+    early_both = sum_parts(to_sets([as_rows(g_out_b)]))
+    early_one = to_sets([as_rows(g_out_a), as_rows(g_router_a), router_rows(g_router_b)])
+    early = reduced(jnp.concatenate([early_both, early_one], axis=1))
+    late_both = sum_parts(to_sets([as_rows(g_qkv_a)]))
+    late = reduced(jnp.concatenate([late_both, to_sets([as_rows(g_qkv_b)])], axis=1))
+    n0, n2, n3, n4 = sizes[0], sizes[2], sizes[3], sizes[4]
+    grad_qkv_a = late[:, :n0].reshape(sets_local, 3, RANK, full_width).transpose(0, 3, 1, 2)
+    grad_qkv_b = late[:, n0:].reshape(sets_local, 3, RANK, local_width).transpose(0, 2, 1, 3)
+    grad_out_b = early[:, :n3].reshape(out_b.shape)
+    grad_out_a = early[:, n3 : n3 + n2].reshape(sets_local, RANK, local_width).transpose(0, 2, 1)
     grad_router_a = (
-        one[:, n1 + n2 : n1 + n2 + n4].reshape(sets_local, RANK, full_width).transpose(0, 2, 1)
-    )
-    grad_router_b = one[:, n1 + n2 + n4, : RANK * EXPERTS].reshape(router_b.shape)
-
-    def expert_grad(g, axes):
-        g = jnp.where(present[:, None, None], g, 0.0).astype(bf16)
-        g = lax.psum(g, axes)
-        g = g.reshape(SETS, locals_n, -1, g.shape[2])
-        return lax.all_to_all(g, "fsdp", split_axis=0, concat_axis=1, tiled=True).astype(f32)
+        early[:, n3 + n2 : n3 + n2 + n4].reshape(sets_local, RANK, full_width).transpose(0, 2, 1)
+    )
+    grad_router_b = early[:, n3 + n2 + n4, : RANK * EXPERTS].reshape(router_b.shape)
+
+    g_wide = sets_of_experts(sums[0], ("ctx", "tp"))
+    g_slim = sets_of_experts(sums[1], ("ctx",))
+
+    def of_experts(g):
+        return g.reshape((sets_local, EXPERTS) + g.shape[3:]).astype(f32)
 
     grad_gu_a = (
-        expert_grad(g_gu_a, ("ctx", "tp"))
+        of_experts(g_wide[:, :, :, :gu_rank])
         .reshape(sets_local, EXPERTS, 2, RANK, full_width)
         .transpose(0, 1, 4, 2, 3)
     )
     grad_gu_b = (
-        expert_grad(g_gu_b, "ctx")
+        of_experts(g_slim[:, :, :, :gu_rank])
         .reshape(sets_local, EXPERTS, 2, RANK, ff_local)
         .transpose(0, 1, 3, 2, 4)
     )
-    grad_down_a = expert_grad(g_dn_a, "ctx").transpose(0, 1, 3, 2)
-    grad_down_b = expert_grad(g_dn_b, ("ctx", "tp"))
+    grad_down_a = of_experts(g_slim[:, :, :, gu_rank:]).transpose(0, 1, 3, 2)
+    grad_down_b = of_experts(g_wide[:, :, :, gu_rank:])
     return (
         mixed, grad_input, grad_qkv_a, grad_qkv_b, grad_out_a, grad_out_b, grad_router_a,
         grad_router_b, grad_gu_a, grad_gu_b, grad_down_a, grad_down_b,

time: 2420 us -> 1920 us (0.79)
  waiting for transfers between devices: 1290 us -> 662 us
  blocking collectives: 259 us -> 26 us
  starting transfers between devices: 31.7 us -> 183 us
  other arithmetic: 128 us -> 235 us
  Pallas kernels: 414 us -> 483 us
  local copies, waits for them, and re-layouts: 145 us -> 189 us
    ppermute x0 -> x86, waiting for transfers between devices: none -> 590 us  [the longest x27 283 us: from_shard(): lax.ppermute(x, 'fsdp', [(i, (i - s) % shard_count) for i in range(shard_...]
    reduce_scatter x6 -> x4, waiting for transfers between devices: 440 us -> 42.7 us  [the longest x2 42.6 us: reduced(): lax.psum_scatter(x, ('fsdp', 'ctx'), scatter_dimension=0, tiled=False)]
    all_gather x9 -> x6, waiting for transfers between devices: 392 us -> 30 us  [the longest x2 30 us: sets_of_experts(): lax.all_gather(by_shard(got, shard_index - shard_at), axes, axis=1, tiled...]
    all_to_all x7 -> x0, waiting for transfers between devices: 225 us -> none  [the longest x4 156 us: experts_of_sets(): return lax.all_to_all(x, 'fsdp', split_axis=1, concat_axis=0, tiled=True)]
    psum x5 -> x0, waiting for transfers between devices: 183 us -> none  [the longest x2 132 us: reduced(): return lax.psum(mine, axes).astype(f32)]
    unnamed x1 -> x0, blocking collectives: 183 us -> none
    ppermute x0 -> x86, starting transfers between devices: none -> 182 us  [the longest x27 111 us: from_shard(): lax.ppermute(x, 'fsdp', [(i, (i - s) % shard_count) for i in range(shard_...]
    pallas_call x1 -> x4, Pallas kernels: 292 us -> 361 us  [expert_pass(): pl.pallas_call(body, grid_spec=pltpu.PrefetchScalarGridSpec(num_scalar_pr...]
  transfers between devices with their start and end apart: 28 -> 96, of which waited for: 23 -> 33; matrix products, arithmetic and copies ran while one was open for 11% -> 26% of each run, Pallas kernels for 2% -> 21%
where the time goes in v2:
time: 1920 us; the launch traced here: 1910 us
  waiting for transfers between devices  662 us (34%)
  Pallas kernels  483 us (25%)
  other arithmetic  235 us (12%)
  local copies, waits for them, and re-layouts  189 us (10%)
  starting transfers between devices  183 us (10%)
  matrix products  112 us (6%)
  blocking collectives  26 us (1%)
    pallas_call x4, Pallas kernels, expert_pass(): pl.pallas_call(body, grid_spec=pltpu.PrefetchScalarGridSpec(num_scalar_pr...  361 us
    ppermute x27, waiting for transfers between devices, from_shard(): lax.ppermute(x, 'fsdp', [(i, (i - s) % shard_count) for i in range(shard_...  283 us
    ppermute x15, waiting for transfers between devices, to_shard(): lax.ppermute(x, 'fsdp', [(i, (i + s) % shard_count) for i in range(shard_...  176 us
    ppermute x20, waiting for transfers between devices, across(): return lax.ppermute(x, 'ctx', [(i, i ^ bit) for i in range(slab_count)])  120 us
    ppermute x27, starting transfers between devices, from_shard(): lax.ppermute(x, 'fsdp', [(i, (i - s) % shard_count) for i in range(shard_...  111 us
    unnamed x302, local copies, waits for them, and re-layouts  92.1 us
    pallas_call x1, Pallas kernels, attention_backward(): pl.pallas_call(body, grid_spec=pltpu.PrefetchScalarGridSpec(num_scalar_pr...  70.9 us
    pallas_call x1, Pallas kernels, attention_forward(): pl.pallas_call(body, grid_spec=pltpu.PrefetchScalarGridSpec(num_scalar_pr...  51.2 us
  transfers between devices with their start and end apart: 96, of which 33 were waited for; matrix products, arithmetic and copies ran while one was open for 26% of the time, Pallas kernels for 21%

profile of v2, /device:TPU:0, one launch (start us, length us, event | category | flops | bytes accessed | tf_op | source)
XLA Modules:
  0.0 1906.4 jit_solution(16940347417046662444)
XLA Ops:
  36.0 8.6 collective-permute-done.1
  45.1 6.6 collective-permute-start.5
  62.6 18.1 collective-permute-done.4
  81.8 6.0 collective-permute-start.8
  93.4 6.9 collective-permute-done.8
  101.8 17.5 collective-permute-done.7
  153.6 22.8 %collective-permute-done.21 = bf16[2,2,128,1024]{3,2,1,0:T(8,128)(2,1)S(1)} collective-permute-done((bf16[2,2,128,1024]{3,2,1,0:T(8,128)(2,1)S(1)}, bf16[2,2,128,1024]{3,2,1,0:T(8,128)(2,1)S(1)}, u32[]{:S(2)}, u32[]{:S(2)}) %collective-permute-start.21) | collective-permute-done | bytes 1048608 | tf_op jit(solution)/shard_map/ppermute | solution.py:439
  183.4 5.1 gather_fusion.5
  188.5 10.4 collective-permute-done.28
  208.7 5.1 gather_fusion.6
  213.8 6.5 collective-permute-done.10
  228.1 5.0 gather_fusion.4
  233.1 9.0 broadcast_select_fusion
  242.2 4.9 copy.169
  264.0 4.6 multiply_reduce_fusion.6
  272.3 5.5 fusion.22
  295.2 10.4 collective-permute-done.31
  313.6 19.0 collective-permute-start.19
  353.4 5.0 collective-permute-start.35
  358.4 90.9 %collective-permute-done.15 = bf16[48,2048]{1,0:T(8,128)(2,1)} collective-permute-done((bf16[48,2048]{1,0:T(8,128)(2,1)S(1)}, bf16[48,2048]{1,0:T(8,128)(2,1)}, u32[]{:S(2)}, u32[]{:S(2)}) %collective-permute-start.15) | collective-permute-done | bytes 196640 | tf_op jit(solution)/shard_map/ppermute | solution.py:426
  465.0 8.9 pad_maximum_fusion.3.v_ref
  479.0 51.2 %attention_forward.1 = (bf16[1024,1024]{1,0:T(8,128)(2,1)}, f32[8,1,1024]{2,1,0:T(1,128)}) custom-call(s32[1]{0:T(128)} %bitcast.slab_ref, bf16[1024,1024]{1,0:T(8,128)(2,1)} %bitcast.533, bf16[2048,1024]{1,0:T(8,128)(2,1)} %pad_maximum_fusion.2.k_ref, bf16[2048,1024]{1,0:T(8,128)(2,1)} %pad_maximum_fusion.3.v_ref, bf16[512,1024]{1,0:T(8,128)(2,1)} %bitcast.542, ...), custom_call_target="tpu_custom_call" | custom-call | tf_op jit(solution)/shard_map/attention_forward/pallas_call | solution.py:138
  530.3 13.0 collective-permute-done.33.cot0_ref
  545.6 4.7 fusion.103
  550.3 10.2 bitcast_add_fusion.2
  564.3 16.0 copy.251
  580.9 9.2 multiply_reduce_fusion.2
  613.3 6.1 broadcast_in_dim.65.swide_ref
  619.3 90.1 %expert_pass.4 = (bf16[1024,1024]{1,0:T(8,128)(2,1)}, bf16[1024,1024]{1,0:T(8,128)(2,1)}, bf16[1024,1024]{1,0:T(8,128)(2,1)}, bf16[1024,1024]{1,0:T(8,128)(2,1)}...) custom-call(s32[4]{0:T(128)} %get-tuple-element.362.order_ref, ...), custom_call_target="tpu_custom_call", output_to_operand_aliasing={{5}: (12, {}), {6}: (13, {})} | custom-call | tf_op jit(solution)/shard_map/expert_pass/pallas_call | solution.py:366
  720.4 56.3 %collective-permute-done.44 = f32[4,1024]{0,1:T(8,128)S(1)} collective-permute-done((f32[4,1024]{0,1:T(8,128)S(1)}, f32[4,1024]{0,1:T(8,128)S(1)}, u32[]{:S(2)}, u32[]{:S(2)}) %collective-permute-start.44) | collective-permute-done | bytes 16416 | tf_op jit(solution)/shard_map/ppermute | solution.py:426
  777.5 89.8 %expert_pass.5 = (bf16[1024,1024]{1,0:T(8,128)(2,1)}, bf16[1024,1024]{1,0:T(8,128)(2,1)}, bf16[1024,1024]{1,0:T(8,128)(2,1)}, bf16[1024,1024]{1,0:T(8,128)(2,1)}...) custom-call(s32[4]{0:T(128)} %get-tuple-element.360.order_ref, ...), custom_call_target="tpu_custom_call", output_to_operand_aliasing={{5}: (12, {}), {6}: (13, {})} | custom-call | tf_op jit(solution)/shard_map/expert_pass/pallas_call | solution.py:366
  877.0 46.4 %collective-permute-start.50 = (bf16[1024,1024]{1,0:T(8,128)(2,1)}, bf16[1024,1024]{1,0:T(8,128)(2,1)S(1)}, u32[]{:S(2)}, u32[]{:S(2)}) collective-permute-start(bf16[1024,1024]{1,0:T(8,128)(2,1)} %constant_dynamic-slice_fusion), channel_id=1, source_target_pairs={{0,8},{8,16},{16,24},{24,0},{1,9},{9,17},{17,25},{25,1},{2,10},{10... | collective-permute-start | bytes 6291464 | tf_op jit(solution)/shard_map/ppermute | solution.py:426
  923.4 56.7 %collective-permute-done.49 = f32[4,1024]{0,1:T(8,128)S(1)} collective-permute-done((f32[4,1024]{0,1:T(8,128)S(1)}, f32[4,1024]{0,1:T(8,128)S(1)}, u32[]{:S(2)}, u32[]{:S(2)}) %collective-permute-start.49) | collective-permute-done | bytes 16416 | tf_op jit(solution)/shard_map/ppermute | solution.py:426
  980.9 90.8 %expert_pass.6 = (bf16[1024,1024]{1,0:T(8,128)(2,1)}, bf16[1024,1024]{1,0:T(8,128)(2,1)}, bf16[1024,1024]{1,0:T(8,128)(2,1)}, bf16[1024,1024]{1,0:T(8,128)(2,1)}...) custom-call(s32[4]{0:T(128)} %get-tuple-element.359.order_ref, ...), custom_call_target="tpu_custom_call", output_to_operand_aliasing={{5}: (12, {}), {6}: (13, {})} | custom-call | tf_op jit(solution)/shard_map/expert_pass/pallas_call | solution.py:366
  1071.8 10.7 collective-permute-start.53
  1087.0 44.9 %collective-permute-done.53 = bf16[1024,1024]{1,0:T(8,128)(2,1)S(1)} collective-permute-done((bf16[1024,1024]{1,0:T(8,128)(2,1)}, bf16[1024,1024]{1,0:T(8,128)(2,1)S(1)}, u32[]{:S(2)}, u32[]{:S(2)}) %collective-permute-start.53) | collective-permute-done | bytes 2097184 | tf_op jit(solution)/shard_map/ppermute | solution.py:431
  1133.9 9.0 collective-permute-done.56
  1143.7 89.9 %expert_pass.7 = (bf16[1024,1024]{1,0:T(8,128)(2,1)}, bf16[1024,1024]{1,0:T(8,128)(2,1)}, bf16[1024,1024]{1,0:T(8,128)(2,1)}, bf16[1024,1024]{1,0:T(8,128)(2,1)}...) custom-call(s32[4]{0:T(128)} %get-tuple-element.361.order_ref, ...), custom_call_target="tpu_custom_call", output_to_operand_aliasing={{5}: (12, {}), {6}: (13, {})} | custom-call | tf_op jit(solution)/shard_map/expert_pass/pallas_call | solution.py:366
  1252.3 8.3 convert_element_type.347
  1273.5 59.1 %collective-permute-done.54 = bf16[1024,1024]{1,0:T(8,128)(2,1)} collective-permute-done((bf16[1024,1024]{1,0:T(8,128)(2,1)}, bf16[1024,1024]{1,0:T(8,128)(2,1)}, u32[]{:S(2)}, u32[]{:S(2)}) %collective-permute-start.54) | collective-permute-done | bytes 2097184 | tf_op jit(solution)/shard_map/ppermute | solution.py:431
  1332.6 15.6 collective-permute-done.58
  1354.4 56.6 %collective-permute-done.65 = f32[4,1024]{0,1:T(8,128)} collective-permute-done((f32[4,1024]{0,1:T(8,128)}, f32[4,1024]{0,1:T(8,128)}, u32[]{:S(2)}, u32[]{:S(2)}) %collective-permute-start.65) | collective-permute-done | bytes 16416 | tf_op jit(solution)/shard_map/ppermute | solution.py:431
  1420.6 5.7 fusion.105
  1428.1 12.4 collective-permute-start.85
  1447.7 7.4 multiply_reduce_fusion.1
  1455.1 15.3 fusion.95
  1474.8 6.2 fusion.21.da_ref
  1480.9 70.9 %attention_backward.1 = (f32[1024,1024]{1,0:T(8,128)}, bf16[2048,1024]{1,0:T(8,128)(2,1)}, bf16[2048,1024]{1,0:T(8,128)(2,1)}, f32[512,1024]{1,0:T(8,128)}, f32[512,1024]{1,0:T(8,128)}) custom-call(s32[1]{0:T(128)} %bitcast.slab_ref, bf16[1024,1024]{1,0:T(8,128)(2,1)} %bitcast.534, bf16[2048,1024]{1,0:T(8,128)(2,1)} %pad_maximum_fusion.2.k_ref, ...), custom_call_target="tpu_custom_call" | custom-call | tf_op jit(solution)/shard_map/attention_backward/pallas_call | solution.py:215
  1568.6 5.4 copy.224
  1574.4 40.4 %collective-permute-done.70 = bf16[2,512,1024]{2,1,0:T(8,128)(2,1)} collective-permute-done((bf16[2,512,1024]{2,1,0:T(8,128)(2,1)}, bf16[2,512,1024]{2,1,0:T(8,128)(2,1)}, u32[]{:S(2)}, u32[]{:S(2)}) %collective-permute-start.70) | collective-permute-done | bytes 2097184 | tf_op jit(solution)/shard_map/ppermute | solution.py:439
  1628.4 21.0 %collective-permute-done.71 = bf16[1,512,1024]{2,1,0:T(8,128)(2,1)} collective-permute-done((bf16[1,512,1024]{2,1,0:T(8,128)(2,1)}, bf16[1,512,1024]{2,1,0:T(8,128)(2,1)}, u32[]{:S(2)}, u32[]{:S(2)}) %collective-permute-start.71) | collective-permute-done | bytes 1048608 | tf_op jit(solution)/shard_map/ppermute | solution.py:439
  1655.0 4.9 multiply_subtract_fusion.1
  1659.9 4.6 pad_maximum_fusion.4
  1703.5 4.7 fusion.106
  1708.2 7.0 fusion.30
  1715.2 6.8 fusion.32
  1722.0 18.3 bitcast_add_fusion
  1743.3 7.1 add_convert_fusion
  1757.0 12.0 all-gather.2
  1776.5 8.5 fusion.8
  1785.0 14.5 fusion.6
  1799.5 42.6 %reduce-scatter.5.cloned.1.call-done = bf16[1,2,48,1024]{3,2,1,0:T(8,128)(2,1)} async-done(((bf16[16,2,48,1024]{3,2,1,0:T(8,128)(2,1)}), bf16[1,2,48,1024]{3,2,1,0:T(8,128)(2,1)}) %reduce-scatter.5.cloned.1.call-update) | async-done | bytes 196624 | tf_op jit(solution)/shard_map/reduce_scatter | solution.py:812
  1842.2 14.0 all-gather.1
  1858.3 30.0 %all-gather.16.cloned.1.call-done = bf16[4,384,2048]{2,1,0:T(8,128)(2,1)} async-done(((bf16[4,48,2048]{2,1,0:T(8,128)(2,1)}), bf16[4,384,2048]{2,1,0:T(8,128)(2,1)}) %all-gather.16.cloned.1.call-update) | async-done | bytes 6291472 | tf_op jit(solution)/shard_map/all_gather | solution.py:624
  (687 shorter events, 418.5 us)
Async XLA Ops:
  7.2 235.0 %all-gather.20.cloned.1.call-start = ((), (), s32[]{:S(2)}) async-start(), calls=%async_computation.13 | async-start | bytes 4456448 | tf_op jit(solution)/shard_map/all_gather | solution.py:499
  13.9 536.4 %all-gather.10.cloned.1.call-start = ((), (), s32[]{:S(2)}) async-start(), calls=%async_computation.4 | async-start | bytes 4456448 | tf_op jit(solution)/shard_map/all_gather | solution.py:647
  51.7 29.0 %collective-permute-start.4 = (bf16[128,1024]{1,0:T(8,128)(2,1)S(1)}, bf16[128,1024]{1,0:T(8,128)(2,1)S(1)}, u32[]{:S(2)}, u32[]{:S(2)}) collective-permute-start(bf16[128,1024]{1,0:T(8,128)(2,1)S(1)} %constant_dynamic-slice_fusion.6), channel_id=1, source_target_pairs={{0,16},{8,24},{16,0},{24,8},{1,17},{9,25},{17,1},{25,9},{2,18},{10... | collective-permute-start | bytes 786440 | tf_op jit(solution)/shard_map/ppermute | solution.py:426
  53.3 27.5 %collective-permute-start.3 = (bf16[128,1024]{1,0:T(8,128)(2,1)S(1)}, bf16[128,1024]{1,0:T(8,128)(2,1)S(1)}, u32[]{:S(2)}, u32[]{:S(2)}) collective-permute-start(bf16[128,1024]{1,0:T(8,128)(2,1)S(1)} %constant_dynamic-slice_fusion.6), channel_id=1, source_target_pairs={{0,24},{8,0},{16,8},{24,16},{1,25},{9,1},{17,9},{25,17},{2,26},{10... | collective-permute-start | bytes 786440 | tf_op jit(solution)/shard_map/ppermute | solution.py:426
  54.2 76.0 %collective-permute-start.20 = (bf16[1,2,128,1024]{3,2,1,0:T(8,128)(2,1)S(1)}, bf16[1,2,128,1024]{3,2,1,0:T(8,128)(2,1)S(1)}, u32[]{:S(2)}, u32[]{:S(2)}) collective-permute-start(bf16[1,2,128,1024]{3,2,1,0:T(8,128)(2,1)S(1)} %maximum_bitcast_fusion.4), channel_id=1, source_target_pairs={{0,2},{2,0},{4,6},{6,4},{1,3},{3,1},{5,7},{7,5},{8,10},{10,8},{12,... | collective-permute-start | bytes 1572872 | tf_op jit(solution)/shard_map/ppermute | solution.py:439
  58.2 69.3 %collective-permute-start.22 = (bf16[1,2,128,1024]{3,2,1,0:T(8,128)(2,1)}, bf16[1,2,128,1024]{3,2,1,0:T(8,128)(2,1)S(1)}, u32[]{:S(2)}, u32[]{:S(2)}) collective-permute-start(bf16[1,2,128,1024]{3,2,1,0:T(8,128)(2,1)} %maximum_bitcast_fusion.5), channel_id=1, source_target_pairs={{0,4},{2,6},{4,0},{6,2},{1,5},{3,7},{5,1},{7,3},{8,12},{10,14},{12... | collective-permute-start | bytes 1572872 | tf_op jit(solution)/shard_map/ppermute | solution.py:439
  87.8 31.4 %collective-permute-start.7 = (bf16[128,1024]{1,0:T(8,128)(2,1)S(1)}, bf16[128,1024]{1,0:T(8,128)(2,1)S(1)}, u32[]{:S(2)}, u32[]{:S(2)}) collective-permute-start(bf16[128,1024]{1,0:T(8,128)(2,1)S(1)} %constant_dynamic-slice_fusion.5), channel_id=1, source_target_pairs={{0,16},{8,24},{16,0},{24,8},{1,17},{9,25},{17,1},{25,9},{2,18},{10... | collective-permute-start | bytes 786440 | tf_op jit(solution)/shard_map/ppermute | solution.py:426
  90.3 30.8 %collective-permute-start.6 = (bf16[128,1024]{1,0:T(8,128)(2,1)S(1)}, bf16[128,1024]{1,0:T(8,128)(2,1)S(1)}, u32[]{:S(2)}, u32[]{:S(2)}) collective-permute-start(bf16[128,1024]{1,0:T(8,128)(2,1)S(1)} %constant_dynamic-slice_fusion.5), channel_id=1, source_target_pairs={{0,24},{8,0},{16,8},{24,16},{1,25},{9,1},{17,9},{25,17},{2,26},{10... | collective-permute-start | bytes 786440 | tf_op jit(solution)/shard_map/ppermute | solution.py:426
  100.4 37.5 %collective-permute-start.27 = (bf16[1,2,128,1024]{3,2,1,0:T(8,128)(2,1)}, bf16[1,2,128,1024]{3,2,1,0:T(8,128)(2,1)}, u32[]{:S(2)}, u32[]{:S(2)}) collective-permute-start(bf16[1,2,128,1024]{3,2,1,0:T(8,128)(2,1)} %maximum_bitcast_fusion.6), channel_id=1, source_target_pairs={{0,2},{2,0},{4,6},{6,4},{1,3},{3,1},{5,7},{7,5},{8,10},{10,8},{12,... | collective-permute-start | bytes 1572872 | tf_op jit(solution)/shard_map/ppermute | solution.py:439
  124.7 486.5 %all-gather.14.cloned.1.call-start = ((), (), s32[]{:S(2)}) async-start(), calls=%async_computation.6 | async-start | bytes 1966080 | tf_op jit(solution)/shard_map/all_gather | solution.py:616
  130.2 50.7 %collective-permute-start.23 = (bf16[2,2,128,1024]{3,2,1,0:T(8,128)(2,1)S(1)}, bf16[2,2,128,1024]{3,2,1,0:T(8,128)(2,1)S(1)}, u32[]{:S(2)}, u32[]{:S(2)}) collective-permute-start(bf16[2,2,128,1024]{3,2,1,0:T(8,128)(2,1)S(1)} %pad_maximum_fusion.18), channel_id=1, source_target_pairs={{0,2},{2,0},{4,6},{6,4},{1,3},{3,1},{5,7},{7,5},{8,10},{10,8},{12,... | collective-permute-start | bytes 3145736 | tf_op jit(solution)/shard_map/ppermute | solution.py:439
  134.2 42.1 %collective-permute-start.21 = (bf16[2,2,128,1024]{3,2,1,0:T(8,128)(2,1)S(1)}, bf16[2,2,128,1024]{3,2,1,0:T(8,128)(2,1)S(1)}, u32[]{:S(2)}, u32[]{:S(2)}) collective-permute-start(bf16[2,2,128,1024]{3,2,1,0:T(8,128)(2,1)S(1)} %pad_maximum_fusion.17), channel_id=1, source_target_pairs={{0,4},{2,6},{4,0},{6,2},{1,5},{3,7},{5,1},{7,3},{8,12},{10,14},{12... | collective-permute-start | bytes 3145736 | tf_op jit(solution)/shard_map/ppermute | solution.py:439
  137.8 66.3 %collective-permute-start.30 = (bf16[2,2,128,1024]{3,2,1,0:T(8,128)(2,1)}, bf16[2,2,128,1024]{3,2,1,0:T(8,128)(2,1)}, u32[]{:S(2)}, u32[]{:S(2)}) collective-permute-start(bf16[2,2,128,1024]{3,2,1,0:T(8,128)(2,1)} %pad_maximum_fusion.20), channel_id=1, source_target_pairs={{0,2},{2,0},{4,6},{6,4},{1,3},{3,1},{5,7},{7,5},{8,10},{10,8},{12,... | collective-permute-start | bytes 3145736 | tf_op jit(solution)/shard_map/ppermute | solution.py:439
  145.5 53.5 %collective-permute-start.28 = (bf16[2,2,128,1024]{3,2,1,0:T(8,128)(2,1)}, bf16[2,2,128,1024]{3,2,1,0:T(8,128)(2,1)}, u32[]{:S(2)}, u32[]{:S(2)}) collective-permute-start(bf16[2,2,128,1024]{3,2,1,0:T(8,128)(2,1)} %pad_maximum_fusion.19), channel_id=1, source_target_pairs={{0,4},{2,6},{4,0},{6,2},{1,5},{3,7},{5,1},{7,3},{8,12},{10,14},{12... | collective-permute-start | bytes 3145736 | tf_op jit(solution)/shard_map/ppermute | solution.py:439
  148.0 77.5 %collective-permute-start.12 = (bf16[2,2,128,1024]{3,2,1,0:T(8,128)(2,1)}, bf16[2,2,128,1024]{3,2,1,0:T(8,128)(2,1)S(1)}, u32[]{:S(2)}, u32[]{:S(2)}) collective-permute-start(bf16[2,2,128,1024]{3,2,1,0:T(8,128)(2,1)} %pad_maximum_fusion.16), channel_id=1, source_target_pairs={{0,2},{2,0},{4,6},{6,4},{1,3},{3,1},{5,7},{7,5},{8,10},{10,8},{12,... | collective-permute-start | bytes 3145736 | tf_op jit(solution)/shard_map/ppermute | solution.py:439
  176.4 43.9 %collective-permute-start.10 = (bf16[2,2,128,1024]{3,2,1,0:T(8,128)(2,1)}, bf16[2,2,128,1024]{3,2,1,0:T(8,128)(2,1)}, u32[]{:S(2)}, u32[]{:S(2)}) collective-permute-start(bf16[2,2,128,1024]{3,2,1,0:T(8,128)(2,1)} %pad_maximum_fusion.15), channel_id=1, source_target_pairs={{0,4},{2,6},{4,0},{6,2},{1,5},{3,7},{5,1},{7,3},{8,12},{10,14},{12... | collective-permute-start | bytes 3145736 | tf_op jit(solution)/shard_map/ppermute | solution.py:439
  293.6 41.4 %collective-permute-start.25 = (bf16[1,512,1024]{2,1,0:T(8,128)(2,1)}, bf16[1,512,1024]{2,1,0:T(8,128)(2,1)}, u32[]{:S(2)}, u32[]{:S(2)}) collective-permute-start(bf16[1,512,1024]{2,1,0:T(8,128)(2,1)} %stack.265), channel_id=1, source_target_pairs={{0,2},{2,0},{4,6},{6,4},{1,3},{3,1},{5,7},{7,5},{8,10},{10,8},{12,... | collective-permute-start | bytes 3145736 | tf_op jit(solution)/shard_map/ppermute | solution.py:439
  308.6 154.7 %collective-permute-start.32 = (bf16[2,512,1024]{2,1,0:T(8,128)(2,1)}, bf16[2,512,1024]{2,1,0:T(8,128)(2,1)}, u32[]{:S(2)}, u32[]{:S(2)}) collective-permute-start(bf16[2,512,1024]{2,1,0:T(8,128)(2,1)} %pad_maximum_fusion.9), channel_id=1, source_target_pairs={{0,2},{2,0},{4,6},{6,4},{1,3},{3,1},{5,7},{7,5},{8,10},{10,8},{12,... | collective-permute-start | bytes 6291464 | tf_op jit(solution)/shard_map/ppermute | solution.py:439
  313.6 30.0 %collective-permute-start.19 = (bf16[96,512]{1,0:T(8,128)(2,1)}, bf16[96,512]{1,0:T(8,128)(2,1)S(1)}, u32[]{:S(2)}, u32[]{:S(2)}) collective-permute-start(bf16[96,512]{1,0:T(8,128)(2,1)} %get-tuple-element.308), channel_id=1, source_target_pairs={{0,8},{8,16},{16,24},{24,0},{1,9},{9,17},{17,25},{25,1},{2,10},{10... | collective-permute-start | bytes 294920 | tf_op jit(solution)/shard_map/ppermute | solution.py:426
  337.8 136.1 %collective-permute-start.26 = (bf16[2,512,1024]{2,1,0:T(8,128)(2,1)}, bf16[2,512,1024]{2,1,0:T(8,128)(2,1)}, u32[]{:S(2)}, u32[]{:S(2)}) collective-permute-start(bf16[2,512,1024]{2,1,0:T(8,128)(2,1)} %pad_maximum_fusion.8), channel_id=1, source_target_pairs={{0,4},{2,6},{4,0},{6,2},{1,5},{3,7},{5,1},{7,3},{8,12},{10,14},{12... | collective-permute-start | bytes 6291464 | tf_op jit(solution)/shard_map/ppermute | solution.py:439
  346.6 102.7 %collective-permute-start.15 = (bf16[48,2048]{1,0:T(8,128)(2,1)S(1)}, bf16[48,2048]{1,0:T(8,128)(2,1)}, u32[]{:S(2)}, u32[]{:S(2)}) collective-permute-start(bf16[48,2048]{1,0:T(8,128)(2,1)S(1)} %get-tuple-element.275), channel_id=1, source_target_pairs={{0,16},{8,24},{16,0},{24,8},{1,17},{9,25},{17,1},{25,9},{2,18},{10... | collective-permute-start | bytes 589832 | tf_op jit(solution)/shard_map/ppermute | solution.py:426
  346.6 102.7 %collective-permute-start.14 = (bf16[48,2048]{1,0:T(8,128)(2,1)S(1)}, bf16[48,2048]{1,0:T(8,128)(2,1)}, u32[]{:S(2)}, u32[]{:S(2)}) collective-permute-start(bf16[48,2048]{1,0:T(8,128)(2,1)S(1)} %get-tuple-element.276), channel_id=1, source_target_pairs={{0,24},{8,0},{16,8},{24,16},{1,25},{9,1},{17,9},{25,17},{2,26},{10... | collective-permute-start | bytes 589832 | tf_op jit(solution)/shard_map/ppermute | solution.py:426
  353.4 176.9 %collective-permute-start.35 = (bf16[1024,1024]{1,0:T(8,128)(2,1)}, bf16[1024,1024]{1,0:T(8,128)(2,1)}, u32[]{:S(2)}, u32[]{:S(2)}) collective-permute-start(bf16[1024,1024]{1,0:T(8,128)(2,1)} %constant_dynamic-slice_fusion.4), channel_id=1, source_target_pairs={{0,8},{8,16},{16,24},{24,0},{1,9},{9,17},{17,25},{25,1},{2,10},{10... | collective-permute-start | bytes 6291464 | tf_op jit(solution)/shard_map/ppermute | solution.py:426
  449.3 81.0 %collective-permute-start.34 = (bf16[1024,1024]{1,0:T(8,128)(2,1)}, bf16[1024,1024]{1,0:T(8,128)(2,1)}, u32[]{:S(2)}, u32[]{:S(2)}) collective-permute-start(bf16[1024,1024]{1,0:T(8,128)(2,1)} %constant_dynamic-slice_fusion.4), channel_id=1, source_target_pairs={{0,16},{8,24},{16,0},{24,8},{1,17},{9,25},{17,1},{25,9},{2,18},{10... | collective-permute-start | bytes 6291464 | tf_op jit(solution)/shard_map/ppermute | solution.py:426
  449.3 94.0 %collective-permute-start.33 = (bf16[1024,1024]{1,0:T(8,128)(2,1)}, bf16[1024,1024]{1,0:T(8,128)(2,1)}, u32[]{:S(2)}, u32[]{:S(2)}) collective-permute-start(bf16[1024,1024]{1,0:T(8,128)(2,1)} %constant_dynamic-slice_fusion.4), channel_id=1, source_target_pairs={{0,24},{8,0},{16,8},{24,16},{1,25},{9,1},{17,9},{25,17},{2,26},{10... | collective-permute-start | bytes 6291464 | tf_op jit(solution)/shard_map/ppermute | solution.py:426
  463.2 148.0 %all-gather.12.cloned.1.call-start = ((), (), s32[]{:S(2)}) async-start(), calls=%async_computation.5 | async-start | bytes 7077888 | tf_op jit(solution)/shard_map/all_gather | solution.py:616
  560.6 865.8 %reduce-scatter.11.cloned.1.call-start = ((), (), s32[]{:S(2)}) async-start(), calls=%async_computation.11 | async-start | bytes 1966080 | tf_op jit(solution)/shard_map/reduce_scatter | solution.py:622
  597.0 112.6 %collective-permute-start.40 = (bf16[1024,1024]{1,0:T(8,128)(2,1)}, bf16[1024,1024]{1,0:T(8,128)(2,1)S(1)}, u32[]{:S(2)}, u32[]{:S(2)}) collective-permute-start(bf16[1024,1024]{1,0:T(8,128)(2,1)} %constant_dynamic-slice_fusion), channel_id=1, source_target_pairs={{0,24},{8,0},{16,8},{24,16},{1,25},{9,1},{17,9},{25,17},{2,26},{10... | collective-permute-start | bytes 6291464 | tf_op jit(solution)/shard_map/ppermute | solution.py:426
  719.8 147.6 %collective-permute-start.45 = (bf16[1024,1024]{1,0:T(8,128)(2,1)}, bf16[1024,1024]{1,0:T(8,128)(2,1)S(1)}, u32[]{:S(2)}, u32[]{:S(2)}) collective-permute-start(bf16[1024,1024]{1,0:T(8,128)(2,1)} %constant_dynamic-slice_fusion), channel_id=1, source_target_pairs={{0,16},{8,24},{16,0},{24,8},{1,17},{9,25},{17,1},{25,9},{2,18},{10... | collective-permute-start | bytes 6291464 | tf_op jit(solution)/shard_map/ppermute | solution.py:426
  719.8 57.0 %collective-permute-start.44 = (f32[4,1024]{0,1:T(8,128)S(1)}, f32[4,1024]{0,1:T(8,128)S(1)}, u32[]{:S(2)}, u32[]{:S(2)}) collective-permute-start(f32[4,1024]{0,1:T(8,128)S(1)} %copy-done.82), channel_id=1, source_target_pairs={{0,24},{8,0},{16,8},{24,16},{1,25},{9,1},{17,9},{25,17},{2,26},{10... | collective-permute-start | bytes 49160 | tf_op jit(solution)/shard_map/ppermute | solution.py:426
  867.9 55.5 %collective-permute-start.48 = (bf16[1024,1024]{1,0:T(8,128)(2,1)}, bf16[1024,1024]{1,0:T(8,128)(2,1)}, u32[]{:S(2)}, u32[]{:S(2)}) collective-permute-start(bf16[1024,1024]{1,0:T(8,128)(2,1)} %collective-permute-done.34.cot0_ref), channel_id=1, source_target_pairs={{0,1},{1,0},{2,3},{3,2},{4,5},{5,4},{6,7},{7,6},{8,9},{9,8},{10,11... | collective-permute-start | bytes 6291464 | tf_op jit(solution)/shard_map/ppermute | solution.py:436
  877.0 205.4 %collective-permute-start.50 = (bf16[1024,1024]{1,0:T(8,128)(2,1)}, bf16[1024,1024]{1,0:T(8,128)(2,1)S(1)}, u32[]{:S(2)}, u32[]{:S(2)}) collective-permute-start(bf16[1024,1024]{1,0:T(8,128)(2,1)} %constant_dynamic-slice_fusion), channel_id=1, source_target_pairs={{0,8},{8,16},{16,24},{24,0},{1,9},{9,17},{17,25},{25,1},{2,10},{10... | collective-permute-start | bytes 6291464 | tf_op jit(solution)/shard_map/ppermute | solution.py:426
  923.4 56.7 %collective-permute-start.49 = (f32[4,1024]{0,1:T(8,128)S(1)}, f32[4,1024]{0,1:T(8,128)S(1)}, u32[]{:S(2)}, u32[]{:S(2)}) collective-permute-start(f32[4,1024]{0,1:T(8,128)S(1)} %copy-done.81), channel_id=1, source_target_pairs={{0,16},{8,24},{16,0},{24,8},{1,17},{9,25},{17,1},{25,9},{2,18},{10... | collective-permute-start | bytes 49160 | tf_op jit(solution)/shard_map/ppermute | solution.py:426
  1071.8 60.2 %collective-permute-start.53 = (bf16[1024,1024]{1,0:T(8,128)(2,1)}, bf16[1024,1024]{1,0:T(8,128)(2,1)S(1)}, u32[]{:S(2)}, u32[]{:S(2)}) collective-permute-start(bf16[1024,1024]{1,0:T(8,128)(2,1)} %add_convert_fusion.7), channel_id=1, source_target_pairs={{0,8},{8,16},{16,24},{24,0},{1,9},{9,17},{17,25},{25,1},{2,10},{10... | collective-permute-start | bytes 6291464 | tf_op jit(solution)/shard_map/ppermute | solution.py:431
  1082.4 49.5 %collective-permute-start.51 = (bf16[1024,1024]{1,0:T(8,128)(2,1)S(1)}, bf16[1024,1024]{1,0:T(8,128)(2,1)S(1)}, u32[]{:S(2)}, u32[]{:S(2)}) collective-permute-start(bf16[1024,1024]{1,0:T(8,128)(2,1)S(1)} %collective-permute-done.50.h0_ref), channel_id=1, source_target_pairs={{0,1},{1,0},{2,3},{3,2},{4,5},{5,4},{6,7},{7,6},{8,9},{9,8},{10,11... | collective-permute-start | bytes 6291464 | tf_op jit(solution)/shard_map/ppermute | solution.py:436
  1082.6 51.3 %collective-permute-start.55 = (bf16[1024,1024]{1,0:T(8,128)(2,1)}, bf16[1024,1024]{1,0:T(8,128)(2,1)}, u32[]{:S(2)}, u32[]{:S(2)}) collective-permute-start(bf16[1024,1024]{1,0:T(8,128)(2,1)} %collective-permute-done.35.cot0_ref), channel_id=1, source_target_pairs={{0,1},{1,0},{2,3},{3,2},{4,5},{5,4},{6,7},{7,6},{8,9},{9,8},{10,11... | collective-permute-start | bytes 6291464 | tf_op jit(solution)/shard_map/ppermute | solution.py:436
  1082.9 60.0 %collective-permute-start.56 = (f32[4,1024]{0,1:T(8,128)S(1)}, f32[4,1024]{0,1:T(8,128)S(1)}, u32[]{:S(2)}, u32[]{:S(2)}) collective-permute-start(f32[4,1024]{0,1:T(8,128)S(1)} %copy-done.80), channel_id=1, source_target_pairs={{0,8},{8,16},{16,24},{24,0},{1,9},{9,17},{17,25},{25,1},{2,10},{10... | collective-permute-start | bytes 49160 | tf_op jit(solution)/shard_map/ppermute | solution.py:426
  1237.5 461.3 %reduce-scatter.9.cloned.1.call-start = ((), (), s32[]{:S(2)}) async-start(), calls=%async_computation.9 | async-start | bytes 7077888 | tf_op jit(solution)/shard_map/reduce_scatter | solution.py:622
  1238.1 28.9 %collective-permute-start.62 = (bf16[1024,1024]{1,0:T(8,128)(2,1)}, bf16[1024,1024]{1,0:T(8,128)(2,1)}, u32[]{:S(2)}, u32[]{:S(2)}) collective-permute-start(bf16[1024,1024]{1,0:T(8,128)(2,1)} %get-tuple-element.178), channel_id=1, source_target_pairs={{0,1},{1,0},{2,3},{3,2},{4,5},{5,4},{6,7},{7,6},{8,9},{9,8},{10,11... | collective-permute-start | bytes 6291464 | tf_op jit(solution)/shard_map/ppermute | solution.py:436
  1238.2 94.4 %collective-permute-start.54 = (bf16[1024,1024]{1,0:T(8,128)(2,1)}, bf16[1024,1024]{1,0:T(8,128)(2,1)}, u32[]{:S(2)}, u32[]{:S(2)}) collective-permute-start(bf16[1024,1024]{1,0:T(8,128)(2,1)} %add_convert_fusion.6), channel_id=1, source_target_pairs={{0,16},{8,24},{16,0},{24,8},{1,17},{9,25},{17,1},{25,9},{2,18},{10... | collective-permute-start | bytes 6291464 | tf_op jit(solution)/shard_map/ppermute | solution.py:431
  1242.3 106.0 %collective-permute-start.58 = (bf16[1024,1024]{1,0:T(8,128)(2,1)}, bf16[1024,1024]{1,0:T(8,128)(2,1)}, u32[]{:S(2)}, u32[]{:S(2)}) collective-permute-start(bf16[1024,1024]{1,0:T(8,128)(2,1)} %add_convert_fusion.5), channel_id=1, source_target_pairs={{0,24},{8,0},{16,8},{24,16},{1,25},{9,1},{17,9},{25,17},{2,26},{10... | collective-permute-start | bytes 6291464 | tf_op jit(solution)/shard_map/ppermute | solution.py:431
  1249.4 103.7 %collective-permute-start.64 = (f32[4,1024]{0,1:T(8,128)}, f32[4,1024]{0,1:T(8,128)}, u32[]{:S(2)}, u32[]{:S(2)}) collective-permute-start(f32[4,1024]{0,1:T(8,128)} %bitcast.126), channel_id=1, source_target_pairs={{0,8},{8,16},{16,24},{24,0},{1,9},{9,17},{17,25},{25,1},{2,10},{10... | collective-permute-start | bytes 49160 | tf_op jit(solution)/shard_map/ppermute | solution.py:431
  1260.6 490.5 %all-gather.18.cloned.1.call-start = ((), (), s32[]{:S(2)}) async-start(), calls=%async_computation.12 | async-start | bytes 1966080 | tf_op jit(solution)/shard_map/all_gather | solution.py:624
  1261.1 149.8 %collective-permute-start.65 = (f32[4,1024]{0,1:T(8,128)}, f32[4,1024]{0,1:T(8,128)}, u32[]{:S(2)}, u32[]{:S(2)}) collective-permute-start(f32[4,1024]{0,1:T(8,128)} %bitcast.128), channel_id=1, source_target_pairs={{0,16},{8,24},{16,0},{24,8},{1,17},{9,25},{17,1},{25,9},{2,18},{10... | collective-permute-start | bytes 49160 | tf_op jit(solution)/shard_map/ppermute | solution.py:431
  1267.0 145.2 %collective-permute-start.66 = (f32[4,1024]{0,1:T(8,128)}, f32[4,1024]{0,1:T(8,128)}, u32[]{:S(2)}, u32[]{:S(2)}) collective-permute-start(f32[4,1024]{0,1:T(8,128)} %bitcast.130), channel_id=1, source_target_pairs={{0,24},{8,0},{16,8},{24,16},{1,25},{9,1},{17,9},{25,17},{2,26},{10... | collective-permute-start | bytes 49160 | tf_op jit(solution)/shard_map/ppermute | solution.py:431
  1352.1 91.9 %collective-permute-start.63 = (bf16[1024,1024]{1,0:T(8,128)(2,1)S(1)}, bf16[1024,1024]{1,0:T(8,128)(2,1)}, u32[]{:S(2)}, u32[]{:S(2)}) collective-permute-start(bf16[1024,1024]{1,0:T(8,128)(2,1)S(1)} %add_convert_fusion.4), channel_id=1, source_target_pairs={{0,1},{1,0},{2,3},{3,2},{4,5},{5,4},{6,7},{7,6},{8,9},{9,8},{10,11... | collective-permute-start | bytes 6291464 | tf_op jit(solution)/shard_map/ppermute | solution.py:436
  1428.1 127.2 %collective-permute-start.85 = (bf16[96,512]{1,0:T(8,128)(2,1)}, bf16[96,512]{1,0:T(8,128)(2,1)}, u32[]{:S(2)}, u32[]{:S(2)}) collective-permute-start(bf16[96,512]{1,0:T(8,128)(2,1)} %get-tuple-element.326), channel_id=1, source_target_pairs={{0,24},{8,0},{16,8},{24,16},{1,25},{9,1},{17,9},{25,17},{2,26},{10... | collective-permute-start | bytes 294920 | tf_op jit(solution)/shard_map/ppermute | solution.py:431
  1440.5 115.4 %collective-permute-start.84 = (bf16[96,512]{1,0:T(8,128)(2,1)}, bf16[96,512]{1,0:T(8,128)(2,1)}, u32[]{:S(2)}, u32[]{:S(2)}) collective-permute-start(bf16[96,512]{1,0:T(8,128)(2,1)} %get-tuple-element.327), channel_id=1, source_target_pairs={{0,16},{8,24},{16,0},{24,8},{1,17},{9,25},{17,1},{25,9},{2,18},{10... | collective-permute-start | bytes 294920 | tf_op jit(solution)/shard_map/ppermute | solution.py:431
  1440.5 115.4 %collective-permute-start.83 = (bf16[96,512]{1,0:T(8,128)(2,1)}, bf16[96,512]{1,0:T(8,128)(2,1)}, u32[]{:S(2)}, u32[]{:S(2)}) collective-permute-start(bf16[96,512]{1,0:T(8,128)(2,1)} %get-tuple-element.328), channel_id=1, source_target_pairs={{0,8},{8,16},{16,24},{24,0},{1,9},{9,17},{17,25},{25,1},{2,10},{10... | collective-permute-start | bytes 294920 | tf_op jit(solution)/shard_map/ppermute | solution.py:431
  1441.2 124.0 %collective-permute-start.68 = (bf16[1024,1024]{1,0:T(8,128)(2,1)}, bf16[1024,1024]{1,0:T(8,128)(2,1)}, u32[]{:S(2)}, u32[]{:S(2)}) collective-permute-start(bf16[1024,1024]{1,0:T(8,128)(2,1)} %add_convert_fusion.3), channel_id=1, source_target_pairs={{0,8},{8,16},{16,24},{24,0},{1,9},{9,17},{17,25},{25,1},{2,10},{10... | collective-permute-start | bytes 6291464 | tf_op jit(solution)/shard_map/ppermute | solution.py:431
  1444.0 121.1 %collective-permute-start.69 = (bf16[1024,1024]{1,0:T(8,128)(2,1)}, bf16[1024,1024]{1,0:T(8,128)(2,1)}, u32[]{:S(2)}, u32[]{:S(2)}) collective-permute-start(bf16[1024,1024]{1,0:T(8,128)(2,1)} %add_convert_fusion.1), channel_id=1, source_target_pairs={{0,24},{8,0},{16,8},{24,16},{1,25},{9,1},{17,9},{25,17},{2,26},{10... | collective-permute-start | bytes 6291464 | tf_op jit(solution)/shard_map/ppermute | solution.py:431
  1555.3 59.5 %collective-permute-start.70 = (bf16[2,512,1024]{2,1,0:T(8,128)(2,1)}, bf16[2,512,1024]{2,1,0:T(8,128)(2,1)}, u32[]{:S(2)}, u32[]{:S(2)}) collective-permute-start(bf16[2,512,1024]{2,1,0:T(8,128)(2,1)} %pad_maximum_fusion.10), channel_id=1, source_target_pairs={{0,2},{2,0},{4,6},{6,4},{1,3},{3,1},{5,7},{7,5},{8,10},{10,8},{12,... | collective-permute-start | bytes 6291464 | tf_op jit(solution)/shard_map/ppermute | solution.py:439
  1558.6 198.5 %reduce-scatter.7.cloned.1.call-start = ((), (), s32[]{:S(2)}) async-start(), calls=%async_computation.8 | async-start | bytes 2228224 | tf_op jit(solution)/shard_map/reduce_scatter | solution.py:812
  1562.0 61.5 %collective-permute-start.73 = (bf16[2,512,1024]{2,1,0:T(8,128)(2,1)}, bf16[2,512,1024]{2,1,0:T(8,128)(2,1)}, u32[]{:S(2)}, u32[]{:S(2)}) collective-permute-start(bf16[2,512,1024]{2,1,0:T(8,128)(2,1)} %pad_maximum_fusion.11), channel_id=1, source_target_pairs={{0,4},{2,6},{4,0},{6,2},{1,5},{3,7},{5,1},{7,3},{8,12},{10,14},{12... | collective-permute-start | bytes 6291464 | tf_op jit(solution)/shard_map/ppermute | solution.py:439
  1564.7 55.1 %collective-permute-start.79 = (f32[8,32,1024]{2,1,0:T(8,128)S(1)}, f32[8,32,1024]{2,1,0:T(8,128)S(1)}, u32[]{:S(2)}, u32[]{:S(2)}) collective-permute-start(f32[8,32,1024]{2,1,0:T(8,128)S(1)} %multiply_reduce_fusion.5), channel_id=1, source_target_pairs={{0,1},{1,0},{2,3},{3,2},{4,5},{5,4},{6,7},{7,6},{8,9},{9,8},{10,11... | collective-permute-start | bytes 3145736 | tf_op jit(solution)/shard_map/ppermute | solution.py:436
  1568.0 111.8 %collective-permute-start.75 = (bf16[1024,1024]{1,0:T(8,128)(2,1)}, bf16[1024,1024]{1,0:T(8,128)(2,1)}, u32[]{:S(2)}, u32[]{:S(2)}) collective-permute-start(bf16[1024,1024]{1,0:T(8,128)(2,1)} %add_convert_fusion.2), channel_id=1, source_target_pairs={{0,16},{8,24},{16,0},{24,8},{1,17},{9,25},{17,1},{25,9},{2,18},{10... | collective-permute-start | bytes 6291464 | tf_op jit(solution)/shard_map/ppermute | solution.py:431
  1617.7 31.8 %collective-permute-start.71 = (bf16[1,512,1024]{2,1,0:T(8,128)(2,1)}, bf16[1,512,1024]{2,1,0:T(8,128)(2,1)}, u32[]{:S(2)}, u32[]{:S(2)}) collective-permute-start(bf16[1,512,1024]{2,1,0:T(8,128)(2,1)} %fusion.51), channel_id=1, source_target_pairs={{0,4},{2,6},{4,0},{6,2},{1,5},{3,7},{5,1},{7,3},{8,12},{10,14},{12... | collective-permute-start | bytes 3145736 | tf_op jit(solution)/shard_map/ppermute | solution.py:439
  1623.0 219.2 %reduce-scatter.5.cloned.1.call-start = ((), (), s32[]{:S(2)}) async-start(), calls=%async_computation.7 | async-start | bytes 3342336 | tf_op jit(solution)/shard_map/reduce_scatter | solution.py:812
  1626.5 46.6 %collective-permute-start.74 = (bf16[1,512,1024]{2,1,0:T(8,128)(2,1)}, bf16[1,512,1024]{2,1,0:T(8,128)(2,1)}, u32[]{:S(2)}, u32[]{:S(2)}) collective-permute-start(bf16[1,512,1024]{2,1,0:T(8,128)(2,1)} %fusion.52), channel_id=1, source_target_pairs={{0,2},{2,0},{4,6},{6,4},{1,3},{3,1},{5,7},{7,5},{8,10},{10,8},{12,... | collective-permute-start | bytes 3145736 | tf_op jit(solution)/shard_map/ppermute | solution.py:439
  1698.7 189.5 %all-gather.16.cloned.1.call-start = ((), (), s32[]{:S(2)}) async-start(), calls=%async_computation.10 | async-start | bytes 7077888 | tf_op jit(solution)/shard_map/all_gather | solution.py:624
  1701.0 39.3 %collective-permute-start.82 = (bf16[48,2048]{1,0:T(8,128)(2,1)}, bf16[48,2048]{1,0:T(8,128)(2,1)}, u32[]{:S(2)}, u32[]{:S(2)}) collective-permute-start(bf16[48,2048]{1,0:T(8,128)(2,1)} %get-tuple-element.316), channel_id=1, source_target_pairs={{0,24},{8,0},{16,8},{24,16},{1,25},{9,1},{17,9},{25,17},{2,26},{10... | collective-permute-start | bytes 589832 | tf_op jit(solution)/shard_map/ppermute | solution.py:431
  1701.0 39.3 %collective-permute-start.81 = (bf16[48,2048]{1,0:T(8,128)(2,1)}, bf16[48,2048]{1,0:T(8,128)(2,1)}, u32[]{:S(2)}, u32[]{:S(2)}) collective-permute-start(bf16[48,2048]{1,0:T(8,128)(2,1)} %get-tuple-element.317), channel_id=1, source_target_pairs={{0,16},{8,24},{16,0},{24,8},{1,17},{9,25},{17,1},{25,9},{2,18},{10... | collective-permute-start | bytes 589832 | tf_op jit(solution)/shard_map/ppermute | solution.py:431
  1702.6 37.7 %collective-permute-start.80 = (bf16[48,2048]{1,0:T(8,128)(2,1)S(1)}, bf16[48,2048]{1,0:T(8,128)(2,1)}, u32[]{:S(2)}, u32[]{:S(2)}) collective-permute-start(bf16[48,2048]{1,0:T(8,128)(2,1)S(1)} %get-tuple-element.318), channel_id=1, source_target_pairs={{0,8},{8,16},{16,24},{24,0},{1,9},{9,17},{17,25},{25,1},{2,10},{10... | collective-permute-start | bytes 589832 | tf_op jit(solution)/shard_map/ppermute | solution.py:431
  1740.3 36.2 %collective-permute-start.77 = (f32[1024,2048]{1,0:T(8,128)}, f32[1024,2048]{1,0:T(8,128)}, u32[]{:S(2)}, u32[]{:S(2)}) collective-permute-start(f32[1024,2048]{1,0:T(8,128)} %bitcast_add_fusion), channel_id=1, source_target_pairs={{0,1},{1,0},{2,3},{3,2},{4,5},{5,4},{6,7},{7,6},{8,9},{9,8},{10,11... | collective-permute-start | bytes 25165832 | tf_op jit(solution)/shard_map/ppermute | solution.py:436
  (162 other events, 4533.9 us)
Sparse Core Ops, SparseCore 0:
  14.0 121.7 all-gather.19
  138.5 117.7 all-gather.9
  463.4 33.0 all-gather.13
  560.7 44.7 all-gather.11
  1237.6 30.1 reduce-scatter.10
  1271.1 61.7 reduce-scatter.8
  1558.7 43.2 all-gather.17
  1623.1 83.3 reduce-scatter.6
  1712.1 130.0 reduce-scatter.4
  1843.9 44.2 all-gather.15

commit v3 on v2

--- a/solution.py
+++ b/solution.py
@@ -521,13 +521,16 @@
     first_scale = lax.rsqrt(jnp.mean(token_vals * token_vals, axis=1, keepdims=True) + epsilon)
     h_first = (token_vals * first_scale * gain_in).astype(bf16)
 
-    def exchange(x, bits):
+    def exchange(x, bits, beside=None):
         blocks = {0: x}
         for bit in bits:
             names = sorted(blocks)
-            got = across(jnp.stack([blocks[i] for i in names]), bit)
+            sent = jnp.stack([blocks[i] for i in names])
+            if bit == bits[-1] and beside is not None:
+                sent, beside = lax.optimization_barrier((sent, beside))
+            got = across(sent, bit)
             blocks.update({i ^ bit: got[at] for at, i in enumerate(names)})
-        return [blocks[i] for i in range(slab_count)]
+        return [blocks[i] for i in range(slab_count)], beside
 
     half_n = shard_count // 2
     near_at = jnp.bitwise_xor(jnp.arange(slab_count, dtype=jnp.int32), slab_index)[None, :]
@@ -539,11 +542,10 @@
         mine = my_slab(x, 0)
         return [mine] + [from_shard(mine, s) for s in range(1, shard_count)]
 
-    def spread(got):
-        near = exchange(jnp.stack(got[:half_n]), slab_bits)
-        far = exchange(jnp.stack(got[half_n:]), slab_bits[::-1])
-        rows_ = jnp.concatenate(near + far, axis=0)
-        return jnp.take(rows_, row_at, axis=0).reshape(full_width, local_width)
+    def spread(got, beside=None):
+        near, beside = exchange(jnp.stack(got[:half_n]), slab_bits, beside)
+        far, beside = exchange(jnp.stack(got[half_n:]), slab_bits[::-1], beside)
+        return jnp.concatenate(near + far, axis=0), beside
 
     got_k = fetch(w_qkv[:, 1])
     got_k, w_v, w_q = lax.optimization_barrier((got_k, w_qkv[:, 2], w_qkv[:, 0]))
@@ -553,54 +555,6 @@
     got_q, w_out, cot_mine, gu_a, gu_b, down_a, down_b = lax.optimization_barrier(
         (got_q, w_out, my_part(cotangent), gu_a, gu_b, down_a, down_b)
     )
-    weights = [spread(got_q), spread(got_k), spread(got_v)]
-    mid_qkv = (
-        ADAPTER_SCALE
-        * jnp.einsum("tnd,tjrd->tnjr", tile_rows(h_first), t_qkv_a, preferred_element_type=f32)
-    ).astype(bf16)
-
-    def project(j):
-        return jnp.dot(h_first, weights[j], preferred_element_type=f32) + jnp.einsum(
-            "tnr,tro->tno", mid_qkv[:, :, j], t_qkv_b[:, j], preferred_element_type=f32
-        ).reshape(row_count, local_width)
-
-    def scale_of(raw):
-        squares = sum_parts(jnp.sum(raw * raw, axis=1))
-        return lax.rsqrt(squares / full_width + epsilon)[:, None]
-
-    k_raw = project(1)
-    k_scale = scale_of(k_raw)
-    value_rows = project(2).astype(bf16)
-    q_raw = project(0)
-    q_scale = scale_of(q_raw)
-
-    def heads_of(x):
-        return x.reshape(x.shape[0], local_heads, HEAD_DIM)
-
-    query_rows = (
-        rotate(heads_of(q_raw * q_scale * gain_q), cosine, sine_part)
-        .reshape(row_count, local_width)
-        .astype(bf16)
-    )
-    key_rows = (
-        rotate(heads_of(k_raw * k_scale * gain_k), cosine, sine_part)
-        .reshape(row_count, local_width)
-        .astype(bf16)
-    )
-
-    def exchange_back(x, bits):
-        blocks = {i: x[i * prompt_rows : (i + 1) * prompt_rows] for i in range(slab_count)}
-        for bit in bits:
-            sent = sorted(i for i in blocks if i & bit)
-            got = across(jnp.stack([blocks[i].astype(bf16) for i in sent]), bit)
-            for at, i in enumerate(sent):
-                blocks[i ^ bit] = blocks[i ^ bit].astype(f32) + got[at].astype(f32)
-                del blocks[i]
-        return blocks[0]
-
-    prompt_keys = jnp.concatenate(exchange(key_rows[:prompt_rows], slab_bits), axis=0)
-    prompt_values = jnp.concatenate(exchange(value_rows[:prompt_rows], slab_bits[::-1]), axis=0)
-    key_own, value_own = key_rows[prompt_rows:], value_rows[prompt_rows:]
     def experts_of_sets(x, axes):
         count, width_x = lax.axis_size(axes), x.shape[3]
         x = x.reshape(sets_local, shard_count, -1, width_x).transpose(1, 0, 2, 3)
@@ -616,10 +570,12 @@
         whole = lax.all_gather(x, axes, axis=1, tiled=True)
         return whole.reshape(SETS, -1, x.shape[2])
 
-    def sets_of_experts(x, axes):
-        width_x = x.shape[2]
-        x = x.astype(bf16).reshape(shard_count, -1, width_x)
-        mine = lax.psum_scatter(x, axes, scatter_dimension=1, tiled=True)
+    def scatter_experts(x, axes):
+        x = x.astype(bf16).reshape(shard_count, -1, x.shape[2])
+        return lax.psum_scatter(x, axes, scatter_dimension=1, tiled=True)
+
+    def sets_of_experts(mine, axes):
+        width_x = mine.shape[2]
         got = [to_shard(mine[s], s) if s else mine[s] for s in range(shard_count)]
         whole = lax.all_gather(by_shard(got, shard_index - shard_at), axes, axis=1, tiled=True)
         return whole.reshape(shard_count, sets_local, locals_n, -1, width_x).transpose(1, 0, 2, 3, 4)
@@ -636,14 +592,83 @@
     )
     wide = experts_of_sets(wide, ("ctx", "tp"))
     slim = experts_of_sets(slim, ("ctx",))
-    cot_got = [from_shard(cot_mine, s) for s in range(1, shard_count)]
-    query_rows, wide, slim = lax.optimization_barrier((query_rows, wide, slim))
+    w_gu = w_gate_up.transpose(0, 2, 1, 3)
+    sums = tuple(
+        jnp.zeros((SETS, 3 * RANK * locals_n, x), f32) for x in (full_width, ff_local)
+    )
+    blocks_k, _ = spread(got_k)
+    blocks_v, _ = spread(got_v)
+    blocks_q, (wide, slim, w_gu) = spread(got_q, (wide, slim, w_gu))
+    cot_mine, wide = lax.optimization_barrier((cot_mine, wide))
+    cot_near = from_shard(cot_mine, 1)
+    blocks_q, cot_near, sums = lax.optimization_barrier((blocks_q, cot_near, sums))
+    weights = jnp.take(jnp.stack([blocks_q, blocks_k, blocks_v]), row_at, axis=1).reshape(
+        3, full_width, local_width
+    )
+    cot_mine, cot_near = lax.optimization_barrier((cot_mine, cot_near))
+    cot_last = from_shard(cot_mine, shard_count - 1)
+    cot_rest = [from_shard(cot_mine, s) for s in range(2, shard_count - 1)]
+    mid_qkv = (
+        ADAPTER_SCALE
+        * jnp.einsum("tnd,tjrd->tnjr", tile_rows(h_first), t_qkv_a, preferred_element_type=f32)
+    ).astype(bf16)
+
+    def project(j):
+        return jnp.dot(h_first, weights[j], preferred_element_type=f32) + jnp.einsum(
+            "tnr,tro->tno", mid_qkv[:, :, j], t_qkv_b[:, j], preferred_element_type=f32
+        ).reshape(row_count, local_width)
+
+    def scale_of(raw):
+        squares = sum_parts(jnp.sum(raw * raw, axis=1))
+        return lax.rsqrt(squares / full_width + epsilon)[:, None]
+
+    k_raw = project(1)
+    k_scale = scale_of(k_raw)
+    value_rows = project(2).astype(bf16)
+    q_raw = project(0)
+    q_scale = scale_of(q_raw)
+
+    def heads_of(x):
+        return x.reshape(x.shape[0], local_heads, HEAD_DIM)
+
+    query_rows = (
+        rotate(heads_of(q_raw * q_scale * gain_q), cosine, sine_part)
+        .reshape(row_count, local_width)
+        .astype(bf16)
+    )
+    key_rows = (
+        rotate(heads_of(k_raw * k_scale * gain_k), cosine, sine_part)
+        .reshape(row_count, local_width)
+        .astype(bf16)
+    )
+
+    def exchange_back(x, bits, beside=None):
+        blocks = {i: x[i * prompt_rows : (i + 1) * prompt_rows] for i in range(slab_count)}
+        for bit in bits:
+            sent = sorted(i for i in blocks if i & bit)
+            rows_ = jnp.stack([blocks[i].astype(bf16) for i in sent])
+            if bit == bits[-1] and beside is not None:
+                rows_, beside = lax.optimization_barrier((rows_, beside))
+            got = across(rows_, bit)
+            for at, i in enumerate(sent):
+                blocks[i ^ bit] = blocks[i ^ bit].astype(f32) + got[at].astype(f32)
+                del blocks[i]
+        return blocks[0], beside
+
+    prompt_values, _ = exchange(value_rows[:prompt_rows], slab_bits[::-1])
+    prompt_keys, cot_last = exchange(key_rows[:prompt_rows], slab_bits, cot_last)
+    prompt_keys = jnp.concatenate(prompt_keys, axis=0)
+    prompt_values = jnp.concatenate(prompt_values, axis=0)
+    key_own, value_own = key_rows[prompt_rows:], value_rows[prompt_rows:]
     wide = gather_adapters(wide, ("ctx", "tp"))
     slim = gather_adapters(slim, ("ctx",))
     attention_rows, log_total = attention_forward(
         slab, query_rows, prompt_keys, prompt_values, key_own, value_own, prompt_rows
     )
-    attention_rows, cot_got = lax.optimization_barrier((attention_rows, cot_got))
+    attention_rows, cot_rest, wide, slim = lax.optimization_barrier(
+        (attention_rows, cot_rest, wide, slim)
+    )
+    cot_got = [cot_near] + cot_rest + [cot_last]
     whole_out = lax.all_gather(my_slab(w_out, 1), ("fsdp", "ctx"), axis=1, tiled=True)
     mid_out = (
         ADAPTER_SCALE
@@ -674,8 +699,6 @@
 
     gu_rank = 2 * RANK
     adapters = (wide, slim)
-    sums = tuple(jnp.zeros(a.shape, f32) for a in adapters)
-    w_gu = w_gate_up.transpose(0, 2, 1, 3)
     part = part_index.reshape(1).astype(jnp.int32)
     h_mine = my_part(h_second)
     cot_steps = [cotangent] + [(x, swap(x)) for x in cot_got]
@@ -686,6 +709,7 @@
             gates_t, ((shard_index - s) % shard_count) * locals_n, locals_n, axis=0
         )
         gate_steps.append((from_shard(block, s) if s else block).T)
+    h_mine, gate_steps = lax.optimization_barrier((h_mine, gate_steps))
     y_steps, dh_steps, d_gate_steps = [], [], []
     h_step = h_second
     h_next = from_shard(h_mine, 1)
@@ -694,19 +718,23 @@
             step_order[s], step_order_sets[s], part, h_step, cot_steps[s], gate_steps[s], w_gu,
             w_down, adapters, tuple(sums),
         )
+        last = s + 1 == shard_count
+        d_gate = d_gate.T
+        dh_send, d_gate, dh_steps, h_next = lax.optimization_barrier(
+            (dh_send, d_gate, dh_steps, h_next)
+        )
+        d_gate = to_shard(d_gate, s) if s else d_gate
         dh = dh_keep.astype(f32) + swap(dh_send).astype(f32)
-        if s:
-            dh = dh.astype(bf16)
-        if s + 1 < shard_count:
+        dh = dh.astype(bf16) if s else dh
+        if not last:
             h_step = (h_next, swap(h_next))
-            sums, h_step, h_mine, dh, dh_steps = lax.optimization_barrier(
-                (sums, h_step, h_mine, dh, dh_steps)
-            )
-            if s + 2 < shard_count:
-                h_next = from_shard(h_mine, s + 2)
+        sums, h_step, h_mine, dh, d_gate = lax.optimization_barrier(
+            (sums, h_step, h_mine, dh, d_gate)
+        )
+        if s + 2 < shard_count:
+            h_next = from_shard(h_mine, s + 2)
         dh_steps.append(to_shard(dh, s) if s else dh)
-        d_gate = d_gate.T
-        d_gate_steps.append(to_shard(d_gate, s) if s else d_gate)
+        d_gate_steps.append(d_gate)
         y_steps.append((y_keep, y_send))
     d_gates = sum_parts(
         by_shard(d_gate_steps, shard_index - shard_at).reshape(EXPERTS, row_count)
@@ -714,9 +742,11 @@
     d_second_mine = sum(dh.astype(f32) for dh in dh_steps).astype(bf16)
     y_steps = [keep.astype(f32) + swap(send).astype(f32) for keep, send in y_steps]
     y_steps = [y.astype(bf16) if s else y for s, y in enumerate(y_steps)]
-    d_second_mine, y_steps = lax.optimization_barrier((d_second_mine, y_steps))
+    d_second_mine, y_steps, sums = lax.optimization_barrier((d_second_mine, y_steps, sums))
+    wide_mine = scatter_experts(sums[0], ("ctx", "tp"))
+    slim_mine = scatter_experts(sums[1], ("ctx",))
     d_second_routed = join_parts(d_second_mine, swap(d_second_mine)).astype(f32)
-    y_odd = [to_shard(y_steps[s], s) for s in range(1, shard_count, 2)]
+    y_first = [to_shard(y_steps[s], s) for s in range(1, shard_count - 1)]
 
     d_probs = jnp.where(chosen, d_gates, 0.0)
     d_logits = (
@@ -755,10 +785,17 @@
         slab, query_rows, prompt_keys, prompt_values, key_own, value_own, attention_rows,
         d_att_rows, log_total, prompt_rows,
     )
-    d_query, y_odd, y_steps = lax.optimization_barrier((d_query, y_odd, y_steps))
-    y_even = [to_shard(y_steps[s], s) for s in range(2, shard_count, 2)]
-    d_key_prompt = exchange_back(d_key_all, slab_bits)
-    d_value_prompt = exchange_back(d_value_all, slab_bits[::-1])
+    d_key_all, d_value_all, y_first, y_last = lax.optimization_barrier(
+        (d_key_all, d_value_all, y_first, y_steps[-1])
+    )
+    y_last = to_shard(y_last, shard_count - 1)
+    d_key_prompt, y_last = exchange_back(d_key_all, slab_bits, y_last)
+    d_value_prompt, _ = exchange_back(d_value_all, slab_bits[::-1])
+    d_key_prompt, wide_mine, slim_mine = lax.optimization_barrier(
+        (d_key_prompt, wide_mine, slim_mine)
+    )
+    g_wide = sets_of_experts(wide_mine, ("ctx", "tp"))
+    g_slim = sets_of_experts(slim_mine, ("ctx",))
     d_key = jnp.concatenate([d_key_prompt, d_key_own], axis=0)
     d_value = jnp.concatenate([d_value_prompt, d_value_own], axis=0)
     d_q_norm = rotate(heads_of(d_query), cosine, -sine_part).reshape(row_count, local_width)
@@ -777,9 +814,8 @@
         - k_raw * (k_scale * k_scale * k_scale) * dots[1][:, None] / full_width
     )
     d_proj = jnp.stack([d_q_raw, d_k_raw, d_value], axis=0).astype(bf16)
-    d_proj, y_even = lax.optimization_barrier((d_proj, y_even))
     mixed_mine = sum(
-        [y.astype(f32) for y in y_steps[:1] + y_odd + y_even], my_part(x_mid)
+        [y.astype(f32) for y in [y_steps[0], *y_first, y_last]], my_part(x_mid)
     ).astype(bf16)
     mixed = join_parts(mixed_mine, swap(mixed_mine))
     dp_tiles = d_proj.reshape(3, tiles, TILE, local_width)
@@ -788,11 +824,12 @@
         * jnp.einsum("jtno,tjro->tnjr", dp_tiles, t_qkv_b, preferred_element_type=f32)
     ).astype(bf16)
     d_first = sum_parts(
-        sum(dot_nt(d_proj[j], weights[j]) for j in range(3))
+        jnp.einsum("jno,jdo->nd", d_proj, weights, preferred_element_type=f32)
         + jnp.einsum("tnjr,tjrd->tnd", d_mid_qkv, t_qkv_a, preferred_element_type=f32).reshape(
             row_count, full_width
         )
     )
+    d_first, g_wide, g_slim = lax.optimization_barrier((d_first, g_wide, g_slim))
     grad_input = d_x_mid + rms_back(token_vals, gain_in, d_first, first_scale, full_width)
     g_qkv_b = jnp.einsum("tnjr,jtno->tjro", mid_qkv, dp_tiles, preferred_element_type=f32)
     g_qkv_a = jnp.einsum(
@@ -801,34 +838,65 @@
 
     def to_sets(pieces_):
         rows_ = jnp.concatenate(pieces_, axis=1)
-        return jnp.sum(tile_hot[:, :, None, None] * rows_[None], axis=1)
+        return jnp.sum(tile_hot[:, :, None, None] * rows_[None], axis=1).astype(bf16)
+
+    def both_parts(x):
+        return (x.astype(f32) + swap(x).astype(f32)).astype(bf16)
+
+    def add(mine, other):
+        return (mine.astype(f32) + other.astype(f32)).astype(bf16)
 
     def reduced(x):
-        n_rows = x.shape[1]
-        pad = -n_rows % (16 * slab_count)
-        x = jnp.pad(x.astype(bf16), ((0, 0), (0, pad), (0, 0)))
-        x = x.reshape(shard_count, sets_local, slab_count, -1, local_width)
-        x = x.transpose(0, 2, 1, 3, 4).reshape((shard_count * slab_count, sets_local, -1, local_width))
-        mine = lax.psum_scatter(x, ("fsdp", "ctx"), scatter_dimension=0, tiled=False)
-        return lax.all_gather(mine, "ctx", axis=1, tiled=True)[:, :n_rows].astype(f32)
-
-    early_both = sum_parts(to_sets([as_rows(g_out_b)]))
-    early_one = to_sets([as_rows(g_out_a), as_rows(g_router_a), router_rows(g_router_b)])
-    early = reduced(jnp.concatenate([early_both, early_one], axis=1))
-    late_both = sum_parts(to_sets([as_rows(g_qkv_a)]))
-    late = reduced(jnp.concatenate([late_both, to_sets([as_rows(g_qkv_b)])], axis=1))
-    n0, n2, n3, n4 = sizes[0], sizes[2], sizes[3], sizes[4]
-    grad_qkv_a = late[:, :n0].reshape(sets_local, 3, RANK, full_width).transpose(0, 3, 1, 2)
-    grad_qkv_b = late[:, n0:].reshape(sets_local, 3, RANK, local_width).transpose(0, 2, 1, 3)
-    grad_out_b = early[:, :n3].reshape(out_b.shape)
-    grad_out_a = early[:, n3 : n3 + n2].reshape(sets_local, RANK, local_width).transpose(0, 2, 1)
-    grad_router_a = (
-        early[:, n3 + n2 : n3 + n2 + n4].reshape(sets_local, RANK, full_width).transpose(0, 2, 1)
-    )
-    grad_router_b = early[:, n3 + n2 + n4, : RANK * EXPERTS].reshape(router_b.shape)
-
-    g_wide = sets_of_experts(sums[0], ("ctx", "tp"))
-    g_slim = sets_of_experts(sums[1], ("ctx",))
+        n_rows, half_width = x.shape[1], local_width // 2
+        x = jnp.pad(x, ((0, 0), (0, -n_rows % (16 * slab_count)), (0, 0)))
+        halves = []
+        for i, bits in enumerate((slab_bits, slab_bits[::-1])):
+            y = x[:, :, i * half_width : (i + 1) * half_width]
+            for bit in bits:
+                high = (slab_index // bit) % 2
+                y = y.reshape(y.shape[0], 2, y.shape[1] // 2, half_width)
+                y = add(
+                    lax.dynamic_index_in_dim(y, high, axis=1, keepdims=False),
+                    across(lax.dynamic_index_in_dim(y, 1 - high, axis=1, keepdims=False), bit),
+                )
+            y = y.reshape(shard_count, sets_local, y.shape[1], half_width)
+            blocks = []
+            for s in range(shard_count):
+                block = lax.dynamic_index_in_dim(
+                    y, (shard_index + s) % shard_count, axis=0, keepdims=False
+                )
+                blocks.append(to_shard(block, s) if s else block)
+            y = sum(block.astype(f32) for block in blocks).astype(bf16)
+            for bit in bits[::-1]:
+                is_high = (slab_index // bit) % 2 == 1
+                other = across(y, bit)
+                y = jnp.concatenate(
+                    [jnp.where(is_high, other, y), jnp.where(is_high, y, other)], axis=1
+                )
+            halves.append(y)
+        return jnp.concatenate(halves, axis=2)[:, :n_rows].astype(f32)
+
+    summed = reduced(
+        jnp.concatenate(
+            [
+                both_parts(to_sets([as_rows(g_qkv_a), as_rows(g_out_b)])),
+                to_sets([as_rows(g_qkv_b), as_rows(g_out_a), as_rows(g_router_a)]),
+                to_sets([router_rows(g_router_b)]),
+            ],
+            axis=1,
+        )
+    )
+    order_ = (sizes[0], sizes[3], sizes[1], sizes[2], sizes[4], sizes[5])
+    cuts = [sum(order_[:i]) for i in range(len(order_) + 1)]
+    s_qkv_a, s_out_b, s_qkv_b, s_out_a, s_router_a, s_router_b = [
+        summed[:, cuts[i] : cuts[i + 1]] for i in range(len(order_))
+    ]
+    grad_qkv_a = s_qkv_a.reshape(sets_local, 3, RANK, full_width).transpose(0, 3, 1, 2)
+    grad_qkv_b = s_qkv_b.reshape(sets_local, 3, RANK, local_width).transpose(0, 2, 1, 3)
+    grad_out_b = s_out_b.reshape(out_b.shape)
+    grad_out_a = s_out_a.reshape(sets_local, RANK, local_width).transpose(0, 2, 1)
+    grad_router_a = s_router_a.reshape(sets_local, RANK, full_width).transpose(0, 2, 1)
+    grad_router_b = s_router_b[:, 0, : RANK * EXPERTS].reshape(router_b.shape)
 
     def of_experts(g):
         return g.reshape((sets_local, EXPERTS) + g.shape[3:]).astype(f32)

time: 1920 us -> 1700 us (0.89)
  waiting for transfers between devices: 662 us -> 489 us
  starting transfers between devices: 183 us -> 149 us
  blocking collectives: 26 us -> 0 us
    ppermute x27, waiting for transfers between devices: 283 us -> 152 us  [from_shard(): lax.ppermute(x, 'fsdp', [(i, (i - s) % shard_count) for i in range(shard_...]
    ppermute x20 -> x28, waiting for transfers between devices: 120 us -> 195 us  [across(): return lax.ppermute(x, 'ctx', [(i, i ^ bit) for i in range(slab_count)])]
    ppermute x15 -> x21, waiting for transfers between devices: 176 us -> 115 us  [to_shard(): lax.ppermute(x, 'fsdp', [(i, (i + s) % shard_count) for i in range(shard_...]
    reduce_scatter x4 -> x2, waiting for transfers between devices: 42.7 us -> 0.04 us  [scatter_experts(): return lax.psum_scatter(x, axes, scatter_dimension=1, tiled=True)]
    ppermute x27, starting transfers between devices: 111 us -> 76.5 us  [from_shard(): lax.ppermute(x, 'fsdp', [(i, (i - s) % shard_count) for i in range(shard_...]
    all_gather x2, waiting for transfers between devices: 30 us -> 0.01 us  [sets_of_experts(): lax.all_gather(by_shard(got, shard_index - shard_at), axes, axis=1, tiled...]
    all_gather x2 -> x0, blocking collectives: 26 us -> none  [reduced(): lax.all_gather(mine, 'ctx', axis=1, tiled=True)[:, :n_rows].astype(f32)]
    unnamed x302 -> x357, local copies, waits for them, and re-layouts: 92.1 us -> 86.6 us
  transfers between devices with their start and end apart: 96 -> 107, of which waited for: 33 -> 47; matrix products, arithmetic and copies ran while one was open for 26% -> 26% of each run, Pallas kernels for 21% -> 29%
where the time goes in v3:
time: 1700 us; the launch traced here: 1690 us
  waiting for transfers between devices  489 us (29%)
  Pallas kernels  482 us (28%)
  other arithmetic  250 us (15%)
  local copies, waits for them, and re-layouts  198 us (12%)
  starting transfers between devices  149 us (9%)
  matrix products  103 us (6%)
    pallas_call x4, Pallas kernels, expert_pass(): pl.pallas_call(body, grid_spec=pltpu.PrefetchScalarGridSpec(num_scalar_pr...  360 us
    ppermute x28, waiting for transfers between devices, across(): return lax.ppermute(x, 'ctx', [(i, i ^ bit) for i in range(slab_count)])  195 us
    ppermute x27, waiting for transfers between devices, from_shard(): lax.ppermute(x, 'fsdp', [(i, (i - s) % shard_count) for i in range(shard_...  152 us
    ppermute x21, waiting for transfers between devices, to_shard(): lax.ppermute(x, 'fsdp', [(i, (i + s) % shard_count) for i in range(shard_...  115 us
    unnamed x357, local copies, waits for them, and re-layouts  86.6 us
    ppermute x27, starting transfers between devices, from_shard(): lax.ppermute(x, 'fsdp', [(i, (i - s) % shard_count) for i in range(shard_...  76.5 us
    pallas_call x1, Pallas kernels, attention_backward(): pl.pallas_call(body, grid_spec=pltpu.PrefetchScalarGridSpec(num_scalar_pr...  70.7 us
    pallas_call x1, Pallas kernels, attention_forward(): pl.pallas_call(body, grid_spec=pltpu.PrefetchScalarGridSpec(num_scalar_pr...  51.2 us
  transfers between devices with their start and end apart: 107, of which 47 were waited for; matrix products, arithmetic and copies ran while one was open for 26% of the time, Pallas kernels for 29%

profile of v3, /device:TPU:0, one launch (start us, length us, event | category | flops | bytes accessed | tf_op | source)
XLA Modules:
  0.0 1686.4 jit_solution(13121201801680218081)
XLA Ops:
  23.1 5.4 collective-permute-done.2
  28.5 14.6 collective-permute-done.1
  44.4 7.0 collective-permute-start.5
  53.8 7.1 collective-permute-done.5
  60.9 19.2 %collective-permute-done.4 = bf16[128,1024]{1,0:T(8,128)(2,1)S(1)} collective-permute-done((bf16[128,1024]{1,0:T(8,128)(2,1)S(1)}, bf16[128,1024]{1,0:T(8,128)(2,1)S(1)}, u32[]{:S(2)}, u32[]{:S(2)}) %collective-permute-start.4) | collective-permute-done | bytes 262176 | tf_op jit(solution)/shard_map/ppermute | solution.py:426
  80.7 6.0 collective-permute-start.8
  97.5 21.0 %collective-permute-done.7 = bf16[128,1024]{1,0:T(8,128)(2,1)S(1)} collective-permute-done((bf16[128,1024]{1,0:T(8,128)(2,1)S(1)}, bf16[128,1024]{1,0:T(8,128)(2,1)S(1)}, u32[]{:S(2)}, u32[]{:S(2)}) %collective-permute-start.7) | collective-permute-done | bytes 262176 | tf_op jit(solution)/shard_map/ppermute | solution.py:426
  124.3 17.4 %collective-permute-start.15 = (bf16[96,512]{1,0:T(8,128)(2,1)}, bf16[96,512]{1,0:T(8,128)(2,1)}, u32[]{:S(2)}, u32[]{:S(2)}) collective-permute-start(bf16[96,512]{1,0:T(8,128)(2,1)} %get-tuple-element.410), channel_id=1, source_target_pairs={{0,8},{8,16},{16,24},{24,0},{1,9},{9,17},{17,25},{25,1},{2,10},{10... | collective-permute-start | bytes 294920 | tf_op jit(solution)/shard_map/ppermute | solution.py:426
  156.3 15.8 copy.234
  202.5 10.1 collective-permute-done.22
  221.4 5.2 collective-permute-done.26
  234.5 24.3 %collective-permute-done.21 = bf16[2,2,128,1024]{3,2,1,0:T(8,128)(2,1)} collective-permute-done((bf16[2,2,128,1024]{3,2,1,0:T(8,128)(2,1)}, bf16[2,2,128,1024]{3,2,1,0:T(8,128)(2,1)}, u32[]{:S(2)}, u32[]{:S(2)}) %collective-permute-start.21) | collective-permute-done | bytes 1048608 | tf_op jit(solution)/shard_map/ppermute | solution.py:439
  269.6 27.2 %collective-permute-done.25 = bf16[2,2,128,1024]{3,2,1,0:T(8,128)(2,1)S(1)} collective-permute-done((bf16[2,2,128,1024]{3,2,1,0:T(8,128)(2,1)S(1)}, bf16[2,2,128,1024]{3,2,1,0:T(8,128)(2,1)S(1)}, u32[]{:S(2)}, u32[]{:S(2)}) %collective-permute-start.25) | collective-permute-done | bytes 1048608 | tf_op jit(solution)/shard_map/ppermute | solution.py:439
  302.4 15.8 collective-permute-done.16
  324.6 9.6 pad_maximum_fusion
  334.2 11.0 gather_fusion
  345.2 6.6 broadcast_select_fusion
  356.7 4.9 copy.174
  384.4 5.2 fusion.29
  405.6 11.4 collective-permute-done.33
  421.5 8.9 collective-permute-done.30
  445.0 29.3 %collective-permute-done.34 = bf16[2,512,1024]{2,1,0:T(8,128)(2,1)} collective-permute-done((bf16[2,512,1024]{2,1,0:T(8,128)(2,1)}, bf16[2,512,1024]{2,1,0:T(8,128)(2,1)}, u32[]{:S(2)}, u32[]{:S(2)}) %collective-permute-start.34) | collective-permute-done | bytes 2097184 | tf_op jit(solution)/shard_map/ppermute | solution.py:439
  476.0 9.1 pad_maximum_fusion.4.v_ref
  489.2 51.2 %attention_forward.1 = (bf16[1024,1024]{1,0:T(8,128)(2,1)}, f32[8,1,1024]{2,1,0:T(1,128)}) custom-call(s32[1]{0:T(128)} %bitcast.slab_ref, bf16[1024,1024]{1,0:T(8,128)(2,1)} %bitcast.574, bf16[2048,1024]{1,0:T(8,128)(2,1)} %pad_maximum_fusion.3.k_ref, bf16[2048,1024]{1,0:T(8,128)(2,1)} %pad_maximum_fusion.4.v_ref, bf16[512,1024]{1,0:T(8,128)(2,1)} %bitcast.579, ...), custom_call_target="tpu_custom_call" | custom-call | tf_op jit(solution)/shard_map/attention_forward/pallas_call | solution.py:138
  547.5 10.2 bitcast_add_fusion.2
  559.0 12.2 collective-permute-done.36
  571.2 8.6 multiply_reduce_fusion.3
  595.7 9.8 collective-permute-done.42
  605.5 21.6 %collective-permute-done.41 = f32[4,1024]{0,1:T(8,128)S(1)} collective-permute-done((f32[4,1024]{0,1:T(8,128)S(1)}, f32[4,1024]{0,1:T(8,128)S(1)}, u32[]{:S(2)}, u32[]{:S(2)}) %collective-permute-start.41) | collective-permute-done | bytes 16416 | tf_op jit(solution)/shard_map/ppermute | solution.py:426
  628.0 12.6 collective-permute-start.43
  643.3 43.5 %collective-permute-done.38 = s32[4]{0:T(128)S(1)} collective-permute-done((s32[4]{0:T(128)S(1)}, s32[4]{0:T(128)S(1)}, u32[]{:S(2)}, u32[]{:S(2)}) %collective-permute-start.38) | collective-permute-done | bytes 48 | tf_op jit(solution)/shard_map/ppermute | solution.py:426
  690.2 6.0 broadcast_in_dim.76.swide_ref
  696.3 89.1 %expert_pass.4 = (bf16[1024,1024]{1,0:T(8,128)(2,1)}, bf16[1024,1024]{1,0:T(8,128)(2,1)}, bf16[1024,1024]{1,0:T(8,128)(2,1)}, bf16[1024,1024]{1,0:T(8,128)(2,1)}...) custom-call(s32[4]{0:T(128)} %get-tuple-element.475.order_ref, ...), custom_call_target="tpu_custom_call", output_to_operand_aliasing={{5}: (12, {}), {6}: (13, {})} | custom-call | tf_op jit(solution)/shard_map/expert_pass/pallas_call | solution.py:366
  798.2 89.8 %expert_pass.5 = (bf16[1024,1024]{1,0:T(8,128)(2,1)}, bf16[1024,1024]{1,0:T(8,128)(2,1)}, bf16[1024,1024]{1,0:T(8,128)(2,1)}, bf16[1024,1024]{1,0:T(8,128)(2,1)}...) custom-call(s32[4]{0:T(128)} %get-tuple-element.474.order_ref, ...), custom_call_target="tpu_custom_call", output_to_operand_aliasing={{5}: (12, {}), {6}: (13, {})} | custom-call | tf_op jit(solution)/shard_map/expert_pass/pallas_call | solution.py:366
  897.6 8.6 collective-permute-done.50
  907.6 90.0 %expert_pass.6 = (bf16[1024,1024]{1,0:T(8,128)(2,1)}, bf16[1024,1024]{1,0:T(8,128)(2,1)}, bf16[1024,1024]{1,0:T(8,128)(2,1)}, bf16[1024,1024]{1,0:T(8,128)(2,1)}...) custom-call(s32[4]{0:T(128)} %get-tuple-element.473.order_ref, ...), custom_call_target="tpu_custom_call", output_to_operand_aliasing={{5}: (12, {}), {6}: (13, {})} | custom-call | tf_op jit(solution)/shard_map/expert_pass/pallas_call | solution.py:366
  1008.7 17.6 %collective-permute-done.56 = f32[4,1024]{0,1:T(8,128)S(1)} collective-permute-done((f32[4,1024]{0,1:T(8,128)}, f32[4,1024]{0,1:T(8,128)S(1)}, u32[]{:S(2)}, u32[]{:S(2)}) %collective-permute-start.56) | collective-permute-done | bytes 16416 | tf_op jit(solution)/shard_map/ppermute | solution.py:431
  1027.6 90.7 %expert_pass.7 = (bf16[1024,1024]{1,0:T(8,128)(2,1)}, bf16[1024,1024]{1,0:T(8,128)(2,1)}, bf16[1024,1024]{1,0:T(8,128)(2,1)}, bf16[1024,1024]{1,0:T(8,128)(2,1)}...) custom-call(s32[4]{0:T(128)} %get-tuple-element.472.order_ref, ...), custom_call_target="tpu_custom_call", output_to_operand_aliasing={{5}: (12, {}), {6}: (13, {})} | custom-call | tf_op jit(solution)/shard_map/expert_pass/pallas_call | solution.py:366
  1129.5 9.7 collective-permute-done.60
  1152.9 34.5 %collective-permute-done.61 = bf16[1024,1024]{1,0:T(8,128)(2,1)S(1)} collective-permute-done((bf16[1024,1024]{1,0:T(8,128)(2,1)S(1)}, bf16[1024,1024]{1,0:T(8,128)(2,1)S(1)}, u32[]{:S(2)}, u32[]{:S(2)}) %collective-permute-start.61) | collective-permute-done | bytes 2097184 | tf_op jit(solution)/shard_map/ppermute | solution.py:431
  1204.6 5.7 fusion.113
  1215.1 8.4 convert_element_type.437
  1229.2 6.8 multiply_reduce_fusion.2
  1236.0 18.3 %fusion.102 = (bf16[1024,2048]{1,0:T(8,128)(2,1)S(1)}, f32[1024,2048]{1,0:T(8,128)}) fusion(f32[1024]{0:T(1024)S(1)} %get-tuple-element.468, f32[1024,2048]{1,0:T(8,128)} %copy-done.3, f32[1024]{0:T(1024)S(1)} %copy-done.140, f32[4,256,2048]{2,1,0:T(8,128)} %fusion.113, f32[1024,2048]{1,0:T(8,128)} %get-tuple-element.469, bf16[1024,1024]{1,0:T(8,128)(2,1)} %copy-done.23, ...), kind=kLoop, calls=%fused_computation.411 | loop fusion | flops 31457280 | bytes 46157824 | tf_op jit(solution)/shard_map/convert_element_type | solution.py:770
  1258.6 6.1 fusion.28.da_ref
  1264.8 70.7 %attention_backward.1 = (f32[1024,1024]{1,0:T(8,128)}, bf16[2048,1024]{1,0:T(8,128)(2,1)}, bf16[2048,1024]{1,0:T(8,128)(2,1)}, f32[512,1024]{1,0:T(8,128)}, f32[512,1024]{1,0:T(8,128)}) custom-call(s32[1]{0:T(128)} %bitcast.slab_ref, bf16[1024,1024]{1,0:T(8,128)(2,1)} %bitcast.575, bf16[2048,1024]{1,0:T(8,128)(2,1)} %pad_maximum_fusion.3.k_ref, ...), custom_call_target="tpu_custom_call" | custom-call | tf_op jit(solution)/shard_map/attention_backward/pallas_call | solution.py:215
  1335.5 15.4 collective-permute-done.69
  1359.6 7.1 copy.191
  1366.8 5.7 bitcast_select_fusion
  1372.7 29.5 %collective-permute-done.75 = bf16[2,512,1024]{2,1,0:T(8,128)(2,1)} collective-permute-done((bf16[2,512,1024]{2,1,0:T(8,128)(2,1)}, bf16[2,512,1024]{2,1,0:T(8,128)(2,1)}, u32[]{:S(2)}, u32[]{:S(2)}) %collective-permute-start.75) | collective-permute-done | bytes 2097184 | tf_op jit(solution)/shard_map/ppermute | solution.py:439
  1419.9 5.2 copy.221
  1425.1 4.9 collective-permute-done.76
  1463.3 5.5 collective-permute-done.80
  1468.8 9.8 collective-permute-done.79
  1480.7 4.9 fusion.26
  1502.5 22.6 %bitcast_add_fusion = f32[1024,2048]{1,0:T(8,128)} fusion(f32[4,256,2048,1]{2,1,3,0:T(8,128)} %fusion.114, bf16[3,2048,1024]{2,1,0:T(8,128)(2,1)} %bitcast_select_fusion, bf16[1,1024,1024]{2,1,0:T(8,128)(2,1)} %fusion.165, bf16[1,1024,1024]{2,1,0:T(8,128)(2,1)} %bitcast.619, bf16[1,1024,1024]{2,1,0:T(8,128)(2,1)} %bitcast.616), kind=kOutput, calls=%fused_computation.30 | convolution fusion | flops 12893290496 | bytes 35651584 | tf_op jit(solution)/shard_map/jno,jdo->nd/dot_general | solution.py:827
  1526.1 7.3 add_convert_fusion.1
  1559.0 10.5 collective-permute-done.85
  1578.1 8.0 collective-permute-done.86
  1598.9 4.9 collective-permute-start.95
  1608.8 4.9 collective-permute-done.95
  1632.0 11.9 add.677
  1643.9 6.6 copy.235
  1655.1 5.5 slice.369
  (776 shorter events, 485.6 us)
Async XLA Ops:
  7.2 349.5 %all-gather.18.cloned.1.call-start = ((), (), s32[]{:S(2)}) async-start(), calls=%async_computation.9 | async-start | bytes 4456448 | tf_op jit(solution)/shard_map/all_gather | solution.py:499
  13.8 526.6 %all-gather.10.cloned.1.call-start = ((), (), s32[]{:S(2)}) async-start(), calls=%async_computation.3 | async-start | bytes 1966080 | tf_op jit(solution)/shard_map/all_gather | solution.py:570
  19.2 23.9 %collective-permute-start.1 = (bf16[128,1024]{1,0:T(8,128)(2,1)S(1)}, bf16[128,1024]{1,0:T(8,128)(2,1)S(1)}, u32[]{:S(2)}, u32[]{:S(2)}) collective-permute-start(bf16[128,1024]{1,0:T(8,128)(2,1)S(1)} %dynamic-slice_bitcast_fusion.7), channel_id=1, source_target_pairs={{0,16},{8,24},{16,0},{24,8},{1,17},{9,25},{17,1},{25,9},{2,18},{10... | collective-permute-start | bytes 786440 | tf_op jit(solution)/shard_map/ppermute | solution.py:426
  51.4 28.7 %collective-permute-start.4 = (bf16[128,1024]{1,0:T(8,128)(2,1)S(1)}, bf16[128,1024]{1,0:T(8,128)(2,1)S(1)}, u32[]{:S(2)}, u32[]{:S(2)}) collective-permute-start(bf16[128,1024]{1,0:T(8,128)(2,1)S(1)} %constant_dynamic-slice_fusion.6), channel_id=1, source_target_pairs={{0,16},{8,24},{16,0},{24,8},{1,17},{9,25},{17,1},{25,9},{2,18},{10... | collective-permute-start | bytes 786440 | tf_op jit(solution)/shard_map/ppermute | solution.py:426
  53.0 27.7 %collective-permute-start.3 = (bf16[128,1024]{1,0:T(8,128)(2,1)S(1)}, bf16[128,1024]{1,0:T(8,128)(2,1)}, u32[]{:S(2)}, u32[]{:S(2)}) collective-permute-start(bf16[128,1024]{1,0:T(8,128)(2,1)S(1)} %constant_dynamic-slice_fusion.6), channel_id=1, source_target_pairs={{0,24},{8,0},{16,8},{24,16},{1,25},{9,1},{17,9},{25,17},{2,26},{10... | collective-permute-start | bytes 786440 | tf_op jit(solution)/shard_map/ppermute | solution.py:426
  86.7 31.7 %collective-permute-start.7 = (bf16[128,1024]{1,0:T(8,128)(2,1)S(1)}, bf16[128,1024]{1,0:T(8,128)(2,1)S(1)}, u32[]{:S(2)}, u32[]{:S(2)}) collective-permute-start(bf16[128,1024]{1,0:T(8,128)(2,1)S(1)} %constant_dynamic-slice_fusion.5), channel_id=1, source_target_pairs={{0,16},{8,24},{16,0},{24,8},{1,17},{9,25},{17,1},{25,9},{2,18},{10... | collective-permute-start | bytes 786440 | tf_op jit(solution)/shard_map/ppermute | solution.py:426
  89.6 28.9 %collective-permute-start.6 = (bf16[128,1024]{1,0:T(8,128)(2,1)S(1)}, bf16[128,1024]{1,0:T(8,128)(2,1)S(1)}, u32[]{:S(2)}, u32[]{:S(2)}) collective-permute-start(bf16[128,1024]{1,0:T(8,128)(2,1)S(1)} %constant_dynamic-slice_fusion.5), channel_id=1, source_target_pairs={{0,24},{8,0},{16,8},{24,16},{1,25},{9,1},{17,9},{25,17},{2,26},{10... | collective-permute-start | bytes 786440 | tf_op jit(solution)/shard_map/ppermute | solution.py:426
  119.3 56.9 %collective-permute-start.9 = (bf16[1,2,128,1024]{3,2,1,0:T(8,128)(2,1)S(1)}, bf16[1,2,128,1024]{3,2,1,0:T(8,128)(2,1)S(1)}, u32[]{:S(2)}, u32[]{:S(2)}) collective-permute-start(bf16[1,2,128,1024]{3,2,1,0:T(8,128)(2,1)S(1)} %maximum_bitcast_fusion.1), channel_id=1, source_target_pairs={{0,2},{2,0},{4,6},{6,4},{1,3},{3,1},{5,7},{7,5},{8,10},{10,8},{12,... | collective-permute-start | bytes 1572872 | tf_op jit(solution)/shard_map/ppermute | solution.py:439
  124.3 24.9 %collective-permute-start.15 = (bf16[96,512]{1,0:T(8,128)(2,1)}, bf16[96,512]{1,0:T(8,128)(2,1)}, u32[]{:S(2)}, u32[]{:S(2)}) collective-permute-start(bf16[96,512]{1,0:T(8,128)(2,1)} %get-tuple-element.410), channel_id=1, source_target_pairs={{0,8},{8,16},{16,24},{24,0},{1,9},{9,17},{17,25},{25,1},{2,10},{10... | collective-permute-start | bytes 294920 | tf_op jit(solution)/shard_map/ppermute | solution.py:426
  149.2 24.8 %collective-permute-start.12 = (bf16[48,2048]{1,0:T(8,128)(2,1)}, bf16[48,2048]{1,0:T(8,128)(2,1)}, u32[]{:S(2)}, u32[]{:S(2)}) collective-permute-start(bf16[48,2048]{1,0:T(8,128)(2,1)} %get-tuple-element.374), channel_id=1, source_target_pairs={{0,8},{8,16},{16,24},{24,0},{1,9},{9,17},{17,25},{25,1},{2,10},{10... | collective-permute-start | bytes 589832 | tf_op jit(solution)/shard_map/ppermute | solution.py:426
  149.2 24.8 %collective-permute-start.11 = (bf16[48,2048]{1,0:T(8,128)(2,1)}, bf16[48,2048]{1,0:T(8,128)(2,1)}, u32[]{:S(2)}, u32[]{:S(2)}) collective-permute-start(bf16[48,2048]{1,0:T(8,128)(2,1)} %get-tuple-element.375), channel_id=1, source_target_pairs={{0,16},{8,24},{16,0},{24,8},{1,17},{9,25},{17,1},{25,9},{2,18},{10... | collective-permute-start | bytes 589832 | tf_op jit(solution)/shard_map/ppermute | solution.py:426
  154.8 22.5 %collective-permute-start.17 = (bf16[1,2,128,1024]{3,2,1,0:T(8,128)(2,1)}, bf16[1,2,128,1024]{3,2,1,0:T(8,128)(2,1)S(1)}, u32[]{:S(2)}, u32[]{:S(2)}) collective-permute-start(bf16[1,2,128,1024]{3,2,1,0:T(8,128)(2,1)} %maximum_bitcast_fusion.2), channel_id=1, source_target_pairs={{0,4},{2,6},{4,0},{6,2},{1,5},{3,7},{5,1},{7,3},{8,12},{10,14},{12... | collective-permute-start | bytes 1572872 | tf_op jit(solution)/shard_map/ppermute | solution.py:439
  179.5 361.0 %all-gather.8.cloned.1.call-start = ((), (), s32[]{:S(2)}) async-start(), calls=%async_computation.2 | async-start | bytes 7077888 | tf_op jit(solution)/shard_map/all_gather | solution.py:570
  180.2 367.2 %all-gather.12.cloned.1.call-start = ((), (), s32[]{:S(2)}) async-start(), calls=%async_computation.4 | async-start | bytes 4456448 | tf_op jit(solution)/shard_map/all_gather | solution.py:672
  191.8 24.2 %collective-permute-start.20 = (bf16[1,2,128,1024]{3,2,1,0:T(8,128)(2,1)S(1)}, bf16[1,2,128,1024]{3,2,1,0:T(8,128)(2,1)S(1)}, u32[]{:S(2)}, u32[]{:S(2)}) collective-permute-start(bf16[1,2,128,1024]{3,2,1,0:T(8,128)(2,1)S(1)} %maximum_bitcast_fusion.3), channel_id=1, source_target_pairs={{0,2},{2,0},{4,6},{6,4},{1,3},{3,1},{5,7},{7,5},{8,10},{10,8},{12,... | collective-permute-start | bytes 1572872 | tf_op jit(solution)/shard_map/ppermute | solution.py:439
  195.9 33.9 %collective-permute-start.24 = (bf16[1,2,128,1024]{3,2,1,0:T(8,128)(2,1)}, bf16[1,2,128,1024]{3,2,1,0:T(8,128)(2,1)}, u32[]{:S(2)}, u32[]{:S(2)}) collective-permute-start(bf16[1,2,128,1024]{3,2,1,0:T(8,128)(2,1)} %maximum_bitcast_fusion.5), channel_id=1, source_target_pairs={{0,2},{2,0},{4,6},{6,4},{1,3},{3,1},{5,7},{7,5},{8,10},{10,8},{12,... | collective-permute-start | bytes 1572872 | tf_op jit(solution)/shard_map/ppermute | solution.py:439
  198.4 28.2 %collective-permute-start.26 = (bf16[1,2,128,1024]{3,2,1,0:T(8,128)(2,1)}, bf16[1,2,128,1024]{3,2,1,0:T(8,128)(2,1)S(1)}, u32[]{:S(2)}, u32[]{:S(2)}) collective-permute-start(bf16[1,2,128,1024]{3,2,1,0:T(8,128)(2,1)} %maximum_bitcast_fusion.6), channel_id=1, source_target_pairs={{0,4},{2,6},{4,0},{6,2},{1,5},{3,7},{5,1},{7,3},{8,12},{10,14},{12... | collective-permute-start | bytes 1572872 | tf_op jit(solution)/shard_map/ppermute | solution.py:439
  213.7 51.0 %collective-permute-start.23 = (bf16[2,2,128,1024]{3,2,1,0:T(8,128)(2,1)}, bf16[2,2,128,1024]{3,2,1,0:T(8,128)(2,1)}, u32[]{:S(2)}, u32[]{:S(2)}) collective-permute-start(bf16[2,2,128,1024]{3,2,1,0:T(8,128)(2,1)} %pad_maximum_fusion.28), channel_id=1, source_target_pairs={{0,2},{2,0},{4,6},{6,4},{1,3},{3,1},{5,7},{7,5},{8,10},{10,8},{12,... | collective-permute-start | bytes 3145736 | tf_op jit(solution)/shard_map/ppermute | solution.py:439
  217.2 41.6 %collective-permute-start.21 = (bf16[2,2,128,1024]{3,2,1,0:T(8,128)(2,1)}, bf16[2,2,128,1024]{3,2,1,0:T(8,128)(2,1)}, u32[]{:S(2)}, u32[]{:S(2)}) collective-permute-start(bf16[2,2,128,1024]{3,2,1,0:T(8,128)(2,1)} %pad_maximum_fusion.27), channel_id=1, source_target_pairs={{0,4},{2,6},{4,0},{6,2},{1,5},{3,7},{5,1},{7,3},{8,12},{10,14},{12... | collective-permute-start | bytes 3145736 | tf_op jit(solution)/shard_map/ppermute | solution.py:439
  219.5 1220.9 %reduce-scatter.5.cloned.1.call-start = ((), (), s32[]{:S(2)}) async-start(), calls=%async_computation.6 | async-start | bytes 1966080 | tf_op jit(solution)/shard_map/reduce_scatter | solution.py:575
  227.8 72.1 %collective-permute-start.27 = (bf16[2,2,128,1024]{3,2,1,0:T(8,128)(2,1)S(1)}, bf16[2,2,128,1024]{3,2,1,0:T(8,128)(2,1)S(1)}, u32[]{:S(2)}, u32[]{:S(2)}) collective-permute-start(bf16[2,2,128,1024]{3,2,1,0:T(8,128)(2,1)S(1)} %pad_maximum_fusion.30), channel_id=1, source_target_pairs={{0,2},{2,0},{4,6},{6,4},{1,3},{3,1},{5,7},{7,5},{8,10},{10,8},{12,... | collective-permute-start | bytes 3145736 | tf_op jit(solution)/shard_map/ppermute | solution.py:439
  231.0 65.8 %collective-permute-start.25 = (bf16[2,2,128,1024]{3,2,1,0:T(8,128)(2,1)S(1)}, bf16[2,2,128,1024]{3,2,1,0:T(8,128)(2,1)S(1)}, u32[]{:S(2)}, u32[]{:S(2)}) collective-permute-start(bf16[2,2,128,1024]{3,2,1,0:T(8,128)(2,1)S(1)} %pad_maximum_fusion.29), channel_id=1, source_target_pairs={{0,4},{2,6},{4,0},{6,2},{1,5},{3,7},{5,1},{7,3},{8,12},{10,14},{12... | collective-permute-start | bytes 3145736 | tf_op jit(solution)/shard_map/ppermute | solution.py:439
  233.3 87.9 %collective-permute-start.18 = (bf16[2,2,128,1024]{3,2,1,0:T(8,128)(2,1)}, bf16[2,2,128,1024]{3,2,1,0:T(8,128)(2,1)S(1)}, u32[]{:S(2)}, u32[]{:S(2)}) collective-permute-start(bf16[2,2,128,1024]{3,2,1,0:T(8,128)(2,1)} %pad_maximum_fusion.26), channel_id=1, source_target_pairs={{0,2},{2,0},{4,6},{6,4},{1,3},{3,1},{5,7},{7,5},{8,10},{10,8},{12,... | collective-permute-start | bytes 3145736 | tf_op jit(solution)/shard_map/ppermute | solution.py:439
  258.8 59.4 %collective-permute-start.16 = (bf16[2,2,128,1024]{3,2,1,0:T(8,128)(2,1)}, bf16[2,2,128,1024]{3,2,1,0:T(8,128)(2,1)S(1)}, u32[]{:S(2)}, u32[]{:S(2)}) collective-permute-start(bf16[2,2,128,1024]{3,2,1,0:T(8,128)(2,1)} %pad_maximum_fusion.25), channel_id=1, source_target_pairs={{0,4},{2,6},{4,0},{6,2},{1,5},{3,7},{5,1},{7,3},{8,12},{10,14},{12... | collective-permute-start | bytes 3145736 | tf_op jit(solution)/shard_map/ppermute | solution.py:439
  264.7 59.0 %collective-permute-start.19 = (bf16[1024,1024]{1,0:T(8,128)(2,1)}, bf16[1024,1024]{1,0:T(8,128)(2,1)}, u32[]{:S(2)}, u32[]{:S(2)}) collective-permute-start(bf16[1024,1024]{1,0:T(8,128)(2,1)} %constant_dynamic-slice_fusion.4), channel_id=1, source_target_pairs={{0,24},{8,0},{16,8},{24,16},{1,25},{9,1},{17,9},{25,17},{2,26},{10... | collective-permute-start | bytes 6291464 | tf_op jit(solution)/shard_map/ppermute | solution.py:426
  323.7 108.3 %collective-permute-start.31 = (bf16[1024,1024]{1,0:T(8,128)(2,1)}, bf16[1024,1024]{1,0:T(8,128)(2,1)}, u32[]{:S(2)}, u32[]{:S(2)}) collective-permute-start(bf16[1024,1024]{1,0:T(8,128)(2,1)} %constant_dynamic-slice_fusion.4), channel_id=1, source_target_pairs={{0,8},{8,16},{16,24},{24,0},{1,9},{9,17},{17,25},{25,1},{2,10},{10... | collective-permute-start | bytes 6291464 | tf_op jit(solution)/shard_map/ppermute | solution.py:426
  391.6 25.4 %collective-permute-start.33 = (bf16[1,512,1024]{2,1,0:T(8,128)(2,1)}, bf16[1,512,1024]{2,1,0:T(8,128)(2,1)}, u32[]{:S(2)}, u32[]{:S(2)}) collective-permute-start(bf16[1,512,1024]{2,1,0:T(8,128)(2,1)} %get-tuple-element.403), channel_id=1, source_target_pairs={{0,4},{2,6},{4,0},{6,2},{1,5},{3,7},{5,1},{7,3},{8,12},{10,14},{12... | collective-permute-start | bytes 3145736 | tf_op jit(solution)/shard_map/ppermute | solution.py:439
  404.2 26.2 %collective-permute-start.30 = (bf16[1,512,1024]{2,1,0:T(8,128)(2,1)}, bf16[1,512,1024]{2,1,0:T(8,128)(2,1)S(1)}, u32[]{:S(2)}, u32[]{:S(2)}) collective-permute-start(bf16[1,512,1024]{2,1,0:T(8,128)(2,1)} %stack.299), channel_id=1, source_target_pairs={{0,2},{2,0},{4,6},{6,4},{1,3},{3,1},{5,7},{7,5},{8,10},{10,8},{12,... | collective-permute-start | bytes 3145736 | tf_op jit(solution)/shard_map/ppermute | solution.py:439
  420.1 54.2 %collective-permute-start.34 = (bf16[2,512,1024]{2,1,0:T(8,128)(2,1)}, bf16[2,512,1024]{2,1,0:T(8,128)(2,1)}, u32[]{:S(2)}, u32[]{:S(2)}) collective-permute-start(bf16[2,512,1024]{2,1,0:T(8,128)(2,1)} %pad_maximum_fusion.12), channel_id=1, source_target_pairs={{0,2},{2,0},{4,6},{6,4},{1,3},{3,1},{5,7},{7,5},{8,10},{10,8},{12,... | collective-permute-start | bytes 6291464 | tf_op jit(solution)/shard_map/ppermute | solution.py:439
  432.1 53.0 %collective-permute-start.32 = (bf16[2,512,1024]{2,1,0:T(8,128)(2,1)}, bf16[2,512,1024]{2,1,0:T(8,128)(2,1)}, u32[]{:S(2)}, u32[]{:S(2)}) collective-permute-start(bf16[2,512,1024]{2,1,0:T(8,128)(2,1)} %pad_maximum_fusion.11), channel_id=1, source_target_pairs={{0,4},{2,6},{4,0},{6,2},{1,5},{3,7},{5,1},{7,3},{8,12},{10,14},{12... | collective-permute-start | bytes 6291464 | tf_op jit(solution)/shard_map/ppermute | solution.py:439
  433.5 106.9 %collective-permute-start.35 = (bf16[1024,1024]{1,0:T(8,128)(2,1)}, bf16[1024,1024]{1,0:T(8,128)(2,1)}, u32[]{:S(2)}, u32[]{:S(2)}) collective-permute-start(bf16[1024,1024]{1,0:T(8,128)(2,1)} %constant_dynamic-slice_fusion.4), channel_id=1, source_target_pairs={{0,16},{8,24},{16,0},{24,8},{1,17},{9,25},{17,1},{25,9},{2,18},{10... | collective-permute-start | bytes 6291464 | tf_op jit(solution)/shard_map/ppermute | solution.py:426
  590.2 36.9 %collective-permute-start.41 = (f32[4,1024]{0,1:T(8,128)S(1)}, f32[4,1024]{0,1:T(8,128)S(1)}, u32[]{:S(2)}, u32[]{:S(2)}) collective-permute-start(f32[4,1024]{0,1:T(8,128)S(1)} %get-tuple-element.434), channel_id=1, source_target_pairs={{0,16},{8,24},{16,0},{24,8},{1,17},{9,25},{17,1},{25,9},{2,18},{10... | collective-permute-start | bytes 49160 | tf_op jit(solution)/shard_map/ppermute | solution.py:426
  592.3 34.8 %collective-permute-start.40 = (f32[4,1024]{0,1:T(8,128)S(1)}, f32[4,1024]{0,1:T(8,128)S(1)}, u32[]{:S(2)}, u32[]{:S(2)}) collective-permute-start(f32[4,1024]{0,1:T(8,128)S(1)} %get-tuple-element.435), channel_id=1, source_target_pairs={{0,24},{8,0},{16,8},{24,16},{1,25},{9,1},{17,9},{25,17},{2,26},{10... | collective-permute-start | bytes 49160 | tf_op jit(solution)/shard_map/ppermute | solution.py:426
  628.0 157.4 %collective-permute-start.43 = (bf16[1024,1024]{1,0:T(8,128)(2,1)}, bf16[1024,1024]{1,0:T(8,128)(2,1)S(1)}, u32[]{:S(2)}, u32[]{:S(2)}) collective-permute-start(bf16[1024,1024]{1,0:T(8,128)(2,1)} %constant_dynamic-slice_fusion.1), channel_id=1, source_target_pairs={{0,24},{8,0},{16,8},{24,16},{1,25},{9,1},{17,9},{25,17},{2,26},{10... | collective-permute-start | bytes 6291464 | tf_op jit(solution)/shard_map/ppermute | solution.py:426
  640.7 46.2 %collective-permute-start.38 = (s32[4]{0:T(128)S(1)}, s32[4]{0:T(128)S(1)}, u32[]{:S(2)}, u32[]{:S(2)}) collective-permute-start(s32[4]{0:T(128)S(1)} %concatenate.131), channel_id=1, source_target_pairs={{0,16},{8,24},{16,0},{24,8},{1,17},{9,25},{17,1},{25,9},{2,18},{10... | collective-permute-start | bytes 56 | tf_op jit(solution)/shard_map/ppermute | solution.py:426
  641.2 45.7 %collective-permute-start.37 = (s32[4]{0:T(128)S(1)}, s32[4]{0:T(128)S(1)}, u32[]{:S(2)}, u32[]{:S(2)}) collective-permute-start(s32[4]{0:T(128)S(1)} %concatenate.131), channel_id=1, source_target_pairs={{0,24},{8,0},{16,8},{24,16},{1,25},{9,1},{17,9},{25,17},{2,26},{10... | collective-permute-start | bytes 56 | tf_op jit(solution)/shard_map/ppermute | solution.py:426
  642.1 44.8 %collective-permute-start.39 = (s32[4]{0:T(128)S(1)}, s32[4]{0:T(128)S(1)}, u32[]{:S(2)}, u32[]{:S(2)}) collective-permute-start(s32[4]{0:T(128)S(1)} %concatenate.131), channel_id=1, source_target_pairs={{0,8},{8,16},{16,24},{24,0},{1,9},{9,17},{17,25},{25,1},{2,10},{10... | collective-permute-start | bytes 56 | tf_op jit(solution)/shard_map/ppermute | solution.py:426
  795.7 93.7 %collective-permute-start.47 = (bf16[1024,1024]{1,0:T(8,128)(2,1)}, bf16[1024,1024]{1,0:T(8,128)(2,1)S(1)}, u32[]{:S(2)}, u32[]{:S(2)}) collective-permute-start(bf16[1024,1024]{1,0:T(8,128)(2,1)} %constant_dynamic-slice_fusion.1), channel_id=1, source_target_pairs={{0,16},{8,24},{16,0},{24,8},{1,17},{9,25},{17,1},{25,9},{2,18},{10... | collective-permute-start | bytes 6291464 | tf_op jit(solution)/shard_map/ppermute | solution.py:426
  906.3 91.4 %collective-permute-start.52 = (bf16[1024,1024]{1,0:T(8,128)(2,1)}, bf16[1024,1024]{1,0:T(8,128)(2,1)}, u32[]{:S(2)}, u32[]{:S(2)}) collective-permute-start(bf16[1024,1024]{1,0:T(8,128)(2,1)} %add_convert_fusion.8), channel_id=1, source_target_pairs={{0,8},{8,16},{16,24},{24,0},{1,9},{9,17},{17,25},{25,1},{2,10},{10... | collective-permute-start | bytes 6291464 | tf_op jit(solution)/shard_map/ppermute | solution.py:431
  907.6 92.8 %collective-permute-start.53 = (bf16[1024,1024]{1,0:T(8,128)(2,1)}, bf16[1024,1024]{1,0:T(8,128)(2,1)S(1)}, u32[]{:S(2)}, u32[]{:S(2)}) collective-permute-start(bf16[1024,1024]{1,0:T(8,128)(2,1)} %constant_dynamic-slice_fusion.1), channel_id=1, source_target_pairs={{0,8},{8,16},{16,24},{24,0},{1,9},{9,17},{17,25},{25,1},{2,10},{10... | collective-permute-start | bytes 6291464 | tf_op jit(solution)/shard_map/ppermute | solution.py:426
  1000.5 25.8 %collective-permute-start.54 = (bf16[1024,1024]{1,0:T(8,128)(2,1)S(1)}, bf16[1024,1024]{1,0:T(8,128)(2,1)S(1)}, u32[]{:S(2)}, u32[]{:S(2)}) collective-permute-start(bf16[1024,1024]{1,0:T(8,128)(2,1)S(1)} %collective-permute-done.53.h0_ref), channel_id=1, source_target_pairs={{0,1},{1,0},{2,3},{3,2},{4,5},{5,4},{6,7},{7,6},{8,9},{9,8},{10,11... | collective-permute-start | bytes 6291464 | tf_op jit(solution)/shard_map/ppermute | solution.py:436
  1001.0 26.6 %collective-permute-start.57 = (bf16[1024,1024]{1,0:T(8,128)(2,1)}, bf16[1024,1024]{1,0:T(8,128)(2,1)}, u32[]{:S(2)}, u32[]{:S(2)}) collective-permute-start(bf16[1024,1024]{1,0:T(8,128)(2,1)} %collective-permute-done.31.cot0_ref), channel_id=1, source_target_pairs={{0,1},{1,0},{2,3},{3,2},{4,5},{5,4},{6,7},{7,6},{8,9},{9,8},{10,11... | collective-permute-start | bytes 6291464 | tf_op jit(solution)/shard_map/ppermute | solution.py:436
  1001.0 25.3 %collective-permute-start.56 = (f32[4,1024]{0,1:T(8,128)}, f32[4,1024]{0,1:T(8,128)S(1)}, u32[]{:S(2)}, u32[]{:S(2)}) collective-permute-start(f32[4,1024]{0,1:T(8,128)} %bitcast.674), channel_id=1, source_target_pairs={{0,16},{8,24},{16,0},{24,8},{1,17},{9,25},{17,1},{25,9},{2,18},{10... | collective-permute-start | bytes 49160 | tf_op jit(solution)/shard_map/ppermute | solution.py:431
  1027.6 93.0 %collective-permute-start.58 = (bf16[1024,1024]{1,0:T(8,128)(2,1)}, bf16[1024,1024]{1,0:T(8,128)(2,1)}, u32[]{:S(2)}, u32[]{:S(2)}) collective-permute-start(bf16[1024,1024]{1,0:T(8,128)(2,1)} %add_convert_fusion.7), channel_id=1, source_target_pairs={{0,16},{8,24},{16,0},{24,8},{1,17},{9,25},{17,1},{25,9},{2,18},{10... | collective-permute-start | bytes 6291464 | tf_op jit(solution)/shard_map/ppermute | solution.py:431
  1120.6 22.4 %collective-permute-start.62 = (bf16[1024,1024]{1,0:T(8,128)(2,1)}, bf16[1024,1024]{1,0:T(8,128)(2,1)S(1)}, u32[]{:S(2)}, u32[]{:S(2)}) collective-permute-start(bf16[1024,1024]{1,0:T(8,128)(2,1)} %get-tuple-element.261), channel_id=1, source_target_pairs={{0,1},{1,0},{2,3},{3,2},{4,5},{5,4},{6,7},{7,6},{8,9},{9,8},{10,11... | collective-permute-start | bytes 6291464 | tf_op jit(solution)/shard_map/ppermute | solution.py:436
  1121.1 24.8 %collective-permute-start.63 = (bf16[1024,1024]{1,0:T(8,128)(2,1)}, bf16[1024,1024]{1,0:T(8,128)(2,1)S(1)}, u32[]{:S(2)}, u32[]{:S(2)}) collective-permute-start(bf16[1024,1024]{1,0:T(8,128)(2,1)} %get-tuple-element.263), channel_id=1, source_target_pairs={{0,1},{1,0},{2,3},{3,2},{4,5},{5,4},{6,7},{7,6},{8,9},{9,8},{10,11... | collective-permute-start | bytes 6291464 | tf_op jit(solution)/shard_map/ppermute | solution.py:436
  1121.1 27.1 %collective-permute-start.64 = (bf16[1024,1024]{1,0:T(8,128)(2,1)}, bf16[1024,1024]{1,0:T(8,128)(2,1)S(1)}, u32[]{:S(2)}, u32[]{:S(2)}) collective-permute-start(bf16[1024,1024]{1,0:T(8,128)(2,1)} %get-tuple-element.265), channel_id=1, source_target_pairs={{0,1},{1,0},{2,3},{3,2},{4,5},{5,4},{6,7},{7,6},{8,9},{9,8},{10,11... | collective-permute-start | bytes 6291464 | tf_op jit(solution)/shard_map/ppermute | solution.py:436
  1121.6 29.0 %collective-permute-start.65 = (bf16[1024,1024]{1,0:T(8,128)(2,1)}, bf16[1024,1024]{1,0:T(8,128)(2,1)S(1)}, u32[]{:S(2)}, u32[]{:S(2)}) collective-permute-start(bf16[1024,1024]{1,0:T(8,128)(2,1)} %get-tuple-element.267), channel_id=1, source_target_pairs={{0,1},{1,0},{2,3},{3,2},{4,5},{5,4},{6,7},{7,6},{8,9},{9,8},{10,11... | collective-permute-start | bytes 6291464 | tf_op jit(solution)/shard_map/ppermute | solution.py:436
  1139.1 48.2 %collective-permute-start.61 = (bf16[1024,1024]{1,0:T(8,128)(2,1)S(1)}, bf16[1024,1024]{1,0:T(8,128)(2,1)S(1)}, u32[]{:S(2)}, u32[]{:S(2)}) collective-permute-start(bf16[1024,1024]{1,0:T(8,128)(2,1)S(1)} %add_convert_fusion.6), channel_id=1, source_target_pairs={{0,24},{8,0},{16,8},{24,16},{1,25},{9,1},{17,9},{25,17},{2,26},{10... | collective-permute-start | bytes 6291464 | tf_op jit(solution)/shard_map/ppermute | solution.py:431
  1192.7 247.8 %reduce-scatter.3.cloned.1.call-start = ((), (), s32[]{:S(2)}) async-start(), calls=%async_computation.5 | async-start | bytes 7077888 | tf_op jit(solution)/shard_map/reduce_scatter | solution.py:575
  1192.7 30.9 %collective-permute-start.66 = (bf16[1024,1024]{1,0:T(8,128)(2,1)S(1)}, bf16[1024,1024]{1,0:T(8,128)(2,1)}, u32[]{:S(2)}, u32[]{:S(2)}) collective-permute-start(bf16[1024,1024]{1,0:T(8,128)(2,1)S(1)} %add_convert_fusion.5), channel_id=1, source_target_pairs={{0,1},{1,0},{2,3},{3,2},{4,5},{5,4},{6,7},{7,6},{8,9},{9,8},{10,11... | collective-permute-start | bytes 6291464 | tf_op jit(solution)/shard_map/ppermute | solution.py:436
  1210.3 125.3 %collective-permute-start.68 = (bf16[1024,1024]{1,0:T(8,128)(2,1)}, bf16[1024,1024]{1,0:T(8,128)(2,1)}, u32[]{:S(2)}, u32[]{:S(2)}) collective-permute-start(bf16[1024,1024]{1,0:T(8,128)(2,1)} %add_convert_fusion.4), channel_id=1, source_target_pairs={{0,8},{8,16},{16,24},{24,0},{1,9},{9,17},{17,25},{25,1},{2,10},{10... | collective-permute-start | bytes 6291464 | tf_op jit(solution)/shard_map/ppermute | solution.py:431
  1210.3 140.6 %collective-permute-start.69 = (bf16[1024,1024]{1,0:T(8,128)(2,1)}, bf16[1024,1024]{1,0:T(8,128)(2,1)}, u32[]{:S(2)}, u32[]{:S(2)}) collective-permute-start(bf16[1024,1024]{1,0:T(8,128)(2,1)} %add_convert_fusion.3), channel_id=1, source_target_pairs={{0,16},{8,24},{16,0},{24,8},{1,17},{9,25},{17,1},{25,9},{2,18},{10... | collective-permute-start | bytes 6291464 | tf_op jit(solution)/shard_map/ppermute | solution.py:431
  1223.6 420.3 %all-gather.14.cloned.1.call-start = ((), (), s32[]{:S(2)}) async-start(), calls=%async_computation.7 | async-start | bytes 7077888 | tf_op jit(solution)/shard_map/all_gather | solution.py:580
  1354.3 47.9 %collective-permute-start.75 = (bf16[2,512,1024]{2,1,0:T(8,128)(2,1)}, bf16[2,512,1024]{2,1,0:T(8,128)(2,1)}, u32[]{:S(2)}, u32[]{:S(2)}) collective-permute-start(bf16[2,512,1024]{2,1,0:T(8,128)(2,1)} %pad_maximum_fusion.14), channel_id=1, source_target_pairs={{0,4},{2,6},{4,0},{6,2},{1,5},{3,7},{5,1},{7,3},{8,12},{10,14},{12... | collective-permute-start | bytes 6291464 | tf_op jit(solution)/shard_map/ppermute | solution.py:439
  1357.3 52.8 %collective-permute-start.70 = (bf16[2,512,1024]{2,1,0:T(8,128)(2,1)}, bf16[2,512,1024]{2,1,0:T(8,128)(2,1)}, u32[]{:S(2)}, u32[]{:S(2)}) collective-permute-start(bf16[2,512,1024]{2,1,0:T(8,128)(2,1)} %pad_maximum_fusion.13), channel_id=1, source_target_pairs={{0,2},{2,0},{4,6},{6,4},{1,3},{3,1},{5,7},{7,5},{8,10},{10,8},{12,... | collective-permute-start | bytes 6291464 | tf_op jit(solution)/shard_map/ppermute | solution.py:439
  1366.7 47.2 %collective-permute-start.71 = (bf16[1024,1024]{1,0:T(8,128)(2,1)S(1)}, bf16[1024,1024]{1,0:T(8,128)(2,1)}, u32[]{:S(2)}, u32[]{:S(2)}) collective-permute-start(bf16[1024,1024]{1,0:T(8,128)(2,1)S(1)} %copy-done.51), channel_id=1, source_target_pairs={{0,24},{8,0},{16,8},{24,16},{1,25},{9,1},{17,9},{25,17},{2,26},{10... | collective-permute-start | bytes 6291464 | tf_op jit(solution)/shard_map/ppermute | solution.py:431
  1405.1 25.0 %collective-permute-start.76 = (bf16[1,512,1024]{2,1,0:T(8,128)(2,1)}, bf16[1,512,1024]{2,1,0:T(8,128)(2,1)}, u32[]{:S(2)}, u32[]{:S(2)}) collective-permute-start(bf16[1,512,1024]{2,1,0:T(8,128)(2,1)} %fusion.45), channel_id=1, source_target_pairs={{0,2},{2,0},{4,6},{6,4},{1,3},{3,1},{5,7},{7,5},{8,10},{10,8},{12,... | collective-permute-start | bytes 3145736 | tf_op jit(solution)/shard_map/ppermute | solution.py:439
  1413.9 24.0 %collective-permute-start.73 = (bf16[1,512,1024]{2,1,0:T(8,128)(2,1)}, bf16[1,512,1024]{2,1,0:T(8,128)(2,1)}, u32[]{:S(2)}, u32[]{:S(2)}) collective-permute-start(bf16[1,512,1024]{2,1,0:T(8,128)(2,1)} %fusion.44), channel_id=1, source_target_pairs={{0,4},{2,6},{4,0},{6,2},{1,5},{3,7},{5,1},{7,3},{8,12},{10,14},{12... | collective-permute-start | bytes 3145736 | tf_op jit(solution)/shard_map/ppermute | solution.py:439
  1480.6 169.9 %all-gather.16.cloned.1.call-start = ((), (), s32[]{:S(2)}) async-start(), calls=%async_computation.8 | async-start | bytes 1966080 | tf_op jit(solution)/shard_map/all_gather | solution.py:580
  1497.8 38.3 %collective-permute-start.84 = (bf16[8,128,1024]{2,1,0:T(8,128)(2,1)}, bf16[8,128,1024]{2,1,0:T(8,128)(2,1)}, u32[]{:S(2)}, u32[]{:S(2)}) collective-permute-start(bf16[8,128,1024]{2,1,0:T(8,128)(2,1)} %multiply_reduce_fusion), channel_id=1, source_target_pairs={{0,1},{1,0},{2,3},{3,2},{4,5},{5,4},{6,7},{7,6},{8,9},{9,8},{10,11... | collective-permute-start | bytes 6291464 | tf_op jit(solution)/shard_map/ppermute | solution.py:436
  1525.1 106.9 %collective-permute-start.77 = (f32[1024,2048]{1,0:T(8,128)}, f32[1024,2048]{1,0:T(8,128)}, u32[]{:S(2)}, u32[]{:S(2)}) collective-permute-start(f32[1024,2048]{1,0:T(8,128)} %bitcast_add_fusion), channel_id=1, source_target_pairs={{0,1},{1,0},{2,3},{3,2},{4,5},{5,4},{6,7},{7,6},{8,9},{9,8},{10,11... | collective-permute-start | bytes 25165832 | tf_op jit(solution)/shard_map/ppermute | solution.py:436
  1543.7 25.8 %collective-permute-start.85 = (bf16[8,128,512]{2,1,0:T(8,128)(2,1)}, bf16[8,128,512]{2,1,0:T(8,128)(2,1)}, u32[]{:S(2)}, u32[]{:S(2)}) collective-permute-start(bf16[8,128,512]{2,1,0:T(8,128)(2,1)} %dynamic-slice_bitcast_fusion.1), channel_id=1, source_target_pairs={{0,2},{2,0},{4,6},{6,4},{1,3},{3,1},{5,7},{7,5},{8,10},{10,8},{12,... | collective-permute-start | bytes 3145736 | tf_op jit(solution)/shard_map/ppermute | solution.py:439
  1547.6 25.8 %collective-permute-start.92 = (bf16[8,128,512]{2,1,0:T(8,128)(2,1)}, bf16[8,128,512]{2,1,0:T(8,128)(2,1)}, u32[]{:S(2)}, u32[]{:S(2)}) collective-permute-start(bf16[8,128,512]{2,1,0:T(8,128)(2,1)} %dynamic-slice_bitcast_fusion), channel_id=1, source_target_pairs={{0,4},{2,6},{4,0},{6,2},{1,5},{3,7},{5,1},{7,3},{8,12},{10,14},{12... | collective-permute-start | bytes 3145736 | tf_op jit(solution)/shard_map/ppermute | solution.py:439
  (201 other events, 4557.0 us)
Sparse Core Ops, SparseCore 0:
  14.0 122.1 all-gather.17
  179.6 38.8 all-gather.9
  221.0 70.8 all-gather.7
  294.4 125.3 all-gather.11
  1192.8 33.4 reduce-scatter.4
  1229.5 61.7 reduce-scatter.2
  1480.8 44.8 all-gather.13
  1578.2 32.5 all-gather.15
